TPU v7x, 32 devices: a whole 2x2x4 slice. The times are simulated.
32 devices in a mesh: grp: 4 (over y, x), fsdp: 8 (over z, core).
Axes of the slice: x: 2, y: 2, z: 4, core: 2. Of those that a mesh axis runs over, the one named last changes fastest.
Arguments:
- tokens: bfloat16 [32, 1024, 768], P(('grp', 'fsdp')), may hold values from -6 to 6
- segments: int32 [32, 1024], P(('grp', 'fsdp')), may hold values from 0 to 8, as said below
- project_weight: bfloat16 [768, 2304], P('fsdp'), may hold values from -0.21875 to 0.21875
- project_bias: bfloat16 [1536], P('fsdp'), may hold values from -1.796875 to 1.796875
- combine_weight: bfloat16 [768, 768], P('fsdp'), may hold values from -1.75 to 1.75
- combine_bias: bfloat16 [768], P('fsdp'), may hold values from -1.796875 to 1.796875
- first_gain: bfloat16 [768], P('fsdp'), may hold values from 0.5 to 1.5
- first_shift: bfloat16 [768], P('fsdp'), may hold values from -1.796875 to 1.796875
- expand_weight: bfloat16 [768, 3072], P('fsdp'), may hold values from -0.21875 to 0.21875
- expand_bias: bfloat16 [3072], P('fsdp'), may hold values from -1.796875 to 1.796875
- reduce_weight: bfloat16 [3072, 768], P('fsdp'), may hold values from -0.109375 to 0.109375
- reduce_bias: bfloat16 [768], P('fsdp'), may hold values from -1.796875 to 1.796875
- second_gain: bfloat16 [768], P('fsdp'), may hold values from 0.5 to 1.5
- second_shift: bfloat16 [768], P('fsdp'), may hold values from -1.796875 to 1.796875
- layer_cotangent: bfloat16 [32, 1024, 768], P(('grp', 'fsdp')), may hold values from -6 to 6
- pooled_cotangent: float32 [32, 8, 768], P(('grp', 'fsdp')), may hold values from -192 to 192
Outputs:
- layer_output: bfloat16 [32, 1024, 768], P(('grp', 'fsdp'))
- pooled: float32 [32, 8, 768], P(('grp', 'fsdp'))
- token_gradient: bfloat16 [32, 1024, 768], P(('grp', 'fsdp'))
- project_weight_grad: float32 [768, 2304], P('fsdp')
- project_bias_grad: float32 [1536], P('fsdp')
- combine_weight_grad: float32 [768, 768], P('fsdp')
- combine_bias_grad: float32 [768], P('fsdp')
- first_gain_grad: float32 [768], P('fsdp')
- first_shift_grad: float32 [768], P('fsdp')
- expand_weight_grad: float32 [768, 3072], P('fsdp')
- expand_bias_grad: float32 [3072], P('fsdp')
- reduce_weight_grad: float32 [3072, 768], P('fsdp')
- reduce_bias_grad: float32 [768], P('fsdp')
- second_gain_grad: float32 [768], P('fsdp')
- second_shift_grad: float32 [768], P('fsdp')
Inputs may be any that keep to these rules, and one draw needn't show every extreme that they name: `segments`: in every row the nonzero ids start at 1 at the row's first token and run 1, 2, 3 and so on, each crop one contiguous run of tokens; padding tokens (0) come only after the last crop of a row.
All inputs are finite; a program needn't handle non-finite values.
Results may differ from a plain program's by a relative error of at most 0.013.
Values may be sent and summed in bfloat16 or wider, within the bound.
No kernel may reach another device: no remote copies, remote signals or barrier semaphores. Data moves between devices by JAX's collectives and lax.ppermute only.
A program may use at most 320 MiB of HBM per device.

v0:
```python
from functools import partial

import jax
import jax.numpy as jnp
from jax import lax
from jax.sharding import PartitionSpec as P

H = 12
DH = 64
SEG = 8


NEG_FILL = -1e30
EPSILON = 1e-12


def norm_forward(values, norm_gain, norm_shift):
    average = jnp.mean(values, axis=-1, keepdims=True)
    centred = values - average
    variance = jnp.mean(centred * centred, axis=-1, keepdims=True)
    inverse = lax.rsqrt(variance + EPSILON)
    normed = centred * inverse
    return (normed * norm_gain + norm_shift, normed, inverse)


def norm_backward(grad_out, normed, inverse, norm_gain):
    gain_term = jnp.sum(grad_out * normed, axis=0)
    shift_term = jnp.sum(grad_out, axis=0)
    scaled = grad_out * norm_gain
    grad_values = inverse * (
        scaled
        - jnp.mean(scaled, axis=-1, keepdims=True)
        - normed * jnp.mean(scaled * normed, axis=-1, keepdims=True)
    )
    return (grad_values, gain_term, shift_term)


def block_scores(query_block, keys_row, seg_query, seg_keys, score_scale):
    scores = (
        jnp.einsum("qhd,khd->hqk", query_block, keys_row, preferred_element_type=jnp.float32)
        * score_scale
    )
    allowed = seg_query[:, None] == seg_keys[None, :]
    return jnp.where(allowed[None], scores, NEG_FILL)


def attend_forward(score_scale, packed):
    query_row, keys_row, values_row, seg_row = packed
    length = seg_row.shape[0]
    block_rows = min(512, length)
    outputs = []
    totals = []
    for offset in range(0, length, block_rows):
        scores = block_scores(
            query_row[offset : offset + block_rows],
            keys_row,
            seg_row[offset : offset + block_rows],
            seg_row,
            score_scale,
        )
        highest = jnp.max(scores, axis=-1, keepdims=True)
        exponent = jnp.exp(scores - highest)
        row_total = jnp.sum(exponent, axis=-1, keepdims=True)
        weights_low = (exponent / row_total).astype(jnp.bfloat16)
        outputs.append(
            jnp.einsum(
                "hqk,khd->qhd", weights_low, values_row, preferred_element_type=jnp.float32
            ).astype(jnp.bfloat16)
        )
        totals.append(highest[..., 0] + jnp.log(row_total[..., 0]))
    return (jnp.concatenate(outputs, axis=0), jnp.concatenate(totals, axis=1))


def attend_backward(score_scale, packed):
    query_row, keys_row, values_row, seg_row, grad_context, log_totals = packed
    length = seg_row.shape[0]
    block_rows = min(512, length)
    grad_keys = jnp.zeros(keys_row.shape, jnp.float32)
    grad_values = jnp.zeros(values_row.shape, jnp.float32)
    grad_queries = []
    for offset in range(0, length, block_rows):
        query_block = query_row[offset : offset + block_rows]
        context_block = grad_context[offset : offset + block_rows]
        scores = block_scores(
            query_block, keys_row, seg_row[offset : offset + block_rows], seg_row, score_scale
        )
        weights = jnp.exp(scores - log_totals[:, offset : offset + block_rows, None])
        grad_weights = jnp.einsum(
            "qhd,khd->hqk", context_block, values_row, preferred_element_type=jnp.float32
        )
        grad_values = grad_values + jnp.einsum(
            "hqk,qhd->khd",
            weights.astype(jnp.bfloat16),
            context_block,
            preferred_element_type=jnp.float32,
        )
        inner_sum = jnp.sum(grad_weights * weights, axis=-1, keepdims=True)
        grad_scores = (weights * (grad_weights - inner_sum)).astype(jnp.bfloat16)
        grad_queries.append(
            jnp.einsum("hqk,khd->qhd", grad_scores, keys_row, preferred_element_type=jnp.float32)
            * score_scale
        )
        grad_keys = (
            grad_keys
            + jnp.einsum(
                "hqk,qhd->khd", grad_scores, query_block, preferred_element_type=jnp.float32
            )
            * score_scale
        )
    return (jnp.concatenate(grad_queries, axis=0), grad_keys, grad_values)


def per_device(
    tokens,
    segments,
    project_weight,
    project_bias,
    combine_weight,
    combine_bias,
    first_gain,
    first_shift,
    expand_weight,
    expand_bias,
    reduce_weight,
    reduce_bias,
    second_gain,
    second_shift,
    layer_cotangent,
    pooled_cotangent,
):
    row_count, length, width = tokens.shape
    count = row_count * length
    flat = tokens.reshape(count, width)
    score_scale = DH ** (-0.5)
    project_full, bias_pair, combine_full, combine_shift, gain_first, shift_first = (
        lax.all_gather(project_weight, "fsdp", axis=0, tiled=True),
        lax.all_gather(project_bias, "fsdp", axis=0, tiled=True),
        lax.all_gather(combine_weight, "fsdp", axis=0, tiled=True),
        lax.all_gather(combine_bias, "fsdp", axis=0, tiled=True),
        lax.all_gather(first_gain, "fsdp", axis=0, tiled=True),
        lax.all_gather(first_shift, "fsdp", axis=0, tiled=True),
    )
    pair_wide = bias_pair.astype(jnp.float32)
    bias_all = jnp.concatenate(
        [pair_wide[:width], jnp.zeros((width,), jnp.float32), pair_wide[width:]]
    )
    triple = (jnp.dot(flat, project_full, preferred_element_type=jnp.float32) + bias_all).astype(
        jnp.bfloat16
    )
    shaped = triple.reshape(row_count, length, 3, H, DH)
    query_all = shaped[:, :, 0]
    keys_all = shaped[:, :, 1]
    values_all = shaped[:, :, 2]
    context, log_totals = lax.map(
        partial(attend_forward, score_scale), (query_all, keys_all, values_all, segments)
    )
    context_flat = context.reshape(count, width)
    attn_out = jnp.dot(
        context_flat, combine_full, preferred_element_type=jnp.float32
    ) + combine_shift.astype(jnp.float32)
    hidden, normed_one, inverse_one = norm_forward(
        flat.astype(jnp.float32) + attn_out,
        gain_first.astype(jnp.float32),
        shift_first.astype(jnp.float32),
    )
    hidden_low = hidden.astype(jnp.bfloat16)
    expand_full, expand_shift, reduce_full, reduce_shift, gain_second, shift_second = (
        lax.all_gather(expand_weight, "fsdp", axis=0, tiled=True),
        lax.all_gather(expand_bias, "fsdp", axis=0, tiled=True),
        lax.all_gather(reduce_weight, "fsdp", axis=0, tiled=True),
        lax.all_gather(reduce_bias, "fsdp", axis=0, tiled=True),
        lax.all_gather(second_gain, "fsdp", axis=0, tiled=True),
        lax.all_gather(second_shift, "fsdp", axis=0, tiled=True),
    )
    pre_act = jnp.dot(
        hidden_low, expand_full, preferred_element_type=jnp.float32
    ) + expand_shift.astype(jnp.float32)
    activ = jax.nn.gelu(pre_act, approximate=False).astype(jnp.bfloat16)
    branch = jnp.dot(activ, reduce_full, preferred_element_type=jnp.float32) + reduce_shift.astype(
        jnp.float32
    )
    result, normed_two, inverse_two = norm_forward(
        hidden + branch, gain_second.astype(jnp.float32), shift_second.astype(jnp.float32)
    )
    result_rows = result.reshape(row_count, length, width)
    slot_ids = jnp.arange(1, SEG + 1, dtype=jnp.int32)
    member = (segments[:, None, :] == slot_ids[None, :, None]).astype(jnp.float32)
    divisor = jnp.maximum(jnp.sum(member, axis=2), 1.0)[..., None]
    pooled = (
        jnp.einsum(
            "rsl,rld->rsd",
            member,
            result_rows,
            precision=lax.Precision.HIGHEST,
            preferred_element_type=jnp.float32,
        )
        / divisor
    )
    expand_back, reduce_back, gain_back = (
        lax.all_gather(expand_weight, "fsdp", axis=0, tiled=True),
        lax.all_gather(reduce_weight, "fsdp", axis=0, tiled=True),
        lax.all_gather(second_gain, "fsdp", axis=0, tiled=True),
    )
    pooled_share = pooled_cotangent / divisor
    spread = jnp.einsum(
        "rsl,rsd->rld",
        member,
        pooled_share,
        precision=lax.Precision.HIGHEST,
        preferred_element_type=jnp.float32,
    )
    grad_result = layer_cotangent.astype(jnp.float32).reshape(count, width) + spread.reshape(
        count, width
    )
    grad_second, gain_delta, shift_delta = norm_backward(
        grad_result, normed_two, inverse_two, gain_back.astype(jnp.float32)
    )
    grad_branch = grad_second.astype(jnp.bfloat16)
    reduce_bias_term = jnp.sum(grad_branch.astype(jnp.float32), axis=0)
    reduce_term = jnp.einsum("nf,nd->fd", activ, grad_branch, preferred_element_type=jnp.float32)
    grad_activ = jnp.einsum(
        "nd,fd->nf", grad_branch, reduce_back, preferred_element_type=jnp.float32
    )
    gelu_pull = jax.vjp(partial(jax.nn.gelu, approximate=False), pre_act)[1]
    grad_pre = gelu_pull(grad_activ)[0].astype(jnp.bfloat16)
    expand_bias_term = jnp.sum(grad_pre.astype(jnp.float32), axis=0)
    expand_term = jnp.einsum("nd,nf->df", hidden_low, grad_pre, preferred_element_type=jnp.float32)
    grad_hidden = grad_second + jnp.einsum(
        "nf,df->nd", grad_pre, expand_back, preferred_element_type=jnp.float32
    )
    ffn_expand, ffn_ebias, ffn_reduce, ffn_rbias, ffn_gain, ffn_shift = (
        lax.psum_scatter(expand_term, "fsdp", scatter_dimension=0, tiled=True),
        lax.psum_scatter(expand_bias_term, "fsdp", scatter_dimension=0, tiled=True),
        lax.psum_scatter(reduce_term, "fsdp", scatter_dimension=0, tiled=True),
        lax.psum_scatter(reduce_bias_term, "fsdp", scatter_dimension=0, tiled=True),
        lax.psum_scatter(gain_delta, "fsdp", scatter_dimension=0, tiled=True),
        lax.psum_scatter(shift_delta, "fsdp", scatter_dimension=0, tiled=True),
    )
    project_back, combine_back, first_back = (
        lax.all_gather(project_weight, "fsdp", axis=0, tiled=True),
        lax.all_gather(combine_weight, "fsdp", axis=0, tiled=True),
        lax.all_gather(first_gain, "fsdp", axis=0, tiled=True),
    )
    grad_first, gain_change, shift_change = norm_backward(
        grad_hidden, normed_one, inverse_one, first_back.astype(jnp.float32)
    )
    grad_attn = grad_first.astype(jnp.bfloat16)
    combine_bias_term = jnp.sum(grad_attn.astype(jnp.float32), axis=0)
    combine_term = jnp.einsum(
        "nc,nd->cd", context_flat, grad_attn, preferred_element_type=jnp.float32
    )
    grad_context = jnp.einsum(
        "nd,cd->nc", grad_attn, combine_back, preferred_element_type=jnp.float32
    ).astype(jnp.bfloat16)
    grad_query, grad_keys, grad_values = lax.map(
        partial(attend_backward, score_scale),
        (
            query_all,
            keys_all,
            values_all,
            segments,
            grad_context.reshape(row_count, length, H, DH),
            log_totals,
        ),
    )
    grad_triple = (
        jnp.stack([grad_query, grad_keys, grad_values], axis=2)
        .astype(jnp.bfloat16)
        .reshape(count, 3 * width)
    )
    column_sums = jnp.sum(grad_triple.astype(jnp.float32), axis=0)
    project_bias_term = jnp.concatenate([column_sums[:width], column_sums[2 * width :]])
    project_term = jnp.einsum("nd,nc->dc", flat, grad_triple, preferred_element_type=jnp.float32)
    token_grad = (
        grad_first
        + jnp.einsum("nc,dc->nd", grad_triple, project_back, preferred_element_type=jnp.float32)
    ).astype(jnp.bfloat16)
    att_project, att_pbias, att_combine, att_cbias, att_gain, att_shift = (
        lax.psum_scatter(project_term, "fsdp", scatter_dimension=0, tiled=True),
        lax.psum_scatter(project_bias_term, "fsdp", scatter_dimension=0, tiled=True),
        lax.psum_scatter(combine_term, "fsdp", scatter_dimension=0, tiled=True),
        lax.psum_scatter(combine_bias_term, "fsdp", scatter_dimension=0, tiled=True),
        lax.psum_scatter(gain_change, "fsdp", scatter_dimension=0, tiled=True),
        lax.psum_scatter(shift_change, "fsdp", scatter_dimension=0, tiled=True),
    )
    summed = lax.psum(
        (
            att_project,
            att_pbias,
            att_combine,
            att_cbias,
            att_gain,
            att_shift,
            ffn_expand,
            ffn_ebias,
            ffn_reduce,
            ffn_rbias,
            ffn_gain,
            ffn_shift,
        ),
        "grp",
    )
    factor = float(count * lax.axis_size("grp") * lax.axis_size("fsdp")) ** (-0.5)
    scaled = [entry * factor for entry in summed]
    return (
        result_rows.astype(jnp.bfloat16),
        pooled,
        token_grad.reshape(row_count, length, width),
        scaled[0],
        scaled[1],
        scaled[2],
        scaled[3],
        scaled[4],
        scaled[5],
        scaled[6],
        scaled[7],
        scaled[8],
        scaled[9],
        scaled[10],
        scaled[11],
    )


def solution(mesh):
    in_specs = (
        P(("grp", "fsdp"), None, None),
        P(("grp", "fsdp"), None),
        P("fsdp", None),
        P("fsdp"),
        P("fsdp", None),
        P("fsdp"),
        P("fsdp"),
        P("fsdp"),
        P("fsdp", None),
        P("fsdp"),
        P("fsdp", None),
        P("fsdp"),
        P("fsdp"),
        P("fsdp"),
        P(("grp", "fsdp"), None, None),
        P(("grp", "fsdp"), None, None),
    )
    out_specs = (
        P(("grp", "fsdp"), None, None),
        P(("grp", "fsdp"), None, None),
        P(("grp", "fsdp"), None, None),
        P("fsdp", None),
        P("fsdp"),
        P("fsdp", None),
        P("fsdp"),
        P("fsdp"),
        P("fsdp"),
        P("fsdp", None),
        P("fsdp"),
        P("fsdp", None),
        P("fsdp"),
        P("fsdp"),
        P("fsdp"),
    )
    return jax.shard_map(
        per_device, mesh=mesh, in_specs=in_specs, out_specs=out_specs, check_vma=False
    )
```

profile of v0, /device:TPU:0, one launch (start us, length us, event | category | flops | bytes accessed | tf_op | source)
XLA Modules:
  0.0 851.4 jit_solution(4170277893705949636)
XLA Ops:
  10.1 1.3 fusion.76
  13.4 0.9 convert_reduce_fusion.4
  18.0 0.8 dynamic-update-slice.3
  18.8 0.9 dynamic-update-slice.1
  19.7 0.8 dynamic-update-slice.5
  20.5 0.8 dynamic-update-slice
  21.4 32.3 %all-reduce.18 = (bf16[1536]{0:T(1024)(128)(2,1)S(1)}, bf16[768]{0:T(1024)(128)(2,1)S(1)}, bf16[768]{0:T(1024)(128)(2,1)S(1)}, bf16[768]{0:T(1024)(128)(2,1)S(1)...) all-reduce(bf16[1536]{0:T(1024)(128)(2,1)S(1)} %dynamic-update-slic, ...), channel_id=1, replica_groups=mesh['grp'=4,'fsdp'=8] {'fsdp'}, use_global_device_ids=true, to_apply=%add | all-reduce | flops 6144 | bytes 24576
  55.4 12.8 %all-gather = bf16[8,1,384]{2,1,0:T(2,128)(2,1)S(1)} all-gather(bf16[1,1,384]{2,1,0:T(2,128)(2,1)S(1)} %reshape.412), channel_id=1, replica_groups=mesh['grp'=4,'fsdp'=8] {'fsdp'}, dimensions={0}, use_global_device_ids=true | all-gather | bytes 6912 | tf_op jit(solution)/shard_map/all_gather | solution.py:169
  68.2 2.6 copy.67
  70.8 1.6 copy.64
  72.4 1.4 broadcast_compare_fusion.1
  73.8 7.7 add_convert_fusion.1
  81.5 6.8 copy.65
  88.3 14.8 %fusion.19 = (f32[12,512]{1,0:T(8,128)S(1)}, f32[12,512,1024]{2,1,0:T(8,128)}) fusion(pred[512,1024]{1,0:T(8,128)(4,1)} %get-tuple-element.175, bf16[1,1024,3,12,64]{1,4,3,2,0:T(8,128)(2,1)} %bitcast.111), kind=kOutput, calls=%fused_computation.44 | convolution fusion | flops 824174592 | bytes 28073984 | tf_op jit(solution)/shard_map/while/body/eval_jaxpr/qhd,khd->hqk/dot_general | solution.py:40
  103.1 12.5 %fusion.1 = f32[12,512]{1,0:T(8,128)S(1)} fusion(f32[12,512]{1,0:T(8,128)S(1)} %get-tuple-element.182, f32[12,512,1024]{2,1,0:T(8,128)} %get-tuple-element.183, pred[512,1024]{1,0:T(8,128)(4,1)} %get-tuple-element.175), kind=kLoop, calls=%fused_computation.13 | loop fusion | flops 25159680 | bytes 25739264 | tf_op jit(solution)/shard_map/while/body/eval_jaxpr/reduce_sum | solution.py:63
  116.2 3.2 copy-done.1
  119.4 10.2 %fusion.36 = bf16[512,12,64]{0,2,1:T(8,128)(2,1)} fusion(f32[12,512]{1,0:T(8,128)S(1)} %fusion.1, f32[12,512]{1,0:T(8,128)S(1)} %get-tuple-element.182, f32[12,512,1024]{2,1,0:T(8,128)S(1)} %copy-done.1, pred[512,1024]{1,0:T(8,128)(4,1)} %get-tuple-element.175, bf16[1,1024,3,12,64]{1,4,3,2,0:T(8,128)(2,1)S(1)} %bitcast.114), kind=kOutput, calls=%fused_computation.90 | convolution fusion | flops 837156864 | bytes 28114944 | tf_op jit(solution)/shard_map/while/body/eval_jaxpr/hqk,khd->qhd/dot_general | solution.py:66
  129.6 11.3 %fusion.18 = (f32[12,512]{1,0:T(8,128)S(1)}, f32[12,512,1024]{2,1,0:T(8,128)}) fusion(pred[512,1024]{1,0:T(8,128)(4,1)S(1)} %get-tuple-element.174, bf16[1,1024,3,12,64]{1,4,3,2,0:T(8,128)(2,1)S(1)} %bitcast.115), kind=kOutput, calls=%fused_computation.43 | convolution fusion | flops 824174592 | bytes 28073984 | tf_op jit(solution)/shard_map/while/body/eval_jaxpr/qhd,khd->hqk/dot_general | solution.py:40
  140.9 12.5 %fusion = f32[12,512]{1,0:T(8,128)S(1)} fusion(f32[12,512]{1,0:T(8,128)S(1)} %get-tuple-element.184, f32[12,512,1024]{2,1,0:T(8,128)} %get-tuple-element.185, pred[512,1024]{1,0:T(8,128)(4,1)S(1)} %get-tuple-element.174), kind=kLoop, calls=%fused_computation.12 | loop fusion | flops 25159680 | bytes 25739264 | tf_op jit(solution)/shard_map/while/body/eval_jaxpr/reduce_sum | solution.py:63
  154.0 2.6 copy-done
  156.7 8.8 %fusion.35 = bf16[512,12,64]{0,2,1:T(8,128)(2,1)} fusion(f32[12,512]{1,0:T(8,128)S(1)} %fusion, f32[12,512]{1,0:T(8,128)S(1)} %get-tuple-element.184, f32[12,512,1024]{2,1,0:T(8,128)S(1)} %copy-done, pred[512,1024]{1,0:T(8,128)(4,1)S(1)} %get-tuple-element.174, bf16[1,1024,3,12,64]{1,4,3,2,0:T(8,128)(2,1)S(1)} %bitcast.116), kind=kOutput, calls=%fused_computation.89 | convolution fusion | flops 837156864 | bytes 28114944 | tf_op jit(solution)/shard_map/while/body/eval_jaxpr/hqk,khd->qhd/dot_general | solution.py:66
  165.5 2.7 pad_maximum_fusion
  168.2 3.9 fusion.77
  172.5 38.4 %multiply_convert_fusion.2 = (bf16[1024,3072]{1,0:T(8,128)(2,1)}, f32[1024,3072]{1,0:T(8,128)}, f32[1024,3072]{1,0:T(8,128)}) fusion(f32[3072]{0:T(1024)S(1)} %bitcast.135, bf16[768,3072]{1,0:T(8,128)(2,1)} %all-gather.10.cloned.1.call-done, f32[1024,768]{0,1:T(8,128)S(1)} %get-tuple-element.187, f32[768]{0:T(1024)S(1)} %convert_element_type.165, ...), kind=kOutput, calls=%fused_computation.24 | convolution fusion | flops 5043388416 | bytes 39348224 | tf_op jit(solution)/shard_map/dot_general | solution.py:175
  211.0 9.3 %fusion.78 = (f32[1024]{0:T(1024)S(1)}, f32[1024,768]{0,1:T(8,128)S(1)}) fusion(f32[768]{0:T(1024)S(1)} %copy-done.41, bf16[1024,3072]{1,0:T(8,128)(2,1)} %get-tuple-element.167, bf16[3072,768]{1,0:T(8,128)(2,1)} %all-gather.12.cloned.1.call-done, f32[768]{0:T(1024)S(1)} %convert_element_type.165, f32[768]{0:T(1024)S(1)} %convert_element_type.164, ...), kind=kOutput, calls=%fused_computation.160 | convolution fusion | flops 4837342208 | bytes 17323008 | tf_op jit(solution)/shard_map/dot_general | solution.py:179
  220.8 3.5 multiply_reduce_fusion.2
  224.3 3.6 convert_reduce_fusion.2
  227.9 19.4 %convert_reduce_fusion = (f32[3072]{0:T(1024)}, bf16[1024,3072]{1,0:T(8,128)(2,1)}) fusion(f32[1024,3072]{1,0:T(8,128)} %get-tuple-element.168, bf16[3072,768]{1,0:T(8,128)(2,1)} %all-gather.12.cloned.1.call-done, f32[1024,768]{0,1:T(8,128)} %get-tuple-element.162, f32[1024,3072]{1,0:T(8,128)} %get-tuple-element.188, f32[3072]{0:T(1024)S(1)} %bitcast.136), kind=kOutput, calls=%fused_computation.20 | convolution fusion | flops 4886098944 | bytes 39346176 | tf_op jit(solution)/shard_map/nd,fd->nf/dot_general | solution.py:221
  247.3 11.0 %multiply_reduce_fusion.3 = (f32[768]{0:T(1024)}, f32[1024]{0:T(1024)S(1)}, f32[1024]{0:T(1024)S(1)}, f32[768]{0:T(1024)}, f32[1024,768]{0,1:T(8,128)S(1)}) fusion(f32[1024,768]{0,1:T(8,128)S(1)} %get-tuple-element.187, f32[1024]{0:T(1024)S(1)} %add_rsqrt_fusion.1, f32[1024]{0:T(1024)S(1)} %broadcast_multiply_fusion.9, f32[768]{0:T(1024)S(1)} %convert_element_type.164, ...), kind=kOutput, calls=%fused_computation.50 | convolution fusion | flops 4839698432 | bytes 20472832 | tf_op jit(solution)/shard_map/nf,df->nd/dot_general | solution.py:228
  258.3 1.7 convert_reduce_fusion.3
  260.0 1.4 convolution_convert_fusion
  261.8 13.4 %fusion.5 = f32[12,64,1024]{2,1,0:T(8,128)} fusion(bf16[512,12,64]{0,2,1:T(8,128)(2,1)S(1)} %bitcast.127, f32[12,512]{1,0:T(8,128)S(1)} %copy-done.24, f32[12,512,1024]{2,1,0:T(8,128)} %get-tuple-element.183, pred[512,1024]{1,0:T(8,128)(4,1)S(1)} %copy-done.8), kind=kOutput, calls=%fused_computation.18 | convolution fusion | flops 830472192 | bytes 29646848 | tf_op jit(solution)/shard_map/while/body/eval_jaxpr/hqk,qhd->khd/dot_general | solution.py:91
  275.3 20.3 %multiply_reduce_fusion = (f32[12,512]{1,0:T(8,128)S(1)}, f32[12,512,1024]{2,1,0:T(8,128)}) fusion(f32[12,512]{1,0:T(8,128)S(1)} %copy-done.24, f32[12,512,1024]{2,1,0:T(8,128)} %get-tuple-element.183, pred[512,1024]{1,0:T(8,128)(4,1)S(1)} %copy-done.8, bf16[512,12,64]{0,2,1:T(8,128)(2,1)S(1)} %bitcast.128, bf16[1,1024,3,12,64]{1,4,3,2,0:T(8,128)(2,1)} %bitcast.112), kind=kOutput, calls=%fused_computation.1 | convolution fusion | flops 836757504 | bytes 53264384 | tf_op jit(solution)/shard_map/while/body/eval_jaxpr/qhd,khd->hqk/dot_general | solution.py:88
  295.6 20.4 %multiply_reduce_fusion.1 = (f32[12,512]{1,0:T(8,128)S(1)}, f32[12,512,1024]{2,1,0:T(8,128)}) fusion(f32[12,512]{1,0:T(8,128)S(1)} %copy-done.23, f32[12,512,1024]{2,1,0:T(8,128)} %get-tuple-element.185, pred[512,1024]{1,0:T(8,128)(4,1)S(1)} %copy-done.6, bf16[512,12,64]{0,2,1:T(8,128)(2,1)S(1)} %bitcast.125, bf16[1,1024,3,12,64]{1,4,3,2,0:T(8,128)(2,1)} %bitcast.113), kind=kOutput, calls=%fused_computation.4 | convolution fusion | flops 836757504 | bytes 53264384 | tf_op jit(solution)/shard_map/while/body/eval_jaxpr/qhd,khd->hqk/dot_general | solution.py:88
  316.0 42.6 %multiply_convert_fusion = (bf16[12,512,1024]{2,1,0:T(8,128)(2,1)}, bf16[12,512,1024]{2,1,0:T(8,128)(2,1)}) fusion(f32[12,512,1024]{2,1,0:T(8,128)} %get-tuple-element.196, f32[12,512]{1,0:T(8,128)S(1)} %get-tuple-element.195, f32[12,512]{1,0:T(8,128)S(1)} %copy-done.24, f32[12,512,1024]{2,1,0:T(8,128)} %get-tuple-element.183, ...), kind=kLoop, calls=%fused_computation | loop fusion | flops 75497472 | bytes 126976000 | tf_op jit(solution)/shard_map/while/body/eval_jaxpr/convert_element_type | solution.py:98
  358.6 8.6 %multiply_bitcast_fusion.2 = bf16[512,12,64]{0,2,1:T(8,128)(2,1)S(1)} fusion(bf16[12,512,1024]{2,1,0:T(8,128)(2,1)} %get-tuple-element.200, bf16[1,1024,3,12,64]{1,4,3,2,0:T(8,128)(2,1)S(1)} %bitcast.119), kind=kOutput, calls=%fused_computation.81 | convolution fusion | flops 806092800 | bytes 14942208 | tf_op jit(solution)/shard_map/while/body/eval_jaxpr/hqk,khd->qhd/dot_general | solution.py:100
  367.2 7.0 fusion.43
  374.3 14.0 %add_bitcast_fusion = bf16[1,1024,1,12,64]{1,4,3,2,0:T(8,128)(2,1)} fusion(f32[12,64,1024]{2,1,0:T(8,128)} %fusion.5, bf16[512,12,64]{0,2,1:T(8,128)(2,1)S(1)} %bitcast.126, f32[12,512]{1,0:T(8,128)S(1)} %copy-done.23, f32[12,512,1024]{2,1,0:T(8,128)} %get-tuple-element.185, pred[512,1024]{1,0:T(8,128)(4,1)S(1)} %copy-done.7), kind=kOutput, calls=%fused_computation.53 | convolution fusion | flops 832045056 | bytes 31219712 | tf_op jit(solution)/shard_map/while/body/eval_jaxpr/hqk,qhd->khd/dot_general | solution.py:91
  388.3 8.6 %multiply_bitcast_fusion.1 = bf16[512,12,64]{0,2,1:T(8,128)(2,1)S(1)} fusion(bf16[12,512,1024]{2,1,0:T(8,128)(2,1)} %get-tuple-element.199, bf16[1,1024,3,12,64]{1,4,3,2,0:T(8,128)(2,1)S(1)} %bitcast.121), kind=kOutput, calls=%fused_computation.80 | convolution fusion | flops 806092800 | bytes 14942208 | tf_op jit(solution)/shard_map/while/body/eval_jaxpr/hqk,khd->qhd/dot_general | solution.py:100
  396.9 7.1 multiply_bitcast_fusion
  405.1 2.2 copy-done.12
  407.3 5.8 convolution_bitcast_fusion
  413.1 8.0 copy.78
  421.2 5.4 fusion.53
  426.7 10.8 %fusion.67 = f32[768,3072]{1,0:T(8,128)} fusion(bf16[1024,3072]{1,0:T(8,128)(2,1)} %get-tuple-element.198, f32[1024,768]{0,1:T(8,128)S(1)} %copy-done.10, f32[768]{0:T(1024)S(1)} %copy-done.40, f32[768]{0:T(1024)S(1)} %convert_element_type.164, f32[1024]{0:T(1024)S(1)} %add_rsqrt_fusion.1, f32[1024]{0:T(1024)S(1)} %broadcast_multiply_fusion.9), kind=kOutput, calls=%fused_computation.152 | convolution fusion | flops 4835770368 | bytes 18888704 | tf_op jit(solution)/shard_map/nd,nf->df/dot_general | solution.py:227
  437.6 1.9 copy-done.14
  439.4 10.3 %fusion.56 = f32[3072,768]{1,0:T(8,128)} fusion(bf16[1024,3072]{1,0:T(8,128)(2,1)} %get-tuple-element.167, f32[1024,768]{0,1:T(8,128)S(1)} %copy-done.14), kind=kOutput, calls=%fused_computation.141 | convolution fusion | flops 4832624640 | bytes 18874368 | tf_op jit(solution)/shard_map/nf,nd->fd/dot_general | solution.py:220
  449.8 47.4 %reduce-scatter.13.cloned.1.call-done = f32[96,2304]{1,0:T(8,128)} async-done(((f32[768,2304]{1,0:T(8,128)}), f32[96,2304]{1,0:T(8,128)}) %reduce-scatter.13.cloned.1.call-update) | async-done | bytes 884752
  497.3 2.6 copy.79
  499.8 35.2 %reduce-scatter.7.cloned.1.call-done = f32[96,768]{1,0:T(8,128)} async-done(((f32[768,768]{1,0:T(8,128)}), f32[96,768]{1,0:T(8,128)}) %reduce-scatter.7.cloned.1.call-update) | async-done | bytes 294928 | tf_op jit(solution)/shard_map/reduce_scatter | solution.py:281
  535.0 100.7 %reduce-scatter.9.cloned.1.call-done = f32[96,3072]{1,0:T(8,128)} async-done(((f32[768,3072]{1,0:T(8,128)}), f32[96,3072]{1,0:T(8,128)}) %reduce-scatter.9.cloned.1.call-update) | async-done | bytes 1179664 | tf_op jit(solution)/shard_map/reduce_scatter | solution.py:232
  635.7 100.2 %reduce-scatter.11.cloned.1.call-done = f32[384,768]{1,0:T(8,128)} async-done(((f32[3072,768]{1,0:T(8,128)}), f32[384,768]{1,0:T(8,128)}) %reduce-scatter.11.cloned.1.call-update) | async-done | bytes 1179664 | tf_op jit(solution)/shard_map/reduce_scatter | solution.py:234
  737.9 1.6 copy.71
  739.6 9.6 %fusion.32 = bf16[1,1024,768]{1,2,0:T(8,128)(2,1)} fusion(f32[1024,768]{0,1:T(8,128)} %copy-done.13, bf16[768,2304]{1,0:T(8,128)(2,1)} %all-gather.6.cloned.1.call-done, bf16[1024,2304]{0,1:T(8,128)(2,1)} %bitcast.124), kind=kOutput, calls=%fused_computation.86 | convolution fusion | flops 3625451520 | bytes 12976128 | tf_op jit(solution)/shard_map/nc,dc->nd/dot_general | solution.py:276
  749.2 2.6 copy.72
  752.0 26.4 %all-reduce.15 = (f32[1536]{0:T(1024)S(1)}, f32[768]{0:T(1024)S(1)}, f32[768]{0:T(1024)S(1)}, f32[768]{0:T(1024)S(1)}, f32[3072]{0:T(1024)S(1)}, /*index=5*/f32[...) all-reduce(f32[1536]{0:T(1024)S(1)} %pad_maximum_fusion.2, ...), channel_id=3, replica_groups=mesh['grp'=4,'fsdp'=8] {'fsdp'}, use_global_device_ids=true, to_apply=%region_18.19.clone | all-reduce | flops 9216 | bytes 73728
  779.1 10.1 %all-reduce.16 = (f32[192]{0:T(256)S(1)}, f32[96]{0:T(128)S(1)}, f32[96]{0:T(128)S(1)}, f32[96]{0:T(128)S(1)}, f32[384]{0:T(512)S(1)}, /*index=5*/f32[96]{0:T(128)S(1)}, f32[96]{0:T(128)S(1)}, f32[96]{0:T(128)S(1)}) all-reduce(f32[192]{0:T(256)S(1)} %dynamic-slice.9, ...), channel_id=1, replica_groups=mesh['grp'=4,'fsdp'=8] {'grp'}, use_global_device_ids=true, to_apply=%region_19.20 | all-reduce | flops 1152 | bytes 9216 | tf_op jit(solution)/shard_map/psum | solution.py:286
  793.5 2.6 fusion.38
  796.1 41.6 %all-reduce.21.cloned.1.call-done = (f32[96,2304]{0,1:T(8,128)}, f32[96,768]{1,0:T(8,128)}, f32[96,3072]{1,0:T(8,128)}, f32[384,768]{1,0:T(8,128)}) async-done(((f32[96,2304]{0,1:T(8,128)}, f32[96,768]{1,0:T(8,128)}, f32[96,3072]{1,0:T(8,128)}, f32[384,768]{1,0:T(8,128)}), (f32[96,2304]{0,1:T(8,128)}, f32[96,768]{1,0:T(8,128)}, f32[96,3072]{1,0:T(8,128)}, ...) | async-done | bytes 3538960 | tf_op jit(solution)/shard_map/psum | solution.py:286
  837.7 1.5 broadcast_multiply_fusion.2
  839.2 1.3 copy.73
  840.5 1.7 broadcast_multiply_fusion.3
  842.2 1.1 broadcast_multiply_fusion.1
  843.3 1.1 broadcast_multiply_fusion
  (188 shorter events, 17.9 us)
Async XLA Ops:
  7.2 65.2 %copy-start.27 = (s32[1,1024]{1,0:T(1,128)S(1)}, s32[1,1024]{1,0:T(1,128)}, u32[]{:S(2)}) copy-start(s32[1,1024]{1,0:T(1,128)} %param.17) | copy-start | bytes 12292
  7.2 63.6 %copy-start.17 = (bf16[1,1024,768]{2,1,0:T(8,128)(2,1)S(1)}, bf16[1,1024,768]{2,1,0:T(8,128)(2,1)}, u32[]{:S(2)}) copy-start(bf16[1,1024,768]{2,1,0:T(8,128)(2,1)} %param.16) | copy-start | bytes 4718596
  7.2 66.6 %all-gather.6.cloned.1.call-start = ((), (), s32[]{:S(2)}) async-start(), calls=%async_computation.4 | async-start | bytes 3981312 | tf_op jit(solution)/shard_map/all_gather | solution.py:136
  7.9 160.2 %all-gather.8.cloned.1.call-start = ((), (), s32[]{:S(2)}) async-start(), calls=%async_computation.5 | async-start | bytes 1327104 | tf_op jit(solution)/shard_map/all_gather | solution.py:138
  8.7 163.8 %all-gather.10.cloned.1.call-start = ((), (), s32[]{:S(2)}) async-start(), calls=%async_computation.6 | async-start | bytes 5308416 | tf_op jit(solution)/shard_map/all_gather | solution.py:168
  9.4 201.5 %all-gather.12.cloned.1.call-start = ((), (), s32[]{:S(2)}) async-start(), calls=%async_computation.7 | async-start | bytes 5308416 | tf_op jit(solution)/shard_map/all_gather | solution.py:170
  10.0 487.3 %reduce-scatter.13.cloned.1.call-start = ((), (), s32[]{:S(2)}) async-start(), calls=%async_computation.11 | async-start | bytes 7962624
  10.1 8.7 %copy-start.46 = (s32[8]{0:T(128)}, s32[8]{0:T(128)S(1)}, u32[]{:S(2)}) copy-start(s32[8]{0:T(128)S(1)} %iota_add_fusion) | copy-start | bytes 100
  53.6 157.3 %copy-start.39 = (f32[768]{0:T(1024)}, f32[768]{0:T(1024)S(1)}, u32[]{:S(2)}) copy-start(f32[768]{0:T(1024)S(1)} %convert_element_type.165) | copy-start | bytes 9220
  73.8 80.2 %copy-start.5 = (pred[512,1024]{1,0:T(8,128)(4,1)}, pred[512,1024]{1,0:T(8,128)(4,1)S(1)}, u32[]{:S(2)}) copy-start(pred[512,1024]{1,0:T(8,128)(4,1)S(1)} %get-tuple-element.174) | copy-start | bytes 1572868
  88.2 27.9 %copy-start.2 = (bf16[1024,2304]{0,1:T(8,128)(2,1)S(1)}, bf16[1024,2304]{0,1:T(8,128)(2,1)}, u32[]{:S(2)}) copy-start(bf16[1024,2304]{0,1:T(8,128)(2,1)} %copy.65) | copy-start | bytes 14155780
  103.1 16.3 %copy-start.1 = (f32[12,512,1024]{2,1,0:T(8,128)S(1)}, f32[12,512,1024]{2,1,0:T(8,128)}, u32[]{:S(2)}) copy-start(f32[12,512,1024]{2,1,0:T(8,128)} %get-tuple-element.183) | copy-start | bytes 75497472
  140.9 15.8 %copy-start = (f32[12,512,1024]{2,1,0:T(8,128)S(1)}, f32[12,512,1024]{2,1,0:T(8,128)}, u32[]{:S(2)}) copy-start(f32[12,512,1024]{2,1,0:T(8,128)} %get-tuple-element.185) | copy-start | bytes 75497472
  172.1 86.2 %copy-start.9 = (f32[1024,768]{0,1:T(8,128)}, f32[1024,768]{0,1:T(8,128)S(1)}, u32[]{:S(2)}) copy-start(f32[1024,768]{0,1:T(8,128)S(1)} %get-tuple-element.187) | copy-start | bytes 9437188
  172.5 38.4 %copy-start.41 = (f32[768]{0:T(1024)S(1)}, f32[768]{0:T(1024)}, u32[]{:S(2)}) copy-start(f32[768]{0:T(1024)} %convert_element_type.169) | copy-start | bytes 9220
  210.9 9.8 %copy-start.19 = (bf16[1,1024,768]{1,2,0:T(8,128)(2,1)S(1)}, bf16[1,1024,768]{1,2,0:T(8,128)(2,1)}, u32[]{:S(2)}) copy-start(bf16[1,1024,768]{1,2,0:T(8,128)(2,1)} %copy.67) | copy-start | bytes 4718596
  210.9 9.8 %copy-start.28 = (s32[1,1024]{1,0:T(1,128)S(1)}, s32[1,1024]{1,0:T(1,128)}, u32[]{:S(2)}) copy-start(s32[1,1024]{1,0:T(1,128)} %param.17) | copy-start | bytes 12292
  210.9 9.8 %copy-start.30 = (f32[768]{0:T(1024)S(1)}, f32[768]{0:T(1024)}, u32[]{:S(2)}) copy-start(f32[768]{0:T(1024)} %convert_element_type.170) | copy-start | bytes 9220
  210.9 9.8 %copy-start.47 = (s32[8]{0:T(128)S(1)}, s32[8]{0:T(128)}, u32[]{:S(2)}) copy-start(s32[8]{0:T(128)} %copy-done.46) | copy-start | bytes 100
  210.9 9.8 %copy-start.49 = (f32[8]{0:T(128)S(1)}, f32[8]{0:T(128)}, u32[]{:S(2)}) copy-start(f32[8]{0:T(128)} %broadcast_maximum_fusion) | copy-start | bytes 100
  211.0 9.8 %copy-start.52 = (f32[1,8,768]{2,1,0:T(8,128)S(1)}, f32[1,8,768]{2,1,0:T(8,128)}, u32[]{:S(2)}) copy-start(f32[1,8,768]{2,1,0:T(8,128)} %param.31) | copy-start | bytes 73732
  220.3 4.0 copy-start.3
  220.3 4.0 copy-start.25
  220.7 3.6 copy-start.32
  220.8 7.1 copy-start.34
  258.3 1.7 copy-start.51
  260.0 1.7 copy-start.13
  260.0 1.8 copy-start.8
  260.0 1.8 copy-start.24
  261.8 33.7 %copy-start.15 = (bf16[512,768]{0,1:T(8,128)(2,1)}, bf16[512,768]{0,1:T(8,128)(2,1)S(1)}, u32[]{:S(2)}) copy-start(bf16[512,768]{0,1:T(8,128)(2,1)S(1)} %get-tuple-element.170) | copy-start | bytes 2359300
  275.3 20.3 %copy-start.6 = (pred[512,1024]{1,0:T(8,128)(4,1)S(1)}, pred[512,1024]{1,0:T(8,128)(4,1)}, u32[]{:S(2)}) copy-start(pred[512,1024]{1,0:T(8,128)(4,1)} %copy-done.5) | copy-start | bytes 1572868
  275.3 20.3 %copy-start.23 = (f32[12,512]{1,0:T(8,128)S(1)}, f32[12,512]{1,0:T(8,128)}, u32[]{:S(2)}) copy-start(f32[12,512]{1,0:T(8,128)} %log_add_fusion.1) | copy-start | bytes 73732
  295.6 63.0 %slice-start = ((s8[4718592]{0:T(1024)(128)(4,1)}), s8[524288]{0:T(1024)(128)(4,1)S(1)}, s32[]{:S(2)}) async-start(s8[4718592]{0:T(1024)(128)(4,1)} %bitcast.117), calls=%async_computation.13 | async-start | bytes 1048576
  316.0 42.6 %slice-start.1 = ((s8[4718592]{0:T(1024)(128)(4,1)}), s8[4194304]{0:T(1024)(128)(4,1)S(1)}, s32[]{:S(2)}) async-start(s8[4718592]{0:T(1024)(128)(4,1)} %bitcast.117), calls=%async_computation.14 | async-start | bytes 8388608
  367.2 7.0 copy-start.7
  367.2 7.0 copy-start.16
  396.9 7.3 copy-start.20
  404.2 3.1 copy-start.18
  405.0 2.3 copy-start.12
  421.1 5.5 copy-start.10
  421.2 5.5 copy-start.40
  421.2 113.8 %reduce-scatter.7.cloned.1.call-start = ((), (), s32[]{:S(2)}) async-start(), calls=%async_computation.8 | async-start | bytes 2654208 | tf_op jit(solution)/shard_map/reduce_scatter | solution.py:281
  426.6 209.1 %reduce-scatter.9.cloned.1.call-start = ((), (), s32[]{:S(2)}) async-start(), calls=%async_computation.9 | async-start | bytes 10616832 | tf_op jit(solution)/shard_map/reduce_scatter | solution.py:232
  437.5 1.9 copy-start.14
  437.5 298.4 %reduce-scatter.11.cloned.1.call-start = ((), (), s32[]{:S(2)}) async-start(), calls=%async_computation.10 | async-start | bytes 10616832 | tf_op jit(solution)/shard_map/reduce_scatter | solution.py:234
  449.8 288.1 %copy-start.11 = (bf16[1,1024,768]{1,2,0:T(8,128)(2,1)S(1)}, bf16[1,1024,768]{1,2,0:T(8,128)(2,1)}, u32[]{:S(2)}) copy-start(bf16[1,1024,768]{1,2,0:T(8,128)(2,1)} %get-tuple-element.169) | copy-start | bytes 4718596
  449.8 387.9 %all-reduce.21.cloned.1.call-start = ((), (), s32[]{:S(2)}) async-start(), calls=%async_computation.12 | async-start | bytes 7667712 | tf_op jit(solution)/shard_map/psum | solution.py:286
  739.5 12.5 %copy-start.36 = (f32[768]{0:T(1024)S(1)}, f32[768]{0:T(1024)}, u32[]{:S(2)}) copy-start(f32[768]{0:T(1024)} %get-tuple-element.161) | copy-start | bytes 9220
  739.5 12.5 %copy-start.37 = (f32[768]{0:T(1024)S(1)}, f32[768]{0:T(1024)}, u32[]{:S(2)}) copy-start(f32[768]{0:T(1024)} %get-tuple-element.163) | copy-start | bytes 9220
  739.5 12.5 %copy-start.38 = (f32[3072]{0:T(1024)S(1)}, f32[3072]{0:T(1024)}, u32[]{:S(2)}) copy-start(f32[3072]{0:T(1024)} %get-tuple-element.197) | copy-start | bytes 36868
  739.5 12.5 %copy-start.42 = (f32[768]{0:T(1024)S(1)}, f32[768]{0:T(1024)}, u32[]{:S(2)}) copy-start(f32[768]{0:T(1024)} %get-tuple-element.126) | copy-start | bytes 9220
  739.5 12.5 %copy-start.43 = (f32[768]{0:T(1024)S(1)}, f32[768]{0:T(1024)}, u32[]{:S(2)}) copy-start(f32[768]{0:T(1024)} %get-tuple-element.132) | copy-start | bytes 9220
  739.5 12.5 %copy-start.44 = (f32[768]{0:T(1024)S(1)}, f32[768]{0:T(1024)}, u32[]{:S(2)}) copy-start(f32[768]{0:T(1024)} %get-tuple-element.128) | copy-start | bytes 9220
  739.5 12.5 %copy-start.45 = (f32[768]{0:T(1024)S(1)}, f32[768]{0:T(1024)}, u32[]{:S(2)}) copy-start(f32[768]{0:T(1024)} %get-tuple-element.133) | copy-start | bytes 9220
  739.5 53.9 %copy-start.4 = (f32[1024,768]{0,1:T(8,128)S(1)}, f32[1024,768]{0,1:T(8,128)}, u32[]{:S(2)}) copy-start(f32[1024,768]{0,1:T(8,128)} %copy-done.3) | copy-start | bytes 9437188
  739.5 53.9 %copy-start.26 = (f32[1024]{0:T(1024)S(1)}, f32[1024]{0:T(1024)}, u32[]{:S(2)}) copy-start(f32[1024]{0:T(1024)} %copy-done.25) | copy-start | bytes 12292
  739.6 53.9 %copy-start.29 = (s32[1,1024]{1,0:T(1,128)S(1)}, s32[1,1024]{1,0:T(1,128)}, u32[]{:S(2)}) copy-start(s32[1,1024]{1,0:T(1,128)} %param.17) | copy-start | bytes 12292
  739.6 53.9 %copy-start.31 = (f32[768]{0:T(1024)S(1)}, f32[768]{0:T(1024)}, u32[]{:S(2)}) copy-start(f32[768]{0:T(1024)} %convert_element_type.170) | copy-start | bytes 9220
  739.6 53.9 %copy-start.33 = (f32[768]{0:T(1024)S(1)}, f32[768]{0:T(1024)}, u32[]{:S(2)}) copy-start(f32[768]{0:T(1024)} %convert_element_type.171) | copy-start | bytes 9220
  739.6 53.9 %copy-start.35 = (f32[1024]{0:T(1024)S(1)}, f32[1024]{0:T(1024)}, u32[]{:S(2)}) copy-start(f32[1024]{0:T(1024)} %copy-done.34) | copy-start | bytes 12292
  739.6 53.9 %copy-start.48 = (s32[8]{0:T(128)S(1)}, s32[8]{0:T(128)}, u32[]{:S(2)}) copy-start(s32[8]{0:T(128)} %copy-done.46) | copy-start | bytes 100
  739.6 53.9 %copy-start.50 = (f32[8]{0:T(128)S(1)}, f32[8]{0:T(128)}, u32[]{:S(2)}) copy-start(f32[8]{0:T(128)} %broadcast_maximum_fusion) | copy-start | bytes 100
  837.7 4.5 copy-start.22
  837.7 5.6 copy-start.21
Sparse Core Ops, SparseCore 0:
  9.7 44.7 all-gather.5
  56.1 21.7 all-gather.7
  79.5 50.7 all-gather.9
  131.8 49.9 all-gather.11
  421.3 75.9 reduce-scatter.12
  499.5 35.5 reduce-scatter.6
  537.3 98.3 reduce-scatter.8
  638.0 97.8 reduce-scatter.10
  740.0 97.6 all-reduce.20
where the time goes:
time: 860 us; the launch traced here: 851 us
  waiting for transfers between devices  328 us (38%)
  matrix products  284 us (33%)
  other arithmetic  92.9 us (11%)
  blocking collectives  81.6 us (9%)
  local copies, waits for them, and re-layouts  46.9 us (5%)
  between operations  18.3 us (2%)
    reduce_scatter x1, waiting for transfers between devices, per_device(): lax.psum_scatter(expand_term, 'fsdp', scatter_dimension=0, tiled=True)  101 us
    reduce_scatter x1, waiting for transfers between devices, per_device(): lax.psum_scatter(reduce_term, 'fsdp', scatter_dimension=0, tiled=True)  100 us
    unnamed x2, blocking collectives  58.7 us
    unnamed x10, waiting for transfers between devices  50.1 us
    convert_element_type x1, other arithmetic, attend_backward(): grad_scores = (weights * (grad_weights - inner_sum)).astype(jnp.bfloat16)  42.6 us
    psum x1, waiting for transfers between devices, per_device(): lax.psum((att_project, att_pbias, att_combine, att_cbias, att_gain, att_s...  41.6 us
    dot_general x2, matrix products, attend_backward(): jnp.einsum('qhd,khd->hqk', context_block, values_row, preferred_element_t...  40.7 us
    unnamed x141, local copies, waits for them, and re-layouts  39.1 us
  transfers between devices with their start and end apart: 9, of which 5 were waited for; matrix products, arithmetic and copies ran while one was open for 23% of the time, Pallas kernels for 0%

commit v1 on v0

v1 whole, which is shorter than its diff:
```python
from functools import partial

import jax
import jax.numpy as jnp
from jax import lax
from jax.experimental import pallas as pl
from jax.experimental.pallas import tpu as pltpu
from jax.sharding import PartitionSpec as P

H = 12
DH = 64
SEG = 8
LANES = 128
NEG_FILL = -1e30
EPSILON = 1e-12
BF16 = jnp.bfloat16
F32 = jnp.float32

TAIL_P = 0.33
TAIL = (
    0.13275454438237264,
    0.11835055488372218,
    0.18469205342974412,
    -0.0957394408156175,
    0.3375615034491361,
    -0.2238704213061762,
    0.04625121306008233,
)
LOG2E = 1.4426950408889634
INV_SQRT_2PI = 0.3989422804014327


def cost(flops, *arrays):
    moved = sum(a.size * a.dtype.itemsize for a in arrays)
    return pl.CostEstimate(flops=int(flops), transcendentals=0, bytes_accessed=int(moved))


def nn(left, right):
    return lax.dot_general(left, right, (((1,), (0,)), ((), ())), preferred_element_type=F32)


def nt(left, right):
    return lax.dot_general(left, right, (((1,), (1,)), ((), ())), preferred_element_type=F32)


def tn(left, right):
    return lax.dot_general(left, right, (((0,), (0,)), ((), ())), preferred_element_type=F32)


def shape_of(dims, kind):
    return jax.ShapeDtypeStruct(dims, kind)


def full_spec(dims):
    return pl.BlockSpec(dims, lambda *_: (0,) * len(dims))


def normal_parts(x):
    bell = jnp.exp2(x * x * (-0.5 * LOG2E))
    t = 1.0 / (1.0 + TAIL_P * jnp.abs(x))
    poly = jnp.full_like(t, TAIL[-1])
    for coefficient in TAIL[-2::-1]:
        poly = poly * t + coefficient
    tail = poly * t * bell
    return jnp.where(x >= 0, 1.0 - tail, tail), bell * INV_SQRT_2PI


def project_kernel(x_ref, w_ref, b_ref, o_ref):
    rows = x_ref.shape[0]
    step = min(256, rows)
    for at in range(0, rows, step):
        o_ref[0, at : at + step, :] = (nn(x_ref[at : at + step, :], w_ref[0]) + b_ref[0]).astype(BF16)


def project(x, weights, bias):
    rows, width = x.shape
    half = width // 2
    return pl.pallas_call(
        project_kernel,
        out_shape=shape_of((3, rows, width), BF16),
        grid=(3, 2),
        in_specs=[
            full_spec((rows, width)),
            pl.BlockSpec((1, width, half), lambda t, j: (t, 0, j)),
            pl.BlockSpec((1, 1, half), lambda t, j: (t, 0, j)),
        ],
        out_specs=pl.BlockSpec((1, rows, half), lambda t, j: (t, 0, j)),
        cost_estimate=cost(6 * rows * width * width, x, weights),
        name="project",
    )(x, weights, bias)


def window_sizes(block, length):
    sizes = [block + extra for extra in (128, 256, 384, 512) if block + extra < length]
    return sizes + [length]


def key_limits(seg, block):
    length = seg.shape[0]
    rows = seg.reshape(length // block, block)
    place = jnp.arange(length, dtype=jnp.int32)[None, :]
    low = jnp.min(jnp.where(seg[None, :] == rows[:, :1], place, length), axis=1)
    high = jnp.max(jnp.where(seg[None, :] == rows[:, -1:], place + 1, 0), axis=1)
    low = low // LANES * LANES
    sizes = window_sizes(block, length)
    size = jnp.full_like(low, sizes[-1])
    for candidate in sizes[-2::-1]:
        size = jnp.where(high - low <= candidate, candidate, size)
    return jnp.stack([jnp.minimum(low, length - size), size])


def for_window(limits_ref, block, sizes, body):
    start = limits_ref[0, block]
    for size in sizes:

        @pl.when(limits_ref[1, block] == size)
        def _(size=size):
            body(pl.multiple_of(start, LANES), size)


def attend_forward_kernel(sizes, limits_ref, q_ref, k_ref, v_ref, segq_ref, segk_ref, o_ref, lse_ref):
    first = lax.broadcasted_iota(jnp.int32, (1, LANES), 1) < DH
    rows = q_ref.shape[1]
    scale = jnp.asarray(DH ** (-0.5), BF16)

    def body(start, size):
        query = q_ref[0] * scale
        keys = k_ref[0, pl.ds(start, size), :]
        values = v_ref[0, pl.ds(start, size), :]
        allowed = segq_ref[...] == segk_ref[:, pl.ds(start, size)]
        parts = []
        stats = []
        for mine in (first, jnp.logical_not(first)):
            scores = nt(jnp.where(mine, query, jnp.zeros_like(query)), keys)
            scores = jnp.where(allowed, scores, NEG_FILL)
            highest = jnp.max(scores, axis=1, keepdims=True)
            exponent = jnp.exp(scores - highest)
            total = jnp.sum(exponent, axis=1, keepdims=True)
            parts.append(nn(exponent.astype(BF16), values) / total)
            stats.append(highest + jnp.log(total))
        o_ref[...] = jnp.where(first, parts[0], parts[1]).astype(BF16)
        both = jnp.where(first, stats[0], stats[1])
        flipped = both.T
        lse_ref[0, 0:1, :] = flipped[0:1, :]
        lse_ref[0, 1:2, :] = flipped[DH : DH + 1, :]

    for_window(limits_ref, pl.program_id(1), sizes, body)


def attend_forward(qkv, limits, seg_column, seg_row, block):
    _, length, width = qkv.shape
    pairs = width // LANES
    return pl.pallas_call(
        partial(attend_forward_kernel, window_sizes(block, length)),
        out_shape=(shape_of((length, width), BF16), shape_of((pairs, 8, length), F32)),
        grid_spec=pltpu.PrefetchScalarGridSpec(
            num_scalar_prefetch=1,
            grid=(pairs, length // block),
            in_specs=[
                pl.BlockSpec((1, block, LANES), lambda p, b, _: (0, b, p)),
                pl.BlockSpec((1, length, LANES), lambda p, b, _: (1, 0, p)),
                pl.BlockSpec((1, length, LANES), lambda p, b, _: (2, 0, p)),
                pl.BlockSpec((block, 1), lambda p, b, _: (b, 0)),
                pl.BlockSpec((1, length), lambda p, b, _: (0, 0)),
            ],
            out_specs=[
                pl.BlockSpec((block, LANES), lambda p, b, _: (b, p)),
                pl.BlockSpec((1, 8, block), lambda p, b, _: (p, 0, b)),
            ],
        ),
        cost_estimate=cost(8 * length * length * width, qkv),
        name="attend_forward",
    )(limits, qkv, qkv, qkv, seg_column, seg_row)


def attend_backward_kernel(
    sizes,
    limits_ref,
    q_ref,
    k_ref,
    v_ref,
    d_ref,
    lse_ref,
    segk_ref,
    segq_ref,
    grad_ref,
    sums_ref,
    dk_ref,
    dv_ref,
    dq_ref,
):
    block = pl.program_id(1)
    first = lax.broadcasted_iota(jnp.int32, (1, LANES), 1) < DH
    rows = q_ref.shape[1]
    scale = jnp.asarray(DH ** (-0.5), BF16)

    @pl.when(block == 0)
    def _():
        dk_ref[...] = jnp.zeros_like(dk_ref)
        dv_ref[...] = jnp.zeros_like(dv_ref)

    def body(start, size):
        query = q_ref[0] * scale
        grads = d_ref[...]
        keys = k_ref[0, pl.ds(start, size), :]
        values = v_ref[0, pl.ds(start, size), :]
        allowed = segk_ref[pl.ds(start, size), :] == segq_ref[...]
        grad_query = []
        grad_key = None
        for h, mine in enumerate((first, jnp.logical_not(first))):
            query_h = jnp.where(mine, query, jnp.zeros_like(query))
            grads_h = jnp.where(mine, grads, jnp.zeros_like(grads))
            scores = nt(keys, query_h)
            weights = jnp.where(allowed, jnp.exp(scores - lse_ref[0, h : h + 1, :]), 0.0)
            grad_weights = nt(values, grads_h)
            inner = jnp.sum(weights * grad_weights, axis=0, keepdims=True)
            grad_scores = (weights * (grad_weights - inner)).astype(BF16)
            dv_h = nn(weights.astype(BF16), grads_h)
            dk_h = nn(grad_scores, query_h)
            grad_query.append(tn(grad_scores, keys))
            grad_key, grad_value = (dk_h, dv_h) if grad_key is None else (grad_key + dk_h, grad_value + dv_h)
        dk_ref[pl.ds(start, size), :] += grad_key
        dv_ref[pl.ds(start, size), :] += grad_value
        place = pl.ds(pl.multiple_of(block * rows, rows), rows)
        dq_ref[place, :] = jnp.where(first, grad_query[0], grad_query[1]) * (DH ** (-0.5))

    for_window(limits_ref, block, sizes, body)

    @pl.when(block == pl.num_programs(1) - 1)
    def _():
        for t, source in enumerate((dq_ref, dk_ref, dv_ref)):
            low = source[...].astype(BF16)
            grad_ref[t] = low
            if t != 1:
                sums_ref[t : t + 1, :] = jnp.sum(low.astype(F32), axis=0, keepdims=True)


def attend_backward(qkv, grad_context, lse, limits, seg_column, seg_row, block, base, pairs, earlier=None):
    _, length, width = qkv.shape
    anywhere = pl.BlockSpec(memory_space=pl.ANY)
    made = (shape_of((3, length, width), BF16), shape_of((8, width), F32))
    kernel = partial(attend_backward_kernel, window_sizes(block, length))
    if earlier is not None:
        inner = kernel

        def kernel(limits_ref, *refs):
            inner(limits_ref, *refs[:7], *refs[9:])

    return pl.pallas_call(
        kernel,
        out_shape=made,
        grid_spec=pltpu.PrefetchScalarGridSpec(
            num_scalar_prefetch=1,
            grid=(pairs, length // block),
            in_specs=[
                pl.BlockSpec((1, block, LANES), lambda p, b, _: (0, b, base + p)),
                pl.BlockSpec((1, length, LANES), lambda p, b, _: (1, 0, base + p)),
                pl.BlockSpec((1, length, LANES), lambda p, b, _: (2, 0, base + p)),
                pl.BlockSpec((block, LANES), lambda p, b, _: (b, base + p)),
                pl.BlockSpec((1, 8, block), lambda p, b, _: (base + p, 0, b)),
                pl.BlockSpec((length, 1), lambda p, b, _: (0, 0)),
                pl.BlockSpec((1, block), lambda p, b, _: (0, b)),
            ]
            + ([] if earlier is None else [anywhere] * 2),
            out_specs=[
                pl.BlockSpec((3, length, LANES), lambda p, b, _: (0, 0, base + p)),
                pl.BlockSpec((8, LANES), lambda p, b, _: (0, base + p)),
            ],
            scratch_shapes=[pltpu.VMEM((length, LANES), F32)] * 3,
        ),
        input_output_aliases={} if earlier is None else {8: 0, 9: 1},
        cost_estimate=cost(12 * length * length * LANES * pairs, qkv),
        name="attend_backward",
    )(limits, qkv, qkv, qkv, grad_context, lse, seg_column, seg_row, *(earlier or ()))


def norm_values(values, gain, shift):
    average = jnp.mean(values, axis=-1, keepdims=True)
    centred = values - average
    variance = jnp.mean(centred * centred, axis=-1, keepdims=True)
    inverse = lax.rsqrt(variance + EPSILON)
    normed = centred * inverse
    return normed * gain + shift, normed, inverse


def norm_pull(grad_out, normed, inverse, gain):
    scaled = grad_out * gain
    mean_scaled = jnp.mean(scaled, axis=-1, keepdims=True)
    mean_product = jnp.mean(scaled * normed, axis=-1, keepdims=True)
    return inverse * (scaled - mean_scaled - normed * mean_product)


def column_sum(values):
    return jnp.sum(values, axis=0, keepdims=True)


def combine_kernel(c_ref, w_ref, x_ref, vec_ref, hidden_ref, low_ref, normed_ref, inverse_ref):
    attn = nn(c_ref[...], w_ref[0]) + vec_ref[0:1, :]
    hidden, normed, inverse = norm_values(x_ref[...].astype(F32) + attn, vec_ref[1:2, :], vec_ref[2:3, :])
    hidden_ref[...] = hidden
    low_ref[...] = hidden.astype(BF16)
    normed_ref[...] = normed
    inverse_ref[...] = inverse


def combine(context, weights, tokens, vectors, block):
    rows, width = context.shape
    row_spec = pl.BlockSpec((block, width), lambda b: (b, 0))
    return pl.pallas_call(
        combine_kernel,
        out_shape=(
            shape_of((rows, width), F32),
            shape_of((rows, width), BF16),
            shape_of((rows, width), F32),
            shape_of((rows, 1), F32),
        ),
        grid=(rows // block,),
        in_specs=[
            row_spec,
            pl.BlockSpec((1, width, width), lambda b: (3, 0, 0)),
            row_spec,
            full_spec(vectors.shape),
        ],
        out_specs=[row_spec, row_spec, row_spec, pl.BlockSpec((block, 1), lambda b: (b, 0))],
        cost_estimate=cost(4 * rows * width * width, context, tokens),
        name="combine",
    )(context, weights, tokens, vectors)


def expand_kernel(x_ref, w_ref, b_ref, act_ref, slope_ref):
    rows = x_ref.shape[0]
    step = min(256, rows)
    for at in range(0, rows, step):
        pre = nn(x_ref[at : at + step, :], w_ref[0]) + b_ref[0]
        mass, bell = normal_parts(pre)
        act_ref[at : at + step, :] = (pre * mass).astype(BF16)
        slope_ref[at : at + step, :] = (mass + pre * bell).astype(BF16)


def expand(hidden_low, weights, bias):
    rows, width = hidden_low.shape
    count = weights.shape[0]
    half = width // 2
    out_spec = pl.BlockSpec((rows, half), lambda t, j: (0, 2 * t + j))
    return pl.pallas_call(
        expand_kernel,
        out_shape=(shape_of((rows, count * width), BF16),) * 2,
        grid=(count, 2),
        in_specs=[
            full_spec((rows, width)),
            pl.BlockSpec((1, width, half), lambda t, j: (t, 0, j)),
            pl.BlockSpec((1, 1, half), lambda t, j: (t, 0, j)),
        ],
        out_specs=[out_spec, out_spec],
        cost_estimate=cost(12 * rows * count * width * width // 3, hidden_low, weights),
        name="expand",
    )(hidden_low, weights, bias)


def reduce_kernel(
    act_ref,
    w_ref,
    hidden_ref,
    vec_ref,
    cot_ref,
    pooled_cot_ref,
    seg_col_ref,
    seg_row_ref,
    out_ref,
    pooled_ref,
    grad_ref,
    grad_low_ref,
    sums_ref,
    share_ref,
):
    at = pl.program_id(0)
    rows = act_ref.shape[0]
    slot = lax.broadcasted_iota(jnp.int32, (16, 1), 0) + 1
    counts = jnp.sum((seg_row_ref[...] == slot).astype(F32), axis=1, keepdims=True)
    divisor = jnp.maximum(counts, 1.0)

    @pl.when(at == 0)
    def _():
        share_ref[...] = jnp.zeros_like(share_ref)
        share = pooled_cot_ref[...] / divisor[0:SEG]
        high = share.astype(BF16).astype(F32)
        share_ref[0:SEG, :] = high
        share_ref[2 * SEG : 3 * SEG, :] = share - high
        sums_ref[...] = jnp.zeros_like(sums_ref)
        pooled_ref[...] = jnp.zeros_like(pooled_ref)

    gain = vec_ref[1:2, :]
    branch = nn(act_ref[...], w_ref[...]) + vec_ref[0:1, :]
    result, normed, inverse = norm_values(hidden_ref[...] + branch, gain, vec_ref[2:3, :])
    out_ref[...] = result.astype(BF16)
    place = pl.ds(pl.multiple_of(at * rows, rows), rows)
    member = (seg_row_ref[:, place] == slot).astype(BF16)
    high = result.astype(BF16)
    rest = (result - high.astype(F32)).astype(BF16)
    pooled_ref[...] += (nn(member, high) + nn(member, rest))[0:SEG]
    lane = lax.broadcasted_iota(jnp.int32, (1, LANES), 1)
    chosen = jnp.where(lane < 2 * SEG, lane + 1, lane - 2 * SEG + 1)
    chosen = jnp.where(lane % (2 * SEG) < SEG, chosen, -1)
    chosen = jnp.where(lane < 4 * SEG, chosen, -1)
    spread = nn((seg_col_ref[...] == chosen).astype(BF16), share_ref[...].astype(BF16))
    grad_result = cot_ref[...].astype(F32) + spread
    grad_second = norm_pull(grad_result, normed, inverse, gain)
    grad_low = grad_second.astype(BF16)
    grad_ref[...] = grad_second
    grad_low_ref[...] = grad_low
    sums_ref[0:1, :] += column_sum(grad_result * normed)
    sums_ref[1:2, :] += column_sum(grad_result)
    sums_ref[2:3, :] += column_sum(grad_low.astype(F32))

    @pl.when(at == pl.num_programs(0) - 1)
    def _():
        pooled_ref[...] = pooled_ref[...] / divisor[0:SEG]


def reduce(act, weights, hidden, vectors, cotangent, pooled_cotangent, seg_column, seg_row, block):
    rows, width = hidden.shape
    depth = act.shape[1]
    row_spec = pl.BlockSpec((block, width), lambda b: (b, 0))
    return pl.pallas_call(
        reduce_kernel,
        out_shape=(
            shape_of((rows, width), BF16),
            shape_of((SEG, width), F32),
            shape_of((rows, width), F32),
            shape_of((rows, width), BF16),
            shape_of((8, width), F32),
        ),
        grid=(rows // block,),
        in_specs=[
            pl.BlockSpec((block, depth), lambda b: (b, 0)),
            full_spec(weights.shape),
            row_spec,
            full_spec(vectors.shape),
            row_spec,
            full_spec(pooled_cotangent.shape),
            pl.BlockSpec((block, 1), lambda b: (b, 0)),
            full_spec(seg_row.shape),
        ],
        out_specs=[
            row_spec,
            full_spec((SEG, width)),
            row_spec,
            row_spec,
            full_spec((8, width)),
        ],
        scratch_shapes=[pltpu.VMEM((LANES, width), F32)],
        cost_estimate=cost(3 * rows * width * depth, act, weights),
        name="reduce",
    )(act, weights, hidden, vectors, cotangent, pooled_cotangent, seg_column, seg_row)


def grad_pre_kernel(g_ref, w_ref, slope_ref, o_ref, sums_ref):
    rows = g_ref.shape[0]
    step = min(256, rows)
    total = None
    for at in range(0, rows, step):
        grad = nt(g_ref[at : at + step, :], w_ref[...]) * slope_ref[at : at + step, :].astype(F32)
        low = grad.astype(BF16)
        o_ref[at : at + step, :] = low
        part = column_sum(low.astype(F32))
        total = part if total is None else total + part
    sums_ref[...] = jnp.broadcast_to(total, sums_ref.shape)


def grad_pre_of(grad_branch, weights, slope):
    rows, width = grad_branch.shape
    depth = weights.shape[0]
    half = width // 2
    return pl.pallas_call(
        grad_pre_kernel,
        out_shape=(shape_of((rows, depth), BF16), shape_of((8, depth), F32)),
        grid=(depth // half,),
        in_specs=[
            full_spec((rows, width)),
            pl.BlockSpec((half, width), lambda j: (j, 0)),
            pl.BlockSpec((rows, half), lambda j: (0, j)),
        ],
        out_specs=[
            pl.BlockSpec((rows, half), lambda j: (0, j)),
            pl.BlockSpec((8, half), lambda j: (0, j)),
        ],
        cost_estimate=cost(3 * rows * width * depth, grad_branch, weights),
        name="grad_pre",
    )(grad_branch, weights, slope)


def grad_hidden_kernel(
    gp_ref, we_ref, second_ref, normed_ref, inverse_ref, vec_ref, wc_ref, first_ref, low_ref, context_ref, sums_ref
):
    @pl.when(pl.program_id(0) == 0)
    def _():
        sums_ref[...] = jnp.zeros_like(sums_ref)

    width = second_ref.shape[1]
    grad_hidden = second_ref[...]
    for t in range(we_ref.shape[0]):
        grad_hidden += nt(gp_ref[:, t * width : (t + 1) * width], we_ref[t])
    normed = normed_ref[...]
    grad_first = norm_pull(grad_hidden, normed, inverse_ref[...], vec_ref[1:2, :])
    low = grad_first.astype(BF16)
    first_ref[...] = grad_first
    low_ref[...] = low
    context_ref[...] = nt(low, wc_ref[0]).astype(BF16)
    sums_ref[0:1, :] += column_sum(grad_hidden * normed)
    sums_ref[1:2, :] += column_sum(grad_hidden)
    sums_ref[2:3, :] += column_sum(low.astype(F32))


def grad_hidden_of(grad_pre, expand_weights, grad_second, normed, inverse, vectors, attend_weights, block):
    rows, width = grad_second.shape
    row_spec = pl.BlockSpec((block, width), lambda b: (b, 0))
    return pl.pallas_call(
        grad_hidden_kernel,
        out_shape=(
            shape_of((rows, width), F32),
            shape_of((rows, width), BF16),
            shape_of((rows, width), BF16),
            shape_of((8, width), F32),
        ),
        grid=(rows // block,),
        in_specs=[
            pl.BlockSpec((block, grad_pre.shape[1]), lambda b: (b, 0)),
            full_spec(expand_weights.shape),
            row_spec,
            row_spec,
            pl.BlockSpec((block, 1), lambda b: (b, 0)),
            full_spec(vectors.shape),
            pl.BlockSpec((1, width, width), lambda b: (3, 0, 0)),
        ],
        out_specs=[row_spec, row_spec, row_spec, full_spec((8, width))],
        cost_estimate=cost(12 * rows * width * width, grad_pre, expand_weights),
        name="grad_hidden",
    )(grad_pre, expand_weights, grad_second, normed, inverse, vectors, attend_weights)


def token_grad_kernel(g_ref, w_ref, first_ref, o_ref):
    total = first_ref[...]
    for t in range(3):
        total += nt(g_ref[t], w_ref[t])
    o_ref[...] = total.astype(BF16)


def token_grad_of(grad_qkv, weights, grad_first, block):
    rows, width = grad_first.shape
    row_spec = pl.BlockSpec((block, width), lambda b: (b, 0))
    return pl.pallas_call(
        token_grad_kernel,
        out_shape=shape_of((rows, width), BF16),
        grid=(rows // block,),
        in_specs=[
            pl.BlockSpec((3, block, width), lambda b: (0, b, 0)),
            pl.BlockSpec((3, width, width), lambda b: (0, 0, 0)),
            row_spec,
        ],
        out_specs=row_spec,
        cost_estimate=cost(6 * rows * width * width, grad_qkv, weights),
        name="token_grad",
    )(grad_qkv, weights, grad_first)


AXES = ("grp", "fsdp")
TAIL_ROWS = 8


def hop(value, shards, move):
    pairs = []
    for g in range(4):
        for f in range(shards):
            to_g, to_f = move(g, f)
            pairs.append((g * shards + f, to_g * shards + to_f))
    return lax.ppermute(value, AXES, pairs)


def along(value, shards, by):
    return hop(value, shards, lambda g, f: (g, (f + 2 * by) % shards))


def swap_first(value, shards):
    return hop(value, shards, lambda g, f: (g ^ (1 + f % 2), f))


def swap_second(value, shards):
    return hop(value, shards, lambda g, f: (g ^ (2 - f % 2), f))


def swap_core(value, shards):
    return hop(value, shards, lambda g, f: (g, f ^ 1))


def after(value, *others):
    return lax.optimization_barrier((value, *others))[0]


def chain_of(block, shards):
    return jnp.stack([block] + [along(block, shards, by) for by in range(1, shards // 2)])


def near_of(chain, shards):
    return jnp.concatenate([chain, swap_first(chain, shards)])


def assemble_kernel(shard, depth, by_rows, has_tail, me_ref, *refs):
    sources, (out_ref, *tail), sems = refs[:4], refs[4:-1], refs[-1]
    g0, z0, c0 = me_ref[0], me_ref[1], me_ref[2]
    copies = []

    def copy(source, target):
        made = pltpu.make_async_copy(source, target, sems.at[len(copies)])
        made.start()
        copies.append(made)

    for k, source in enumerate(sources):
        core = c0 if k < 2 else 1 - c0
        for t in range(2):
            part = g0 ^ (t * (1 + core)) ^ ((k % 2) * (2 - core))
            for s in range(depth):
                place = lax.rem(z0 + depth - s, depth) * 2 + core
                at = t * depth + s
                block = source.at[at, pl.ds(0, shard), :]
                if by_rows:
                    copy(block, out_ref.at[pl.ds(pl.multiple_of((place * 4 + part) * shard, shard), shard), :])
                else:
                    copy(block, out_ref.at[part, pl.ds(pl.multiple_of(place * shard, shard), shard), :])
                if has_tail and k % 2 == 0 and t == 0:
                    copy(source.at[at, pl.ds(shard, TAIL_ROWS), :], tail[0].at[place])
    for made in copies:
        made.wait()


def assemble(me, arrays, shard, shards, by_rows):
    width = arrays[0].shape[2]
    has_tail = arrays[0].shape[1] > shard
    out = [shape_of((4 * shards * shard, width) if by_rows else (4, shards * shard, width), BF16)]
    if has_tail:
        out.append(shape_of((shards, TAIL_ROWS, width), BF16))
    anywhere = pl.BlockSpec(memory_space=pl.ANY)
    return pl.pallas_call(
        partial(assemble_kernel, shard, shards // 2, by_rows, has_tail),
        out_shape=out,
        grid_spec=pltpu.PrefetchScalarGridSpec(
            num_scalar_prefetch=1,
            grid=(1,),
            in_specs=[anywhere] * 4,
            out_specs=[full_spec(made.shape) for made in out],
            scratch_shapes=[pltpu.SemaphoreType.DMA((4 * shards + shards,))],
        ),
        name="assemble",
    )(me, *arrays)


def slots_of(me_ref, part, place_z, core, depth):
    apart = part ^ me_ref[0]
    first = (apart >> core) & 1
    second = (apart >> (1 - core)) & 1
    return (first * 2 + second) * depth + lax.rem(place_z + depth - me_ref[1], depth)


def weight_grad_kernel(shard, depth, kind, has_tail, me_ref, *refs):
    count = {"rows": 2, "columns": 2, "attend": 4}[kind]
    inputs = refs[:count]
    tail_ref = refs[count] if has_tail else None
    keep_ref, send_ref, left_ref, stage_ref, sems = refs[-5:]
    step = pl.program_id(0)
    c0 = me_ref[2]
    width = stage_ref.shape[2]
    pieces = width // shard

    def each(j, act):
        for k in range(pieces):
            if kind == "rows":
                place_z, core, part = j, k // 4, k % 4
            else:
                place_z, core, part = k // 2, k % 2, j
            slot = slots_of(me_ref, part, place_z, core, depth)

            def both(target):
                act(
                    pltpu.make_async_copy(
                        stage_ref.at[j, pl.ds(k * shard, shard), :], target.at[slot, pl.ds(0, shard), :], sems.at[j, k]
                    )
                )
                if has_tail:
                    act(
                        pltpu.make_async_copy(
                            tail_ref.at[j, k], target.at[slot, pl.ds(shard, TAIL_ROWS), :], sems.at[j, pieces + k]
                        )
                    )

            @pl.when(c0 == core)
            def _():
                both(keep_ref)

            @pl.when(c0 != core)
            def _():
                both(send_ref)

    def flip(source):
        left_ref[...] = source[...].T

    if kind == "rows":
        flip(inputs[0])
        right = inputs[1]
    elif kind == "columns":
        pl.when(step == 0)(lambda: flip(inputs[0]))
        right = inputs[1]
    else:
        pl.when(step == 0)(lambda: flip(inputs[0]))
        pl.when(step == 3)(lambda: flip(inputs[1]))
        right = None

    def multiply(right):
        rows = min(256, width)
        for at in range(0, width, rows):
            stage_ref[step, at : at + rows, :] = nn(left_ref[at : at + rows, :], right).astype(BF16)

    if kind == "attend":
        pl.when(step < 3)(lambda: multiply(inputs[2][0]))
        pl.when(step == 3)(lambda: multiply(inputs[3][...]))
    else:
        multiply(right[...])
    each(step, lambda made: made.start())

    @pl.when(step == pl.num_programs(0) - 1)
    def _():
        for j in range(4):
            each(j, lambda made: made.wait())


def weight_grad(me, kind, inputs, tail, shard, shards):
    rows, width = inputs[0].shape[0], min(inputs[0].shape[-1], inputs[-1].shape[-1])
    whole = full_spec((rows, width))
    block = pl.BlockSpec((rows, width), lambda j, _: (0, j))
    specs = {
        "rows": [block, whole],
        "columns": [whole, block],
        "attend": [whole, whole, pl.BlockSpec((1, rows, width), lambda j, _: (jnp.minimum(j, 2), 0, 0)), whole],
    }[kind]
    anywhere = pl.BlockSpec(memory_space=pl.ANY)
    has_tail = tail is not None
    pieces = width // shard
    height = shard + (TAIL_ROWS if has_tail else 0)
    return pl.pallas_call(
        partial(weight_grad_kernel, shard, shards // 2, kind, has_tail),
        out_shape=(shape_of((2 * shards, height, width), BF16),) * 2,
        grid_spec=pltpu.PrefetchScalarGridSpec(
            num_scalar_prefetch=1,
            grid=(4,),
            in_specs=specs + [full_spec(tail.shape)] * has_tail if has_tail else specs,
            out_specs=[anywhere] * 2,
            scratch_shapes=[
                pltpu.VMEM((width, rows), BF16),
                pltpu.VMEM((4, width, width), BF16),
                pltpu.SemaphoreType.DMA((4, 2 * pieces)),
            ],
        ),
        cost_estimate=cost(8 * rows * width * width, *inputs),
        name="weight_grad_" + kind,
    )(me, *inputs, *([tail] if has_tail else []))


def add(*parts):
    return sum(part.astype(F32) for part in parts).astype(BF16)


def halves(keep, got):
    middle = keep.shape[0] // 2
    return add(keep[:middle], got[:middle]), add(keep[middle:], got[middle:])


def sum_chain(kept, got, shards):
    total = [add(kept[s], got[s]) for s in range(kept.shape[0])]
    return total[0], [along(total[s], shards, s) for s in range(1, kept.shape[0])]


def place_kernel(shard, factor, kind, me_ref, in_ref, *outs):
    step = pl.program_id(0)
    value = in_ref[0, 0:shard, :].astype(F32) * factor
    if kind == "attend":
        pl.when(step < 3)(lambda: outs[0].__setitem__(..., value))
        pl.when(step == 3)(lambda: outs[1].__setitem__(..., value))
    else:
        outs[0][...] = value


def place_blocks(me, blocks, kind, shard, factor):
    _, height, width = blocks.shape

    def source(j, me_ref):
        apart = j ^ me_ref[0]
        first = (apart >> me_ref[2]) & 1
        second = (apart >> (1 - me_ref[2])) & 1
        return (first * 2 + second, 0, 0)

    out_shape, out_specs = {
        "rows": ([(4 * shard, width)], [pl.BlockSpec((shard, width), lambda j, _: (j, 0))]),
        "columns": ([(shard, 4 * width)], [pl.BlockSpec((shard, width), lambda j, _: (0, j))]),
        "attend": (
            [(shard, 3 * width), (shard, width)],
            [
                pl.BlockSpec((shard, width), lambda j, _: (0, jnp.minimum(j, 2))),
                pl.BlockSpec((shard, width), lambda j, _: (0, 0)),
            ],
        ),
    }[kind]
    return pl.pallas_call(
        partial(place_kernel, shard, factor, kind),
        out_shape=[shape_of(dims, F32) for dims in out_shape],
        grid_spec=pltpu.PrefetchScalarGridSpec(
            num_scalar_prefetch=1,
            grid=(4,),
            in_specs=[pl.BlockSpec((1, height, width), source)],
            out_specs=out_specs,
        ),
        name="place_" + kind,
    )(me, blocks)


def pack_rows(vectors, shards, width):
    packed = jnp.concatenate([v.reshape(shards, -1) for v in vectors], axis=1)
    packed = packed.reshape(shards, 4, -1).transpose(1, 0, 2).astype(BF16)
    return jnp.pad(packed[:, :, None, :], ((0, 0), (0, 0), (0, TAIL_ROWS - 1), (0, width - packed.shape[2])))


def unpack_rows(me, blocks, shard, sizes, factor):
    total = sum(sizes) * shard
    rows = blocks[:, shard, : total // 4].astype(F32) * factor
    ordered = []
    for j in range(4):
        apart = j ^ me[0]
        at = ((apart >> me[2]) & 1) * 2 + ((apart >> (1 - me[2])) & 1)
        ordered.append(lax.dynamic_index_in_dim(rows, at, 0, keepdims=False))
    flat = jnp.concatenate(ordered)
    out = []
    at = 0
    for size in sizes:
        out.append(flat[at * shard : (at + size) * shard])
        at += size
    return out


def vector_rows(*vectors):
    return jnp.stack([v.astype(F32) for v in vectors] + [jnp.zeros_like(vectors[0], F32)] * (8 - len(vectors)))


def split_small(small_full, shard, sizes):
    parts = []
    at = 0
    for size in sizes:
        parts.append(small_full[:, at * shard : (at + size) * shard].reshape(-1).astype(F32))
        at += size
    return parts


SMALL_ATTEND = (2, 1, 1, 1)
SMALL_FEED = (4, 1, 1, 1)


def per_device(
    tokens,
    segments,
    project_weight,
    project_bias,
    combine_weight,
    combine_bias,
    first_gain,
    first_shift,
    expand_weight,
    expand_bias,
    reduce_weight,
    reduce_bias,
    second_gain,
    second_shift,
    layer_cotangent,
    pooled_cotangent,
):
    row_count, length, width = tokens.shape
    shard = combine_weight.shape[0]
    shards = lax.axis_size("fsdp")
    flat = tokens.reshape(length, width)
    seg = segments.reshape(length)
    seg_row = segments
    seg_column = seg.reshape(length, 1)
    block = 256
    limits = key_limits(seg, block)
    replica, member = lax.axis_index("grp"), lax.axis_index("fsdp")
    me = jnp.stack([replica, member // 2, member % 2]).astype(jnp.int32)
    fast = lax.axis_size("grp") == 4 and shards % 2 == 0 and shard % 32 == 0 and width == shard * 8
    small = jnp.concatenate(
        [project_bias, combine_bias, first_gain, first_shift, expand_bias, reduce_bias, second_gain, second_shift]
    )

    if fast:
        lead = jnp.where(
            replica < 3,
            lax.dynamic_slice(project_weight, (0, jnp.minimum(replica, 2) * width), (shard, width)),
            combine_weight,
        )
        rows = jnp.pad(small, (0, TAIL_ROWS * width - small.shape[0])).reshape(TAIL_ROWS, width)
        lead = jnp.concatenate([lead, rows])
        chain_a = chain_of(lead, shards)
        part = after(lax.dynamic_slice(expand_weight, (0, replica * width), (shard, width)), chain_a)
        chain_e = chain_of(part, shards)
        near_a = near_of(chain_a, shards)
        far_a = swap_second(near_a, shards)
        arrays = (near_a, far_a, swap_core(near_a, shards), swap_core(far_a, shards))
        attend_full, small_full = assemble(me, arrays, shard, shards, False)
        small_full = small_full.reshape(shards, -1)
        near_e = near_of(after(chain_e, far_a), shards)
    else:
        attend_shard = jnp.concatenate(
            [project_weight.reshape(shard, 3, width).transpose(1, 0, 2), combine_weight[None]], axis=0
        )
        expand_shard = expand_weight.reshape(shard, 4, width).transpose(1, 0, 2)
        attend_full = lax.all_gather(attend_shard, "fsdp", axis=1, tiled=True)
        small_full = lax.all_gather(small, "fsdp", axis=0, tiled=False)
        expand_full = lax.all_gather(expand_shard, "fsdp", axis=1, tiled=True)
        reduce_full = lax.all_gather(reduce_weight, "fsdp", axis=0, tiled=True)
    bias_pair, bias_combine, gain_one, shift_one, bias_expand, bias_reduce, gain_two, shift_two = split_small(
        small_full, shard, SMALL_ATTEND + SMALL_FEED
    )
    bias_all = jnp.stack([bias_pair[:width], jnp.zeros((width,), F32), bias_pair[width:]]).reshape(3, 1, width)

    qkv = project(flat, attend_full, bias_all)
    if fast:
        qkv = after(qkv, near_e)
        far_e = swap_second(near_e, shards)
        part = lax.dynamic_slice(reduce_weight, (replica * shard, 0), (shard, width))
        chain_r = chain_of(after(part, near_e), shards)
    context, lse = attend_forward(qkv, limits, seg_column, seg_row, block)
    vec_one = vector_rows(bias_combine, gain_one, shift_one)
    vec_two = vector_rows(bias_reduce, gain_two, shift_two)
    if fast:
        context = after(context, far_e, chain_r)
        arrays = (near_e, far_e, swap_core(near_e, shards), swap_core(far_e, shards))
        near_r = near_of(chain_r, shards)
    hidden, hidden_low, normed, inverse = combine(context, attend_full, flat, vec_one, 256)
    if fast:
        hidden_low, *arrays = lax.optimization_barrier((hidden_low, *arrays, near_r))[:-1]
        expand_full = assemble(me, arrays, shard, shards, False)[0]
        far_r = swap_second(near_r, shards)
    act, slope = expand(hidden_low, expand_full, bias_expand.reshape(4, 1, width))
    if fast:
        act, far_r = lax.optimization_barrier((act, far_r))
        arrays = (near_r, far_r, swap_core(near_r, shards), swap_core(far_r, shards))
        reduce_full = assemble(me, arrays, shard, shards, True)[0]
    result_low, pooled, grad_second, grad_branch, sums_two = reduce(
        act,
        reduce_full,
        hidden,
        vec_two,
        layer_cotangent.reshape(length, width),
        pooled_cotangent.reshape(SEG, width),
        seg_column,
        seg_row,
        256,
    )
    factor = float(length * lax.axis_size("grp") * shards) ** (-0.5)
    if fast:
        keep_r, send_r = weight_grad(me, "rows", (act, grad_branch), None, shard, shards)
        got = swap_core(send_r, shards)
        grad_branch = after(grad_branch, send_r)
    grad_pre, sums_pre = grad_pre_of(grad_branch, reduce_full, slope)
    feed_vectors = [sums_pre[0], sums_two[2], sums_two[0], sums_two[1]]
    if fast:
        grad_pre, got = lax.optimization_barrier((grad_pre, got))
        keep_r, send_r = halves(keep_r, got)
        got_r = swap_first(send_r, shards)
        rows = pack_rows(feed_vectors, shards, width)
        keep_e, send_e = weight_grad(me, "columns", (hidden_low, after(grad_pre, send_r)), rows, shard, shards)
        send_e, got_r = lax.optimization_barrier((send_e, got_r))
        got_e = swap_core(send_e, shards)
        keep_r, send_r = halves(keep_r, got_r)
        got_r = swap_second(send_r, shards)
        grad_pre = after(grad_pre, send_e, send_r)
    grad_first, grad_attn, grad_context, sums_one = grad_hidden_of(
        grad_pre, expand_full, grad_second, normed, inverse, vec_one, attend_full, 256
    )
    if fast:
        pieces = 2
        grad_context, got_e, got_r = lax.optimization_barrier((grad_context, got_e, got_r))
        own_r, parts_r = sum_chain(keep_r, got_r, shards)
        keep_e, send_e = halves(keep_e, got_e)
        got_e = swap_first(send_e, shards)
        grad_qkv = attend_backward(
            qkv, after(grad_context, own_r, send_e), lse, limits, seg_column, seg_row, block, 0, pieces
        )
        first_qkv, got_e, *parts_r = lax.optimization_barrier((grad_qkv[0], got_e, *parts_r))
        own_r = add(own_r, *parts_r)
        pair_r = jnp.stack([own_r, swap_second(own_r, shards)])
        keep_e, send_e = halves(keep_e, got_e)
        got_e = swap_second(send_e, shards)
        grad_qkv = attend_backward(
            qkv,
            after(grad_context, send_e, own_r),
            lse,
            limits,
            seg_column,
            seg_row,
            block,
            pieces,
            pieces,
            (first_qkv, grad_qkv[1]),
        )
        first_qkv, got_e, pair_r = lax.optimization_barrier((grad_qkv[0], got_e, pair_r))
        reduce_blocks = jnp.concatenate([pair_r, swap_first(pair_r, shards)])
        own_e, parts_e = sum_chain(keep_e, got_e, shards)
        grad_qkv, sums_qkv = attend_backward(
            qkv,
            after(grad_context, own_e),
            lse,
            limits,
            seg_column,
            seg_row,
            block,
            2 * pieces,
            width // LANES - 2 * pieces,
            (first_qkv, grad_qkv[1]),
        )
        grad_qkv, *parts_e = lax.optimization_barrier((grad_qkv, *parts_e))
        own_e = add(own_e, *parts_e)
        pair_e = jnp.stack([own_e, swap_second(own_e, shards)])
    else:
        grad_qkv, sums_qkv = attend_backward(
            qkv, grad_context, lse, limits, seg_column, seg_row, block, 0, width // LANES
        )
    attend_vectors = [jnp.concatenate([sums_qkv[0], sums_qkv[2]]), sums_one[2], sums_one[0], sums_one[1]]
    if fast:
        rows = pack_rows(attend_vectors, shards, width)
        keep_a, send_a = weight_grad(
            me, "attend", (flat, context, after(grad_qkv, own_e), grad_attn), rows, shard, shards
        )
        send_a, pair_e = lax.optimization_barrier((send_a, pair_e))
        expand_blocks = jnp.concatenate([pair_e, swap_first(pair_e, shards)])
        got_a = swap_core(send_a, shards)
        keep_a, send_a = halves(keep_a, got_a)
        got_a = swap_first(send_a, shards)
        token_grad = token_grad_of(after(grad_qkv, send_a), attend_full, grad_first, 256)
        token_grad, got_a = lax.optimization_barrier((token_grad, got_a))
        keep_a, send_a = halves(keep_a, got_a)
        own_a, parts_a = sum_chain(keep_a, swap_second(send_a, shards), shards)
        own_a = add(own_a, *parts_a)
        pair_a = jnp.stack([own_a, swap_second(own_a, shards)])
        attend_blocks = jnp.concatenate([pair_a, swap_first(pair_a, shards)])
    else:
        token_grad = token_grad_of(grad_qkv, attend_full, grad_first, 256)

    if fast:
        reduce_grad = place_blocks(me, reduce_blocks, "rows", shard, factor)[0]
        expand_grad = place_blocks(me, expand_blocks, "columns", shard, factor)[0]
        project_grad, combine_grad = place_blocks(me, attend_blocks, "attend", shard, factor)
        small_grads = unpack_rows(me, attend_blocks, shard, SMALL_ATTEND, factor)
        small_grads += unpack_rows(me, expand_blocks, shard, SMALL_FEED, factor)
    else:

        def finish(term, axis):
            part = lax.psum_scatter(term.astype(BF16), "fsdp", scatter_dimension=axis, tiled=True)
            return lax.psum(part, "grp").astype(F32) * factor

        reduce_grad = finish(tn(act, grad_branch), 0)
        grad = jnp.stack([tn(hidden_low, grad_pre[:, t * width : (t + 1) * width]) for t in range(4)])
        expand_grad = finish(grad, 1).transpose(1, 0, 2).reshape(shard, 4 * width)
        grad = finish(jnp.stack([tn(flat, grad_qkv[t]) for t in range(3)] + [tn(context, grad_attn)]), 1)
        project_grad, combine_grad = grad[:3].transpose(1, 0, 2).reshape(shard, 3 * width), grad[3]
        packed = jnp.concatenate([v.reshape(shards, -1) for v in attend_vectors + feed_vectors], axis=1).reshape(-1)
        packed = lax.psum(lax.psum_scatter(packed, "fsdp", scatter_dimension=0, tiled=True), "grp") * factor
        small_grads = split_small(packed[None], shard, SMALL_ATTEND + SMALL_FEED)
    return (
        result_low.reshape(row_count, length, width),
        pooled.reshape(row_count, SEG, width),
        token_grad.reshape(row_count, length, width),
        project_grad,
        small_grads[0],
        combine_grad,
        small_grads[1],
        small_grads[2],
        small_grads[3],
        expand_grad,
        small_grads[4],
        reduce_grad,
        small_grads[5],
        small_grads[6],
        small_grads[7],
    )


def solution(mesh):
    in_specs = (
        P(("grp", "fsdp"), None, None),
        P(("grp", "fsdp"), None),
        P("fsdp", None),
        P("fsdp"),
        P("fsdp", None),
        P("fsdp"),
        P("fsdp"),
        P("fsdp"),
        P("fsdp", None),
        P("fsdp"),
        P("fsdp", None),
        P("fsdp"),
        P("fsdp"),
        P("fsdp"),
        P(("grp", "fsdp"), None, None),
        P(("grp", "fsdp"), None, None),
    )
    out_specs = (
        P(("grp", "fsdp"), None, None),
        P(("grp", "fsdp"), None, None),
        P(("grp", "fsdp"), None, None),
        P("fsdp", None),
        P("fsdp"),
        P("fsdp", None),
        P("fsdp"),
        P("fsdp"),
        P("fsdp"),
        P("fsdp", None),
        P("fsdp"),
        P("fsdp", None),
        P("fsdp"),
        P("fsdp"),
        P("fsdp"),
    )
    return jax.shard_map(
        per_device, mesh=mesh, in_specs=in_specs, out_specs=out_specs, check_vma=False
    )
```

time: 860 us -> 417 us (0.48)
  matrix products: 284 us -> 0 us
  waiting for transfers between devices: 328 us -> 70.1 us
  Pallas kernels: 0 us -> 226 us
  blocking collectives: 81.6 us -> 0 us
  other arithmetic: 92.9 us -> 27 us
  starting transfers between devices: 0.36 us -> 58.3 us
  local copies, waits for them, and re-layouts: 46.9 us -> 28.5 us
  between operations: 18.3 us -> 1.56 us
    dot_general x26 -> x0, matrix products: 284 us -> none  [the longest x2 40.7 us: attend_backward(): jnp.einsum('qhd,khd->hqk', context_block, values_row, preferred_element_t...]
    reduce_scatter x3 -> x0, waiting for transfers between devices: 236 us -> none  [the longest x1 101 us: per_device(): lax.psum_scatter(expand_term, 'fsdp', scatter_dimension=0, tiled=True)]
    pallas_call x0 -> x20, Pallas kernels: none -> 226 us  [the longest x3 45.4 us: attend_backward(): pl.pallas_call(kernel, out_shape=made, grid_spec=pltpu.PrefetchScalarGrid...]
    ppermute x0 -> x45, waiting for transfers between devices: none -> 70.1 us  [hop(): return lax.ppermute(value, AXES, pairs)]
    unnamed x2 -> x0, blocking collectives: 58.7 us -> none
    ppermute x0 -> x45, starting transfers between devices: none -> 58.3 us  [hop(): return lax.ppermute(value, AXES, pairs)]
    unnamed x10 -> x0, waiting for transfers between devices: 50.1 us -> none
    psum x1 -> x0, waiting for transfers between devices: 41.6 us -> none  [per_device(): lax.psum((att_project, att_pbias, att_combine, att_cbias, att_gain, att_s...]
  transfers between devices with their start and end apart: 9 -> 45, of which waited for: 5 -> 18; matrix products, arithmetic and copies ran while one was open for 23% -> 6% of each run, Pallas kernels for 0% -> 46%
where the time goes in v1:
time: 417 us; the launch traced here: 411 us
  Pallas kernels  226 us (54%)
  waiting for transfers between devices  70.1 us (17%)
  starting transfers between devices  58.3 us (14%)
  local copies, waits for them, and re-layouts  28.5 us (7%)
  other arithmetic  27 us (6%)
    ppermute x45, waiting for transfers between devices, hop(): return lax.ppermute(value, AXES, pairs)  70.1 us
    ppermute x45, starting transfers between devices, hop(): return lax.ppermute(value, AXES, pairs)  58.3 us
    pallas_call x3, Pallas kernels, attend_backward(): pl.pallas_call(kernel, out_shape=made, grid_spec=pltpu.PrefetchScalarGrid...  45.4 us
    pallas_call x3, Pallas kernels, weight_grad(): pl.pallas_call(partial(weight_grad_kernel, shard, shards // 2, kind, has_...  34.2 us
    pallas_call x1, Pallas kernels, attend_forward(): pl.pallas_call(partial(attend_forward_kernel, window_sizes(block, length)...  28.1 us
    pallas_call x1, Pallas kernels, expand(): pl.pallas_call(expand_kernel, out_shape=(shape_of((rows, count * width),...  20 us
    convert_element_type x12, other arithmetic, add(): return sum((part.astype(F32) for part in parts)).astype(BF16)  18.5 us
    pallas_call x3, Pallas kernels, assemble(): pl.pallas_call(partial(assemble_kernel, shard, shards // 2, by_rows, has_...  17 us
  transfers between devices with their start and end apart: 45, of which 18 were waited for; matrix products, arithmetic and copies ran while one was open for 6% of the time, Pallas kernels for 46%

profile of v1, /device:TPU:0, one launch (start us, length us, event | category | flops | bytes accessed | tf_op | source)
XLA Modules:
  0.0 411.3 jit_solution(9435701155426529737)
XLA Ops:
  0.7 5.5 %concatenate.61 = bf16[1152]{0:T(1024)(128)(2,1)S(1)} concatenate(bf16[192]{0:T(256)(128)(2,1)} %param.19, bf16[96]{0:T(256)(128)(2,1)} %param.21, bf16[96]{0:T(256)(128)(2,1)} %param.22, bf16[96]{0:T(256)(128)(2,1)} %param.23, bf16[384]{0:T(512)(128)(2,1)} %param.25, bf16[96]{0:T(256)(128)(2,1)} %param.27, bf16[96]{0:T(256)(128)(2,1)} %param.28, bf16[96]{0:T(256)(128)(2,1)} %param.29), dimensions={0} | concatenate | bytes 4608 | tf_op jit(solution)/shard_map/concatenate | solution.py:893
  7.2 3.1 collective-permute-start
  10.3 2.6 collective-permute-start.1
  14.3 3.1 collective-permute-done
  17.4 6.0 %collective-permute-done.1 = bf16[104,768]{1,0:T(8,128)(2,1)S(1)} collective-permute-done((bf16[104,768]{1,0:T(8,128)(2,1)S(1)}, bf16[104,768]{1,0:T(8,128)(2,1)S(1)}, u32[]{:S(2)}, u32[]{:S(2)}) %collective-permute-start.1) | collective-permute-done | bytes 159776 | tf_op jit(solution)/shard_map/ppermute | solution.py:576
  23.5 1.6 collective-permute-start.3
  25.1 8.9 %collective-permute-done.3 = bf16[4,104,768]{2,1,0:T(8,128)(2,1)S(1)} collective-permute-done((bf16[4,104,768]{2,1,0:T(8,128)(2,1)S(1)}, bf16[4,104,768]{2,1,0:T(8,128)(2,1)S(1)}, u32[]{:S(2)}, u32[]{:S(2)}) %collective-permute-start.3) | collective-permute-done | bytes 639008 | tf_op jit(solution)/shard_map/ppermute | solution.py:576
  34.0 1.6 collective-permute-start.4
  36.9 3.9 collective-permute-start.7
  40.8 1.6 collective-permute-start.8
  43.7 3.0 collective-permute-done.7
  46.6 4.1 collective-permute-done.8
  56.7 4.7 %collective-permute-done.10 = bf16[4,96,768]{2,1,0:T(8,128)(2,1)} collective-permute-done((bf16[4,96,768]{2,1,0:T(8,128)(2,1)S(1)}, bf16[4,96,768]{2,1,0:T(8,128)(2,1)}, u32[]{:S(2)}, u32[]{:S(2)}) %collective-permute-start.10) | collective-permute-done | bytes 589856 | tf_op jit(solution)/shard_map/ppermute | solution.py:576
  62.6 3.9 collective-permute-start.12
  66.5 1.6 collective-permute-start.13
  69.0 3.4 collective-permute-done.12
  72.4 1.5 collective-permute-start.11
  73.9 2.5 collective-permute-done.13
  80.9 5.7 %assemble.3 = (bf16[4,768,768]{2,1,0:T(8,128)(2,1)}, bf16[8,8,768]{2,1,0:T(8,128)(2,1)}) custom-call(s32[3]{0:T(128)} %pad_add_fusion.1.me_ref, bf16[8,104,768]{2,1,0:T(8,128)(2,1)} %copy-done.5, bf16[8,104,768]{2,1,0:T(8,128)(2,1)} %collective-permute-done.4.refs_1_, bf16[8,104,768]{2,1,0:T(8,128)(2,1)} %copy-done.10, ...), custom_call_target="tpu_custom_call" | custom-call | tf_op jit(solution)/shard_map/assemble/pallas_call | solution.py:642
  88.4 9.5 %project.1.q_ref.k_ref.v_ref.refs_0_.refs_1_.refs_2_ = bf16[3,1024,768]{2,1,0:T(8,128)(2,1)} custom-call(bf16[1024,768]{1,0:T(8,128)(2,1)} %bitcast.163, bf16[4,768,768]{2,1,0:T(8,128)(2,1)} %get-tuple-element.93.w_ref.wc_ref, f32[3,1,768]{2,1,0:T(1,128)} %copy.52.b_ref), custom_call_target="tpu_custom_call" | custom-call | flops 3623878656 | bytes 6291456 | tf_op jit(solution)/shard_map/project/pallas_call | solution.py:78
  98.3 28.1 %attend_forward.1 = (bf16[1024,768]{1,0:T(8,128)(2,1)}, f32[6,8,1024]{2,1,0:T(8,128)}) custom-call(s32[2,4]{1,0:T(2,128)} %pad_add_fusion.limits_ref, bf16[3,1024,768]{2,1,0:T(8,128)(2,1)} %project.1.q_ref.k_ref.v_ref.refs_0_.refs_1_.refs_2_, bf16[3,1024,768]{2,1,0:T(8,128)(2,1)} %project.1.q_ref.k_ref.v_ref.refs_0_.refs_1_.refs_2_, ...), custom_call_target="tpu_custom_call" | custom-call | flops 6442450944 | bytes 4718592 | tf_op jit(solution)/shard_map/attend_forward/pallas_call | solution.py:153
  129.3 7.2 %combine.1 = (f32[1024,768]{1,0:T(8,128)}, bf16[1024,768]{1,0:T(8,128)(2,1)}, f32[1024,768]{1,0:T(8,128)}, f32[1024,1]{1,0:T(8,128)}) custom-call(bf16[1024,768]{1,0:T(8,128)(2,1)} %get-tuple-element.100.c_ref.refs_1_, bf16[4,768,768]{2,1,0:T(8,128)(2,1)} %get-tuple-element.93.w_ref.wc_ref, bf16[1024,768]{1,0:T(8,128)(2,1)} %bitcast.164, ...), custom_call_target="tpu_custom_call" | custom-call | flops 2415919104 | bytes 3145728 | tf_op jit(solution)/shard_map/combine/pallas_call | solution.py:309
  136.5 5.7 %assemble.4.w_ref.we_ref = bf16[4,768,768]{2,1,0:T(8,128)(2,1)} custom-call(s32[3]{0:T(128)} %pad_add_fusion.1.me_ref, bf16[8,96,768]{2,1,0:T(8,128)(2,1)} %copy-done.2, bf16[8,96,768]{2,1,0:T(8,128)(2,1)} %collective-permute-done.11.refs_1_, bf16[8,96,768]{2,1,0:T(8,128)(2,1)} %collective-permute-done.15.refs_2_, ...), custom_call_target="tpu_custom_call" | custom-call | tf_op jit(solution)/shard_map/assemble/pallas_call | solution.py:642
  142.2 20.0 %expand.1 = (bf16[1024,3072]{1,0:T(8,128)(2,1)}, bf16[1024,3072]{1,0:T(8,128)(2,1)}) custom-call(bf16[1024,768]{1,0:T(8,128)(2,1)} %get-tuple-element.102.x_ref.refs_0_, bf16[4,768,768]{2,1,0:T(8,128)(2,1)} %assemble.4.w_ref.we_ref, f32[4,1,768]{2,1,0:T(1,128)} %reshape.355.b_ref), custom_call_target="tpu_custom_call" | custom-call | flops 9663676416 | bytes 6291456 | tf_op jit(solution)/shard_map/expand/pallas_call | solution.py:345
  163.5 1.8 collective-permute-done.20.refs_3_
  166.4 5.7 %assemble.5.w_ref = bf16[3072,768]{1,0:T(8,128)(2,1)} custom-call(s32[3]{0:T(128)} %pad_add_fusion.1.me_ref, bf16[8,96,768]{2,1,0:T(8,128)(2,1)} %copy-done.8, bf16[8,96,768]{2,1,0:T(8,128)(2,1)} %collective-permute-done.18.refs_1_, bf16[8,96,768]{2,1,0:T(8,128)(2,1)} %collective-permute-done.19.refs_2_, bf16[8,96,768]{2,1,0:T(8,128)(2,1)} %copy-done.12), custom_call_target="tpu_custom_call" | custom-call | tf_op jit(solution)/shard_map/assemble/pallas_call | solution.py:642
  172.0 15.6 %reduce.23 = (bf16[1024,768]{1,0:T(8,128)(2,1)}, f32[8,768]{1,0:T(8,128)}, f32[1024,768]{1,0:T(8,128)}, bf16[1024,768]{1,0:T(8,128)(2,1)}, f32[8,768]{1,0:T(8,128)}) custom-call(bf16[1024,3072]{1,0:T(8,128)(2,1)} %get-tuple-element.108.act_ref.refs_0_, bf16[3072,768]{1,0:T(8,128)(2,1)} %assemble.5.w_ref, f32[1024,768]{1,0:T(8,128)} %get-tuple-element.110.hidden_ref, ...), custom_call_target="tpu_custom_call" | custom-call | flops 7247757312 | bytes 11010048 | tf_op jit(solution)/shard_map/reduce/pallas_call | solution.py:424
  187.6 10.7 %weight_grad_rows.1 = (bf16[16,96,768]{2,1,0:T(8,128)(2,1)}, bf16[16,96,768]{2,1,0:T(8,128)(2,1)}) custom-call(s32[3]{0:T(128)} %pad_add_fusion.1.me_ref, bf16[1024,3072]{1,0:T(8,128)(2,1)} %get-tuple-element.108.act_ref.refs_0_, bf16[1024,768]{1,0:T(8,128)(2,1)} %get-tuple-element.115.refs_1_.g_ref), custom_call_target="tpu_custom_call" | custom-call | flops 4831838208 | bytes 7864320 | tf_op jit(solution)/shard_map/weight_grad_rows/pallas_call | solution.py:747
  198.7 13.1 %grad_pre.1 = (bf16[1024,3072]{1,0:T(8,128)(2,1)}, f32[8,3072]{1,0:T(8,128)}) custom-call(bf16[1024,768]{1,0:T(8,128)(2,1)} %get-tuple-element.115.refs_1_.g_ref, bf16[3072,768]{1,0:T(8,128)(2,1)} %assemble.5.w_ref, bf16[1024,3072]{1,0:T(8,128)(2,1)} %get-tuple-element.116.slope_ref), custom_call_target="tpu_custom_call" | custom-call | flops 7247757312 | bytes 6291456 | tf_op jit(solution)/shard_map/grad_pre/pallas_call | solution.py:474
  213.3 4.1 add_convert_fusion.4
  220.5 11.0 %weight_grad_columns.1 = (bf16[16,104,768]{2,1,0:T(8,128)(2,1)}, bf16[16,104,768]{2,1,0:T(8,128)(2,1)}) custom-call(s32[3]{0:T(128)} %pad_add_fusion.1.me_ref, bf16[1024,768]{1,0:T(8,128)(2,1)} %get-tuple-element.102.x_ref.refs_0_, bf16[1024,3072]{1,0:T(8,128)(2,1)} %get-tuple-element.127.refs_1_.gp_ref, bf16[4,8,8,768]{3,2,1,0:T(8,128)(2,1)} %pad.13.refs_2_), custom_call_target="tpu_custom_call" | custom-call | flops 4831838208 | bytes 7864320 | tf_op jit(solution)/shard_map/weight_grad_columns/pallas_call | solution.py:747
  231.5 2.2 collective-permute-done.22
  234.0 1.9 collective-permute-start.24
  235.9 15.3 %grad_hidden.1 = (f32[1024,768]{1,0:T(8,128)}, bf16[1024,768]{1,0:T(8,128)(2,1)}, bf16[1024,768]{1,0:T(8,128)(2,1)}, f32[8,768]{1,0:T(8,128)}) custom-call(bf16[1024,3072]{1,0:T(8,128)(2,1)} %get-tuple-element.127.refs_1_.gp_ref, bf16[4,768,768]{2,1,0:T(8,128)(2,1)} %assemble.4.w_ref.we_ref, f32[1024,768]{1,0:T(8,128)} %get-tuple-element.128.second_ref, ...), custom_call_target="tpu_custom_call" | custom-call | flops 7247757312 | bytes 11010048 | tf_op jit(solution)/shard_map/grad_hidden/pallas_call | solution.py:517
  252.1 4.1 %add_convert_fusion.2 = (bf16[8,104,768]{2,1,0:T(8,128)(2,1)}, bf16[8,104,768]{2,1,0:T(8,128)(2,1)S(1)}) fusion(bf16[16,104,768]{2,1,0:T(8,128)(2,1)} %collective-permute-done.23, bf16[16,104,768]{2,1,0:T(8,128)(2,1)} %get-tuple-element.133), kind=kLoop, calls=%fused_computation.2 | loop fusion | flops 5111808 | bytes 7667712 | tf_op jit(solution)/shard_map/convert_element_type | solution.py:767
  257.0 2.0 fusion.14
  259.0 3.2 collective-permute-start.26
  262.4 2.1 collective-permute-start.28
  264.5 15.3 %attend_backward.3 = (bf16[3,1024,768]{2,1,0:T(8,128)(2,1)}, f32[8,768]{1,0:T(8,128)}) custom-call(s32[2,4]{1,0:T(2,128)} %pad_add_fusion.limits_ref, bf16[3,1024,768]{2,1,0:T(8,128)(2,1)} %project.1.q_ref.k_ref.v_ref.refs_0_.refs_1_.refs_2_, bf16[3,1024,768]{2,1,0:T(8,128)(2,1)} %project.1.q_ref.k_ref.v_ref.refs_0_.refs_1_.refs_2_, ...), custom_call_target="tpu_custom_call" | custom-call | flops 3221225472 | bytes 4718592 | tf_op jit(solution)/shard_map/attend_backward/pallas_call | solution.py:249
  280.9 1.6 add_convert_fusion.8
  282.7 2.1 collective-permute-start.30
  284.7 15.1 %attend_backward.4 = (bf16[3,1024,768]{2,1,0:T(8,128)(2,1)}, f32[8,768]{1,0:T(8,128)}) custom-call(s32[2,4]{1,0:T(2,128)} %pad_add_fusion.limits_ref, bf16[3,1024,768]{2,1,0:T(8,128)(2,1)} %project.1.q_ref.k_ref.v_ref.refs_0_.refs_1_.refs_2_, ...), custom_call_target="tpu_custom_call", output_to_operand_aliasing={{0}: (8, {}), {1}: (9, {})} | custom-call | flops 3221225472 | bytes 4718592 | tf_op jit(solution)/shard_map/attend_backward/pallas_call | solution.py:249
  300.9 3.0 collective-permute-start.33
  303.9 15.1 %attend_backward.5 = (bf16[3,1024,768]{2,1,0:T(8,128)(2,1)}, f32[8,768]{1,0:T(8,128)}) custom-call(s32[2,4]{1,0:T(2,128)} %pad_add_fusion.limits_ref, bf16[3,1024,768]{2,1,0:T(8,128)(2,1)} %project.1.q_ref.k_ref.v_ref.refs_0_.refs_1_.refs_2_, ...), custom_call_target="tpu_custom_call", output_to_operand_aliasing={{0}: (8, {}), {1}: (9, {})} | custom-call | flops 3221225472 | bytes 4718592 | tf_op jit(solution)/shard_map/attend_backward/pallas_call | solution.py:249
  321.1 12.5 %weight_grad_attend.1 = (bf16[16,104,768]{2,1,0:T(8,128)(2,1)}, bf16[16,104,768]{2,1,0:T(8,128)(2,1)}) custom-call(s32[3]{0:T(128)} %pad_add_fusion.1.me_ref, bf16[1024,768]{1,0:T(8,128)(2,1)} %bitcast.165, bf16[1024,768]{1,0:T(8,128)(2,1)} %get-tuple-element.100.c_ref.refs_1_, bf16[3,1024,768]{2,1,0:T(8,128)(2,1)} %get-tuple-element.163.refs_2_.g_ref, ...), custom_call_target="tpu_custom_call" | custom-call | flops 4831838208 | bytes 9437184 | tf_op jit(solution)/shard_map/weight_grad_attend/pallas_call | solution.py:747
  333.8 5.0 %collective-permute-done.35 = bf16[16,104,768]{2,1,0:T(8,128)(2,1)S(1)} collective-permute-done((bf16[16,104,768]{2,1,0:T(8,128)(2,1)}, bf16[16,104,768]{2,1,0:T(8,128)(2,1)S(1)}, u32[]{:S(2)}, u32[]{:S(2)}) %collective-permute-start.35) | collective-permute-done | bytes 2555936 | tf_op jit(solution)/shard_map/ppermute | solution.py:576
  338.8 3.4 add_convert_fusion
  342.3 1.9 collective-permute-start.36
  344.3 8.5 %token_grad.1 = bf16[1024,768]{1,0:T(8,128)(2,1)} custom-call(bf16[3,1024,768]{2,1,0:T(8,128)(2,1)} %get-tuple-element.163.refs_2_.g_ref, bf16[4,768,768]{2,1,0:T(8,128)(2,1)} %get-tuple-element.93.w_ref.wc_ref, f32[1024,768]{1,0:T(8,128)} %get-tuple-element.164.first_ref), custom_call_target="tpu_custom_call" | custom-call | flops 3623878656 | bytes 9437184 | tf_op jit(solution)/shard_map/token_grad/pallas_call | solution.py:551
  352.8 7.0 %collective-permute-done.36 = bf16[8,104,768]{2,1,0:T(8,128)(2,1)} collective-permute-done((bf16[8,104,768]{2,1,0:T(8,128)(2,1)}, bf16[8,104,768]{2,1,0:T(8,128)(2,1)}, u32[]{:S(2)}, u32[]{:S(2)}) %collective-permute-start.36) | collective-permute-done | bytes 1277984 | tf_op jit(solution)/shard_map/ppermute | solution.py:576
  359.8 2.4 add_convert_fusion.7
  362.2 2.0 collective-permute-start.37
  364.3 1.8 collective-permute-start.43
  366.0 1.8 pad_maximum_fusion.4.in_ref
  367.9 4.0 place_rows.1
  371.9 2.8 collective-permute-done.43
  378.0 2.8 collective-permute-start.40
  380.8 4.3 %collective-permute-done.38 = bf16[104,768]{1,0:T(8,128)(2,1)S(1)} collective-permute-done((bf16[104,768]{1,0:T(8,128)(2,1)S(1)}, bf16[104,768]{1,0:T(8,128)(2,1)S(1)}, u32[]{:S(2)}, u32[]{:S(2)}) %collective-permute-start.38) | collective-permute-done | bytes 159776 | tf_op jit(solution)/shard_map/ppermute | solution.py:576
  385.1 4.8 %collective-permute-done.39 = bf16[104,768]{1,0:T(8,128)(2,1)S(1)} collective-permute-done((bf16[104,768]{1,0:T(8,128)(2,1)S(1)}, bf16[104,768]{1,0:T(8,128)(2,1)S(1)}, u32[]{:S(2)}, u32[]{:S(2)}) %collective-permute-start.39) | collective-permute-done | bytes 159776 | tf_op jit(solution)/shard_map/ppermute | solution.py:576
  390.1 1.8 collective-permute-start.41
  391.9 4.0 place_columns.1
  396.6 1.6 collective-permute-start.42
  399.5 4.2 %collective-permute-done.42 = bf16[2,104,768]{2,1,0:T(8,128)(2,1)S(1)} collective-permute-done((bf16[2,104,768]{2,1,0:T(8,128)(2,1)S(1)}, bf16[2,104,768]{2,1,0:T(8,128)(2,1)S(1)}, u32[]{:S(2)}, u32[]{:S(2)}) %collective-permute-start.42) | collective-permute-done | bytes 319520 | tf_op jit(solution)/shard_map/ppermute | solution.py:576
  404.6 4.1 %place_attend.1 = (f32[96,2304]{1,0:T(8,128)}, f32[96,768]{1,0:T(8,128)}) custom-call(s32[3]{0:T(128)} %pad_add_fusion.1.me_ref, bf16[4,104,768]{2,1,0:T(8,128)(2,1)} %copy-done.3), custom_call_target="tpu_custom_call" | custom-call | tf_op jit(solution)/shard_map/place_attend/pallas_call | solution.py:810
  (191 shorter events, 45.4 us)
Async XLA Ops:
  0.6 36.2 %copy-start = (bf16[96,3072]{1,0:T(8,128)(2,1)S(1)}, bf16[96,3072]{1,0:T(8,128)(2,1)}, u32[]{:S(2)}) copy-start(bf16[96,3072]{1,0:T(8,128)(2,1)} %param.24) | copy-start | bytes 1769476
  7.2 10.2 %collective-permute-start = (bf16[104,768]{1,0:T(8,128)(2,1)S(1)}, bf16[104,768]{1,0:T(8,128)(2,1)S(1)}, u32[]{:S(2)}, u32[]{:S(2)}) collective-permute-start(bf16[104,768]{1,0:T(8,128)(2,1)S(1)} %get-tuple-element.205), channel_id=1, source_target_pairs={{0,2},{1,3},{2,4},{3,5},{4,6},{5,7},{6,0},{7,1},{8,10},{9,11},{10,... | collective-permute-start | bytes 479240 | tf_op jit(solution)/shard_map/ppermute | solution.py:576
  10.3 13.1 %collective-permute-start.1 = (bf16[104,768]{1,0:T(8,128)(2,1)S(1)}, bf16[104,768]{1,0:T(8,128)(2,1)S(1)}, u32[]{:S(2)}, u32[]{:S(2)}) collective-permute-start(bf16[104,768]{1,0:T(8,128)(2,1)S(1)} %get-tuple-element.205), channel_id=1, source_target_pairs={{0,4},{1,5},{2,6},{3,7},{4,0},{5,1},{6,2},{7,3},{8,12},{9,13},{10,... | collective-permute-start | bytes 479240 | tf_op jit(solution)/shard_map/ppermute | solution.py:576
  12.9 10.5 %collective-permute-start.2 = (bf16[104,768]{1,0:T(8,128)(2,1)S(1)}, bf16[104,768]{1,0:T(8,128)(2,1)S(1)}, u32[]{:S(2)}, u32[]{:S(2)}) collective-permute-start(bf16[104,768]{1,0:T(8,128)(2,1)S(1)} %get-tuple-element.205), channel_id=1, source_target_pairs={{0,6},{1,7},{2,0},{3,1},{4,2},{5,3},{6,4},{7,5},{8,14},{9,15},{10,... | collective-permute-start | bytes 479240 | tf_op jit(solution)/shard_map/ppermute | solution.py:576
  23.5 12.6 %copy-start.15 = (s32[1,1024]{1,0:T(1,128)S(1)}, s32[1,1024]{1,0:T(1,128)}, u32[]{:S(2)}) copy-start(s32[1,1024]{1,0:T(1,128)} %refs_6_.3) | copy-start | bytes 12292
  23.5 10.5 %collective-permute-start.3 = (bf16[4,104,768]{2,1,0:T(8,128)(2,1)S(1)}, bf16[4,104,768]{2,1,0:T(8,128)(2,1)S(1)}, u32[]{:S(2)}, u32[]{:S(2)}) collective-permute-start(bf16[4,104,768]{2,1,0:T(8,128)(2,1)S(1)} %pad_maximum_fusion), channel_id=1, source_target_pairs={{0,8},{1,17},{2,10},{3,19},{4,12},{5,21},{6,14},{7,23},{8,0},{9,25... | collective-permute-start | bytes 1916936 | tf_op jit(solution)/shard_map/ppermute | solution.py:576
  34.0 22.7 %copy-start.5 = (bf16[8,104,768]{2,1,0:T(8,128)(2,1)}, bf16[8,104,768]{2,1,0:T(8,128)(2,1)S(1)}, u32[]{:S(2)}) copy-start(bf16[8,104,768]{2,1,0:T(8,128)(2,1)S(1)} %constant_dynamic-update-slice_fusion.refs_0_) | copy-start | bytes 3833860
  34.0 17.4 %collective-permute-start.4 = (bf16[8,104,768]{2,1,0:T(8,128)(2,1)S(1)}, bf16[8,104,768]{2,1,0:T(8,128)(2,1)}, u32[]{:S(2)}, u32[]{:S(2)}) collective-permute-start(bf16[8,104,768]{2,1,0:T(8,128)(2,1)S(1)} %constant_dynamic-update-slice_fusion.refs_0_), channel_id=1, source_target_pairs={{0,16},{1,9},{2,18},{3,11},{4,20},{5,13},{6,22},{7,15},{8,24},{9,1... | collective-permute-start | bytes 3833864 | tf_op jit(solution)/shard_map/ppermute | solution.py:576
  36.9 9.7 %collective-permute-start.7 = (bf16[96,768]{1,0:T(8,128)(2,1)S(1)}, bf16[96,768]{1,0:T(8,128)(2,1)S(1)}, u32[]{:S(2)}, u32[]{:S(2)}) collective-permute-start(bf16[96,768]{1,0:T(8,128)(2,1)S(1)} %constant_dynamic-slice_fusion.9), channel_id=1, source_target_pairs={{0,2},{1,3},{2,4},{3,5},{4,6},{5,7},{6,0},{7,1},{8,10},{9,11},{10,... | collective-permute-start | bytes 442376 | tf_op jit(solution)/shard_map/ppermute | solution.py:576
  40.8 9.9 %collective-permute-start.8 = (bf16[96,768]{1,0:T(8,128)(2,1)S(1)}, bf16[96,768]{1,0:T(8,128)(2,1)S(1)}, u32[]{:S(2)}, u32[]{:S(2)}) collective-permute-start(bf16[96,768]{1,0:T(8,128)(2,1)S(1)} %constant_dynamic-slice_fusion.9), channel_id=1, source_target_pairs={{0,4},{1,5},{2,6},{3,7},{4,0},{5,1},{6,2},{7,3},{8,12},{9,13},{10,... | collective-permute-start | bytes 442376 | tf_op jit(solution)/shard_map/ppermute | solution.py:576
  42.5 8.2 %collective-permute-start.9 = (bf16[96,768]{1,0:T(8,128)(2,1)S(1)}, bf16[96,768]{1,0:T(8,128)(2,1)S(1)}, u32[]{:S(2)}, u32[]{:S(2)}) collective-permute-start(bf16[96,768]{1,0:T(8,128)(2,1)S(1)} %constant_dynamic-slice_fusion.9), channel_id=1, source_target_pairs={{0,6},{1,7},{2,0},{3,1},{4,2},{5,3},{6,4},{7,5},{8,14},{9,15},{10,... | collective-permute-start | bytes 442376 | tf_op jit(solution)/shard_map/ppermute | solution.py:576
  51.5 10.0 %collective-permute-start.10 = (bf16[4,96,768]{2,1,0:T(8,128)(2,1)S(1)}, bf16[4,96,768]{2,1,0:T(8,128)(2,1)}, u32[]{:S(2)}, u32[]{:S(2)}) collective-permute-start(bf16[4,96,768]{2,1,0:T(8,128)(2,1)S(1)} %pad_maximum_fusion.2), channel_id=1, source_target_pairs={{0,8},{1,17},{2,10},{3,19},{4,12},{5,21},{6,14},{7,23},{8,0},{9,25... | collective-permute-start | bytes 1769480 | tf_op jit(solution)/shard_map/ppermute | solution.py:576
  56.1 22.7 %collective-permute-start.5 = (bf16[8,104,768]{2,1,0:T(8,128)(2,1)S(1)}, bf16[8,104,768]{2,1,0:T(8,128)(2,1)S(1)}, u32[]{:S(2)}, u32[]{:S(2)}) collective-permute-start(bf16[8,104,768]{2,1,0:T(8,128)(2,1)S(1)} %constant_dynamic-update-slice_fusion.refs_0_), channel_id=1, source_target_pairs={{0,1},{1,0},{2,3},{3,2},{4,5},{5,4},{6,7},{7,6},{8,9},{9,8},{10,11... | collective-permute-start | bytes 3833864 | tf_op jit(solution)/shard_map/ppermute | solution.py:576
  56.2 24.7 %collective-permute-start.6 = (bf16[8,104,768]{2,1,0:T(8,128)(2,1)}, bf16[8,104,768]{2,1,0:T(8,128)(2,1)}, u32[]{:S(2)}, u32[]{:S(2)}) collective-permute-start(bf16[8,104,768]{2,1,0:T(8,128)(2,1)} %collective-permute-done.4.refs_1_), channel_id=1, source_target_pairs={{0,1},{1,0},{2,3},{3,2},{4,5},{5,4},{6,7},{7,6},{8,9},{9,8},{10,11... | collective-permute-start | bytes 3833864 | tf_op jit(solution)/shard_map/ppermute | solution.py:576
  62.6 24.1 %copy-start.2 = (bf16[8,96,768]{2,1,0:T(8,128)(2,1)}, bf16[8,96,768]{2,1,0:T(8,128)(2,1)S(1)}, u32[]{:S(2)}) copy-start(bf16[8,96,768]{2,1,0:T(8,128)(2,1)S(1)} %constant_dynamic-update-slice_fusion.5.refs_0_) | copy-start | bytes 3538948
  62.6 9.8 %collective-permute-start.12 = (bf16[96,768]{1,0:T(8,128)(2,1)S(1)}, bf16[96,768]{1,0:T(8,128)(2,1)S(1)}, u32[]{:S(2)}, u32[]{:S(2)}) collective-permute-start(bf16[96,768]{1,0:T(8,128)(2,1)S(1)} %constant_dynamic-slice_fusion.8), channel_id=1, source_target_pairs={{0,2},{1,3},{2,4},{3,5},{4,6},{5,7},{6,0},{7,1},{8,10},{9,11},{10,... | collective-permute-start | bytes 442376 | tf_op jit(solution)/shard_map/ppermute | solution.py:576
  66.5 9.9 %collective-permute-start.13 = (bf16[96,768]{1,0:T(8,128)(2,1)S(1)}, bf16[96,768]{1,0:T(8,128)(2,1)S(1)}, u32[]{:S(2)}, u32[]{:S(2)}) collective-permute-start(bf16[96,768]{1,0:T(8,128)(2,1)S(1)} %constant_dynamic-slice_fusion.8), channel_id=1, source_target_pairs={{0,4},{1,5},{2,6},{3,7},{4,0},{5,1},{6,2},{7,3},{8,12},{9,13},{10,... | collective-permute-start | bytes 442376 | tf_op jit(solution)/shard_map/ppermute | solution.py:576
  68.2 8.2 %collective-permute-start.14 = (bf16[96,768]{1,0:T(8,128)(2,1)S(1)}, bf16[96,768]{1,0:T(8,128)(2,1)S(1)}, u32[]{:S(2)}, u32[]{:S(2)}) collective-permute-start(bf16[96,768]{1,0:T(8,128)(2,1)S(1)} %constant_dynamic-slice_fusion.8), channel_id=1, source_target_pairs={{0,6},{1,7},{2,0},{3,1},{4,2},{5,3},{6,4},{7,5},{8,14},{9,15},{10,... | collective-permute-start | bytes 442376 | tf_op jit(solution)/shard_map/ppermute | solution.py:576
  72.4 25.5 %collective-permute-start.11 = (bf16[8,96,768]{2,1,0:T(8,128)(2,1)S(1)}, bf16[8,96,768]{2,1,0:T(8,128)(2,1)}, u32[]{:S(2)}, u32[]{:S(2)}) collective-permute-start(bf16[8,96,768]{2,1,0:T(8,128)(2,1)S(1)} %constant_dynamic-update-slice_fusion.5.refs_0_), channel_id=1, source_target_pairs={{0,16},{1,9},{2,18},{3,11},{4,20},{5,13},{6,22},{7,15},{8,24},{9,1... | collective-permute-start | bytes 3538952 | tf_op jit(solution)/shard_map/ppermute | solution.py:576
  76.4 60.1 %collective-permute-start.15 = (bf16[8,96,768]{2,1,0:T(8,128)(2,1)S(1)}, bf16[8,96,768]{2,1,0:T(8,128)(2,1)}, u32[]{:S(2)}, u32[]{:S(2)}) collective-permute-start(bf16[8,96,768]{2,1,0:T(8,128)(2,1)S(1)} %constant_dynamic-update-slice_fusion.5.refs_0_), channel_id=1, source_target_pairs={{0,1},{1,0},{2,3},{3,2},{4,5},{5,4},{6,7},{7,6},{8,9},{9,8},{10,11... | collective-permute-start | bytes 3538952 | tf_op jit(solution)/shard_map/ppermute | solution.py:576
  77.3 49.1 %collective-permute-start.17 = (bf16[4,96,768]{2,1,0:T(8,128)(2,1)}, bf16[4,96,768]{2,1,0:T(8,128)(2,1)}, u32[]{:S(2)}, u32[]{:S(2)}) collective-permute-start(bf16[4,96,768]{2,1,0:T(8,128)(2,1)} %pad_maximum_fusion.3), channel_id=1, source_target_pairs={{0,8},{1,17},{2,10},{3,19},{4,12},{5,21},{6,14},{7,23},{8,0},{9,25... | collective-permute-start | bytes 1769480 | tf_op jit(solution)/shard_map/ppermute | solution.py:576
  78.8 1.0 copy-start.6
  79.8 1.0 copy-start.10
  97.9 28.4 %copy-start.7 = (bf16[8,96,768]{2,1,0:T(8,128)(2,1)S(1)}, bf16[8,96,768]{2,1,0:T(8,128)(2,1)}, u32[]{:S(2)}) copy-start(bf16[8,96,768]{2,1,0:T(8,128)(2,1)} %copy-done.6) | copy-start | bytes 3538948
  97.9 38.6 %collective-permute-start.16 = (bf16[8,96,768]{2,1,0:T(8,128)(2,1)}, bf16[8,96,768]{2,1,0:T(8,128)(2,1)}, u32[]{:S(2)}, u32[]{:S(2)}) collective-permute-start(bf16[8,96,768]{2,1,0:T(8,128)(2,1)} %collective-permute-done.11.refs_1_), channel_id=1, source_target_pairs={{0,1},{1,0},{2,3},{3,2},{4,5},{5,4},{6,7},{7,6},{8,9},{9,8},{10,11... | collective-permute-start | bytes 3538952 | tf_op jit(solution)/shard_map/ppermute | solution.py:576
  127.5 9.0 %copy-start.8 = (bf16[8,96,768]{2,1,0:T(8,128)(2,1)}, bf16[8,96,768]{2,1,0:T(8,128)(2,1)S(1)}, u32[]{:S(2)}) copy-start(bf16[8,96,768]{2,1,0:T(8,128)(2,1)S(1)} %constant_dynamic-update-slice_fusion.7.refs_0_) | copy-start | bytes 3538948
  127.5 34.7 %collective-permute-start.18 = (bf16[8,96,768]{2,1,0:T(8,128)(2,1)S(1)}, bf16[8,96,768]{2,1,0:T(8,128)(2,1)}, u32[]{:S(2)}, u32[]{:S(2)}) collective-permute-start(bf16[8,96,768]{2,1,0:T(8,128)(2,1)S(1)} %constant_dynamic-update-slice_fusion.7.refs_0_), channel_id=1, source_target_pairs={{0,16},{1,9},{2,18},{3,11},{4,20},{5,13},{6,22},{7,15},{8,24},{9,1... | collective-permute-start | bytes 3538952 | tf_op jit(solution)/shard_map/ppermute | solution.py:576
  129.3 34.2 %collective-permute-start.19 = (bf16[8,96,768]{2,1,0:T(8,128)(2,1)S(1)}, bf16[8,96,768]{2,1,0:T(8,128)(2,1)}, u32[]{:S(2)}, u32[]{:S(2)}) collective-permute-start(bf16[8,96,768]{2,1,0:T(8,128)(2,1)S(1)} %constant_dynamic-update-slice_fusion.7.refs_0_), channel_id=1, source_target_pairs={{0,1},{1,0},{2,3},{3,2},{4,5},{5,4},{6,7},{7,6},{8,9},{9,8},{10,11... | collective-permute-start | bytes 3538952 | tf_op jit(solution)/shard_map/ppermute | solution.py:576
  162.2 3.2 collective-permute-start.20
  165.4 1.0 copy-start.12
  198.3 13.5 %collective-permute-start.21 = (bf16[16,96,768]{2,1,0:T(8,128)(2,1)}, bf16[16,96,768]{2,1,0:T(8,128)(2,1)S(1)}, u32[]{:S(2)}, u32[]{:S(2)}) collective-permute-start(bf16[16,96,768]{2,1,0:T(8,128)(2,1)} %get-tuple-element.114), channel_id=1, source_target_pairs={{0,1},{1,0},{2,3},{3,2},{4,5},{5,4},{6,7},{7,6},{8,9},{9,8},{10,11... | collective-permute-start | bytes 7077896 | tf_op jit(solution)/shard_map/ppermute | solution.py:576
  211.8 1.5 copy-start.4
  213.3 5.9 %copy-start.16 = (f32[8,768]{1,0:T(8,128)S(1)}, f32[8,768]{1,0:T(8,128)}, u32[]{:S(2)}) copy-start(f32[8,768]{1,0:T(8,128)} %get-tuple-element.123) | copy-start | bytes 73732
  217.3 16.4 %collective-permute-start.22 = (bf16[8,96,768]{2,1,0:T(8,128)(2,1)}, bf16[8,96,768]{2,1,0:T(8,128)(2,1)S(1)}, u32[]{:S(2)}, u32[]{:S(2)}) collective-permute-start(bf16[8,96,768]{2,1,0:T(8,128)(2,1)} %get-tuple-element.186), channel_id=1, source_target_pairs={{0,8},{1,17},{2,10},{3,19},{4,12},{5,21},{6,14},{7,23},{8,0},{9,25... | collective-permute-start | bytes 3538952 | tf_op jit(solution)/shard_map/ppermute | solution.py:576
  233.8 17.5 %collective-permute-start.23 = (bf16[16,104,768]{2,1,0:T(8,128)(2,1)}, bf16[16,104,768]{2,1,0:T(8,128)(2,1)}, u32[]{:S(2)}, u32[]{:S(2)}) collective-permute-start(bf16[16,104,768]{2,1,0:T(8,128)(2,1)} %get-tuple-element.125), channel_id=1, source_target_pairs={{0,1},{1,0},{2,3},{3,2},{4,5},{5,4},{6,7},{7,6},{8,9},{9,8},{10,11... | collective-permute-start | bytes 7667720 | tf_op jit(solution)/shard_map/ppermute | solution.py:576
  234.0 17.2 %collective-permute-start.24 = (bf16[4,96,768]{2,1,0:T(8,128)(2,1)S(1)}, bf16[4,96,768]{2,1,0:T(8,128)(2,1)S(1)}, u32[]{:S(2)}, u32[]{:S(2)}) collective-permute-start(bf16[4,96,768]{2,1,0:T(8,128)(2,1)S(1)} %get-tuple-element.192), channel_id=1, source_target_pairs={{0,16},{1,9},{2,18},{3,11},{4,20},{5,13},{6,22},{7,15},{8,24},{9,1... | collective-permute-start | bytes 1769480 | tf_op jit(solution)/shard_map/ppermute | solution.py:576
  251.2 0.8 copy-start.13
  252.1 4.6 %copy-start.17 = (f32[8,768]{1,0:T(8,128)S(1)}, f32[8,768]{1,0:T(8,128)}, u32[]{:S(2)}) copy-start(f32[8,768]{1,0:T(8,128)} %get-tuple-element.159) | copy-start | bytes 73732
  256.2 23.6 %collective-permute-start.25 = (bf16[8,104,768]{2,1,0:T(8,128)(2,1)}, bf16[8,104,768]{2,1,0:T(8,128)(2,1)S(1)}, u32[]{:S(2)}, u32[]{:S(2)}) collective-permute-start(bf16[8,104,768]{2,1,0:T(8,128)(2,1)} %get-tuple-element.183), channel_id=1, source_target_pairs={{0,8},{1,17},{2,10},{3,19},{4,12},{5,21},{6,14},{7,23},{8,0},{9,25... | collective-permute-start | bytes 3833864 | tf_op jit(solution)/shard_map/ppermute | solution.py:576
  259.0 20.8 %collective-permute-start.26 = (bf16[96,768]{1,0:T(8,128)(2,1)}, bf16[96,768]{1,0:T(8,128)(2,1)S(1)}, u32[]{:S(2)}, u32[]{:S(2)}) collective-permute-start(bf16[96,768]{1,0:T(8,128)(2,1)} %get-tuple-element.202), channel_id=1, source_target_pairs={{0,2},{1,3},{2,4},{3,5},{4,6},{5,7},{6,0},{7,1},{8,10},{9,11},{10,... | collective-permute-start | bytes 442376 | tf_op jit(solution)/shard_map/ppermute | solution.py:576
  262.2 17.6 %collective-permute-start.27 = (bf16[96,768]{1,0:T(8,128)(2,1)S(1)}, bf16[96,768]{1,0:T(8,128)(2,1)S(1)}, u32[]{:S(2)}, u32[]{:S(2)}) collective-permute-start(bf16[96,768]{1,0:T(8,128)(2,1)S(1)} %get-tuple-element.201), channel_id=1, source_target_pairs={{0,4},{1,5},{2,6},{3,7},{4,0},{5,1},{6,2},{7,3},{8,12},{9,13},{10,... | collective-permute-start | bytes 442376 | tf_op jit(solution)/shard_map/ppermute | solution.py:576
  262.4 17.4 %collective-permute-start.28 = (bf16[96,768]{1,0:T(8,128)(2,1)S(1)}, bf16[96,768]{1,0:T(8,128)(2,1)S(1)}, u32[]{:S(2)}, u32[]{:S(2)}) collective-permute-start(bf16[96,768]{1,0:T(8,128)(2,1)S(1)} %get-tuple-element.200), channel_id=1, source_target_pairs={{0,6},{1,7},{2,0},{3,1},{4,2},{5,3},{6,4},{7,5},{8,14},{9,15},{10,... | collective-permute-start | bytes 442376 | tf_op jit(solution)/shard_map/ppermute | solution.py:576
  279.8 1.1 copy-start.11
  280.9 1.7 copy-start.14
  282.5 17.4 %collective-permute-start.29 = (bf16[4,104,768]{2,1,0:T(8,128)(2,1)S(1)}, bf16[4,104,768]{2,1,0:T(8,128)(2,1)S(1)}, u32[]{:S(2)}, u32[]{:S(2)}) collective-permute-start(bf16[4,104,768]{2,1,0:T(8,128)(2,1)S(1)} %get-tuple-element.189), channel_id=1, source_target_pairs={{0,16},{1,9},{2,18},{3,11},{4,20},{5,13},{6,22},{7,15},{8,24},{9,1... | collective-permute-start | bytes 1916936 | tf_op jit(solution)/shard_map/ppermute | solution.py:576
  282.7 17.1 %collective-permute-start.30 = (bf16[96,768]{1,0:T(8,128)(2,1)S(1)}, bf16[96,768]{1,0:T(8,128)(2,1)S(1)}, u32[]{:S(2)}, u32[]{:S(2)}) collective-permute-start(bf16[96,768]{1,0:T(8,128)(2,1)S(1)} %add_convert_fusion.21), channel_id=1, source_target_pairs={{0,16},{1,9},{2,18},{3,11},{4,20},{5,13},{6,22},{7,15},{8,24},{9,1... | collective-permute-start | bytes 442376 | tf_op jit(solution)/shard_map/ppermute | solution.py:576
  300.0 20.9 %collective-permute-start.31 = (bf16[104,768]{1,0:T(8,128)(2,1)S(1)}, bf16[104,768]{1,0:T(8,128)(2,1)S(1)}, u32[]{:S(2)}, u32[]{:S(2)}) collective-permute-start(bf16[104,768]{1,0:T(8,128)(2,1)S(1)} %get-tuple-element.198), channel_id=1, source_target_pairs={{0,2},{1,3},{2,4},{3,5},{4,6},{5,7},{6,0},{7,1},{8,10},{9,11},{10,... | collective-permute-start | bytes 479240 | tf_op jit(solution)/shard_map/ppermute | solution.py:576
  300.1 20.8 %collective-permute-start.32 = (bf16[104,768]{1,0:T(8,128)(2,1)S(1)}, bf16[104,768]{1,0:T(8,128)(2,1)S(1)}, u32[]{:S(2)}, u32[]{:S(2)}) collective-permute-start(bf16[104,768]{1,0:T(8,128)(2,1)S(1)} %get-tuple-element.197), channel_id=1, source_target_pairs={{0,4},{1,5},{2,6},{3,7},{4,0},{5,1},{6,2},{7,3},{8,12},{9,13},{10,... | collective-permute-start | bytes 479240 | tf_op jit(solution)/shard_map/ppermute | solution.py:576
  300.9 20.1 %collective-permute-start.33 = (bf16[104,768]{1,0:T(8,128)(2,1)S(1)}, bf16[104,768]{1,0:T(8,128)(2,1)S(1)}, u32[]{:S(2)}, u32[]{:S(2)}) collective-permute-start(bf16[104,768]{1,0:T(8,128)(2,1)S(1)} %get-tuple-element.196), channel_id=1, source_target_pairs={{0,6},{1,7},{2,0},{3,1},{4,2},{5,3},{6,4},{7,5},{8,14},{9,15},{10,... | collective-permute-start | bytes 479240 | tf_op jit(solution)/shard_map/ppermute | solution.py:576
  321.0 12.6 %collective-permute-start.34 = (bf16[104,768]{1,0:T(8,128)(2,1)S(1)}, bf16[104,768]{1,0:T(8,128)(2,1)S(1)}, u32[]{:S(2)}, u32[]{:S(2)}) collective-permute-start(bf16[104,768]{1,0:T(8,128)(2,1)S(1)} %add_convert_fusion.16), channel_id=1, source_target_pairs={{0,16},{1,9},{2,18},{3,11},{4,20},{5,13},{6,22},{7,15},{8,24},{9,1... | collective-permute-start | bytes 479240 | tf_op jit(solution)/shard_map/ppermute | solution.py:576
  333.7 5.1 %collective-permute-start.35 = (bf16[16,104,768]{2,1,0:T(8,128)(2,1)}, bf16[16,104,768]{2,1,0:T(8,128)(2,1)S(1)}, u32[]{:S(2)}, u32[]{:S(2)}) collective-permute-start(bf16[16,104,768]{2,1,0:T(8,128)(2,1)} %get-tuple-element.162), channel_id=1, source_target_pairs={{0,1},{1,0},{2,3},{3,2},{4,5},{5,4},{6,7},{7,6},{8,9},{9,8},{10,11... | collective-permute-start | bytes 7667720 | tf_op jit(solution)/shard_map/ppermute | solution.py:576
  342.3 17.6 %collective-permute-start.36 = (bf16[8,104,768]{2,1,0:T(8,128)(2,1)}, bf16[8,104,768]{2,1,0:T(8,128)(2,1)}, u32[]{:S(2)}, u32[]{:S(2)}) collective-permute-start(bf16[8,104,768]{2,1,0:T(8,128)(2,1)} %get-tuple-element.182), channel_id=1, source_target_pairs={{0,8},{1,17},{2,10},{3,19},{4,12},{5,21},{6,14},{7,23},{8,0},{9,25... | collective-permute-start | bytes 3833864 | tf_op jit(solution)/shard_map/ppermute | solution.py:576
  344.1 21.9 %collective-permute-start.44 = (bf16[2,96,768]{2,1,0:T(8,128)(2,1)S(1)}, bf16[2,96,768]{2,1,0:T(8,128)(2,1)}, u32[]{:S(2)}, u32[]{:S(2)}) collective-permute-start(bf16[2,96,768]{2,1,0:T(8,128)(2,1)S(1)} %pad_maximum_fusion.7), channel_id=1, source_target_pairs={{0,8},{1,17},{2,10},{3,19},{4,12},{5,21},{6,14},{7,23},{8,0},{9,25... | collective-permute-start | bytes 884744 | tf_op jit(solution)/shard_map/ppermute | solution.py:576
  362.2 13.9 %collective-permute-start.37 = (bf16[4,104,768]{2,1,0:T(8,128)(2,1)}, bf16[4,104,768]{2,1,0:T(8,128)(2,1)S(1)}, u32[]{:S(2)}, u32[]{:S(2)}) collective-permute-start(bf16[4,104,768]{2,1,0:T(8,128)(2,1)} %get-tuple-element.188), channel_id=1, source_target_pairs={{0,16},{1,9},{2,18},{3,11},{4,20},{5,13},{6,22},{7,15},{8,24},{9,1... | collective-permute-start | bytes 1916936 | tf_op jit(solution)/shard_map/ppermute | solution.py:576
  364.3 10.4 %collective-permute-start.43 = (bf16[2,104,768]{2,1,0:T(8,128)(2,1)S(1)}, bf16[2,104,768]{2,1,0:T(8,128)(2,1)S(1)}, u32[]{:S(2)}, u32[]{:S(2)}) collective-permute-start(bf16[2,104,768]{2,1,0:T(8,128)(2,1)S(1)} %pad_maximum_fusion.5), channel_id=1, source_target_pairs={{0,8},{1,17},{2,10},{3,19},{4,12},{5,21},{6,14},{7,23},{8,0},{9,25... | collective-permute-start | bytes 958472 | tf_op jit(solution)/shard_map/ppermute | solution.py:576
  374.7 17.2 %copy-start.9 = (bf16[4,104,768]{2,1,0:T(8,128)(2,1)}, bf16[4,104,768]{2,1,0:T(8,128)(2,1)S(1)}, u32[]{:S(2)}) copy-start(bf16[4,104,768]{2,1,0:T(8,128)(2,1)S(1)} %constant_dynamic-update-slice_fusion.12.in_ref) | copy-start | bytes 1916932
  376.3 8.8 %collective-permute-start.38 = (bf16[104,768]{1,0:T(8,128)(2,1)S(1)}, bf16[104,768]{1,0:T(8,128)(2,1)S(1)}, u32[]{:S(2)}, u32[]{:S(2)}) collective-permute-start(bf16[104,768]{1,0:T(8,128)(2,1)S(1)} %get-tuple-element.193), channel_id=1, source_target_pairs={{0,2},{1,3},{2,4},{3,5},{4,6},{5,7},{6,0},{7,1},{8,10},{9,11},{10,... | collective-permute-start | bytes 479240 | tf_op jit(solution)/shard_map/ppermute | solution.py:576
  377.2 12.8 %collective-permute-start.39 = (bf16[104,768]{1,0:T(8,128)(2,1)S(1)}, bf16[104,768]{1,0:T(8,128)(2,1)S(1)}, u32[]{:S(2)}, u32[]{:S(2)}) collective-permute-start(bf16[104,768]{1,0:T(8,128)(2,1)S(1)} %get-tuple-element.195), channel_id=1, source_target_pairs={{0,4},{1,5},{2,6},{3,7},{4,0},{5,1},{6,2},{7,3},{8,12},{9,13},{10,... | collective-permute-start | bytes 479240 | tf_op jit(solution)/shard_map/ppermute | solution.py:576
  378.0 12.0 %collective-permute-start.40 = (bf16[104,768]{1,0:T(8,128)(2,1)S(1)}, bf16[104,768]{1,0:T(8,128)(2,1)S(1)}, u32[]{:S(2)}, u32[]{:S(2)}) collective-permute-start(bf16[104,768]{1,0:T(8,128)(2,1)S(1)} %get-tuple-element.194), channel_id=1, source_target_pairs={{0,6},{1,7},{2,0},{3,1},{4,2},{5,3},{6,4},{7,5},{8,14},{9,15},{10,... | collective-permute-start | bytes 479240 | tf_op jit(solution)/shard_map/ppermute | solution.py:576
  390.1 6.5 %collective-permute-start.41 = (bf16[104,768]{1,0:T(8,128)(2,1)S(1)}, bf16[104,768]{1,0:T(8,128)(2,1)S(1)}, u32[]{:S(2)}, u32[]{:S(2)}) collective-permute-start(bf16[104,768]{1,0:T(8,128)(2,1)S(1)} %fusion.2), channel_id=1, source_target_pairs={{0,16},{1,9},{2,18},{3,11},{4,20},{5,13},{6,22},{7,15},{8,24},{9,1... | collective-permute-start | bytes 479240 | tf_op jit(solution)/shard_map/ppermute | solution.py:576
  396.6 14.5 %copy-start.1 = (bf16[96,3072]{1,0:T(8,128)(2,1)S(1)}, bf16[96,3072]{1,0:T(8,128)(2,1)}, u32[]{:S(2)}) copy-start(bf16[96,3072]{1,0:T(8,128)(2,1)} %param.24) | copy-start | bytes 1769476
  396.6 7.1 %collective-permute-start.42 = (bf16[2,104,768]{2,1,0:T(8,128)(2,1)S(1)}, bf16[2,104,768]{2,1,0:T(8,128)(2,1)S(1)}, u32[]{:S(2)}, u32[]{:S(2)}) collective-permute-start(bf16[2,104,768]{2,1,0:T(8,128)(2,1)S(1)} %pad_maximum_fusion.6), channel_id=1, source_target_pairs={{0,8},{1,17},{2,10},{3,19},{4,12},{5,21},{6,14},{7,23},{8,0},{9,25... | collective-permute-start | bytes 958472 | tf_op jit(solution)/shard_map/ppermute | solution.py:576
  403.7 0.8 copy-start.3

commit v2 on v1

--- a/solution.py
+++ b/solution.py
@@ -90,6 +90,9 @@
     )(x, weights, bias)
 
 
+MASKED = -1e30
+
+
 def window_sizes(block, length):
     sizes = [block + extra for extra in (128, 256, 384, 512) if block + extra < length]
     return sizes + [length]
@@ -118,36 +121,68 @@
             body(pl.multiple_of(start, LANES), size)
 
 
-def attend_forward_kernel(sizes, limits_ref, q_ref, k_ref, v_ref, segq_ref, segk_ref, o_ref, lse_ref):
-    first = lax.broadcasted_iota(jnp.int32, (1, LANES), 1) < DH
-    rows = q_ref.shape[1]
-    scale = jnp.asarray(DH ** (-0.5), BF16)
+def chunks_of(size, most):
+    return [(at, min(most, size - at)) for at in range(0, size, most)]
+
+
+def head_lanes():
+    lane = lax.broadcasted_iota(jnp.int32, (1, LANES), 1)
+    first = lane < DH
+    return (first, jnp.logical_not(first)), lane % DH
+
+
+def mask_keys(k_ref, seg_ref, kx_ref):
+    mine, lane = head_lanes()
+    keys = k_ref[0]
+    outside = jnp.where(seg_ref[...] == lane, 0.0, jnp.where(lane <= SEG, MASKED, 0.0)).astype(BF16)
+    for h in range(2):
+        kx_ref[h] = jnp.where(mine[h], keys, outside)
+
+
+def mask_queries(query, seg):
+    mine, lane = head_lanes()
+    inside = (seg == lane).astype(BF16)
+    return [jnp.where(own, query, inside) for own in mine]
+
+
+def attend_forward_kernel(
+    sizes, limits_ref, q_ref, k_ref, v_ref, segq_ref, segk_ref, o_ref, lse_ref, kx_ref, vt_ref, s_ref
+):
+    block = pl.program_id(1)
+
+    @pl.when(block == 0)
+    def _():
+        mask_keys(k_ref, segk_ref, kx_ref)
+        vt_ref[...] = v_ref[0].T
 
     def body(start, size):
-        query = q_ref[0] * scale
-        keys = k_ref[0, pl.ds(start, size), :]
-        values = v_ref[0, pl.ds(start, size), :]
-        allowed = segq_ref[...] == segk_ref[:, pl.ds(start, size)]
+        queries = mask_queries(q_ref[0] * jnp.asarray(DH ** (-0.5), BF16), segq_ref[...])
         parts = []
-        stats = []
-        for mine in (first, jnp.logical_not(first)):
-            scores = nt(jnp.where(mine, query, jnp.zeros_like(query)), keys)
-            scores = jnp.where(allowed, scores, NEG_FILL)
-            highest = jnp.max(scores, axis=1, keepdims=True)
-            exponent = jnp.exp(scores - highest)
-            total = jnp.sum(exponent, axis=1, keepdims=True)
-            parts.append(nn(exponent.astype(BF16), values) / total)
-            stats.append(highest + jnp.log(total))
-        o_ref[...] = jnp.where(first, parts[0], parts[1]).astype(BF16)
-        both = jnp.where(first, stats[0], stats[1])
-        flipped = both.T
-        lse_ref[0, 0:1, :] = flipped[0:1, :]
-        lse_ref[0, 1:2, :] = flipped[DH : DH + 1, :]
-
-    for_window(limits_ref, pl.program_id(1), sizes, body)
-
-
-def attend_forward(qkv, limits, seg_column, seg_row, block):
+        for h in range(2):
+            highest = None
+            for at, count in chunks_of(size, 128):
+                scores = nt(kx_ref[h, pl.ds(start + at, count), :], queries[h])
+                s_ref[h, at : at + count, :] = scores
+                top = jnp.max(scores, axis=0, keepdims=True)
+                highest = top if highest is None else jnp.maximum(highest, top)
+            total = None
+            out = None
+            scaled = highest * LOG2E
+            for at, count in chunks_of(size, 256):
+                exponent = jnp.exp2(s_ref[h, at : at + count, :] * LOG2E - scaled)
+                part = jnp.sum(exponent, axis=0, keepdims=True)
+                total = part if total is None else total + part
+                values = vt_ref[h * DH : (h + 1) * DH, pl.ds(start + at, count)]
+                part = nn(values, exponent.astype(BF16))
+                out = part if out is None else out + part
+            parts.append(out / total)
+            lse_ref[0, h : h + 1, :] = scaled + jnp.log2(total)
+        o_ref[...] = jnp.concatenate(parts).T.astype(BF16)
+
+    for_window(limits_ref, block, sizes, body)
+
+
+def attend_forward(qkv, limits, seg_column, block):
     _, length, width = qkv.shape
     pairs = width // LANES
     return pl.pallas_call(
@@ -161,16 +196,21 @@
                 pl.BlockSpec((1, length, LANES), lambda p, b, _: (1, 0, p)),
                 pl.BlockSpec((1, length, LANES), lambda p, b, _: (2, 0, p)),
                 pl.BlockSpec((block, 1), lambda p, b, _: (b, 0)),
-                pl.BlockSpec((1, length), lambda p, b, _: (0, 0)),
+                pl.BlockSpec((length, 1), lambda p, b, _: (0, 0)),
             ],
             out_specs=[
                 pl.BlockSpec((block, LANES), lambda p, b, _: (b, p)),
                 pl.BlockSpec((1, 8, block), lambda p, b, _: (p, 0, b)),
             ],
+            scratch_shapes=[
+                pltpu.VMEM((2, length, LANES), BF16),
+                pltpu.VMEM((LANES, length), BF16),
+                pltpu.VMEM((2, length, block), F32),
+            ],
         ),
         cost_estimate=cost(8 * length * length * width, qkv),
         name="attend_forward",
-    )(limits, qkv, qkv, qkv, seg_column, seg_row)
+    )(limits, qkv, qkv, qkv, seg_column, seg_column)
 
 
 def attend_backward_kernel(
@@ -180,49 +220,57 @@
     k_ref,
     v_ref,
     d_ref,
+    o_ref,
     lse_ref,
+    segq_ref,
     segk_ref,
-    segq_ref,
     grad_ref,
     sums_ref,
+    kx_ref,
+    kt_ref,
     dk_ref,
     dv_ref,
     dq_ref,
 ):
     block = pl.program_id(1)
-    first = lax.broadcasted_iota(jnp.int32, (1, LANES), 1) < DH
     rows = q_ref.shape[1]
-    scale = jnp.asarray(DH ** (-0.5), BF16)
+    mine, _ = head_lanes()
 
     @pl.when(block == 0)
     def _():
         dk_ref[...] = jnp.zeros_like(dk_ref)
         dv_ref[...] = jnp.zeros_like(dv_ref)
+        mask_keys(k_ref, segk_ref, kx_ref)
+        kt_ref[...] = k_ref[0].T
 
     def body(start, size):
-        query = q_ref[0] * scale
+        query = q_ref[0] * jnp.asarray(DH ** (-0.5), BF16)
         grads = d_ref[...]
-        keys = k_ref[0, pl.ds(start, size), :]
-        values = v_ref[0, pl.ds(start, size), :]
-        allowed = segk_ref[pl.ds(start, size), :] == segq_ref[...]
-        grad_query = []
-        grad_key = None
-        for h, mine in enumerate((first, jnp.logical_not(first))):
-            query_h = jnp.where(mine, query, jnp.zeros_like(query))
-            grads_h = jnp.where(mine, grads, jnp.zeros_like(grads))
-            scores = nt(keys, query_h)
-            weights = jnp.where(allowed, jnp.exp(scores - lse_ref[0, h : h + 1, :]), 0.0)
-            grad_weights = nt(values, grads_h)
-            inner = jnp.sum(weights * grad_weights, axis=0, keepdims=True)
-            grad_scores = (weights * (grad_weights - inner)).astype(BF16)
-            dv_h = nn(weights.astype(BF16), grads_h)
-            dk_h = nn(grad_scores, query_h)
-            grad_query.append(tn(grad_scores, keys))
-            grad_key, grad_value = (dk_h, dv_h) if grad_key is None else (grad_key + dk_h, grad_value + dv_h)
-        dk_ref[pl.ds(start, size), :] += grad_key
-        dv_ref[pl.ds(start, size), :] += grad_value
+        none = jnp.zeros_like(query)
+        queries = mask_queries(query, segq_ref[...])
+        plain = jnp.concatenate([jnp.where(own, query, none) for own in mine])
+        pulls = [jnp.where(own, grads, none) for own in mine]
+        pulled = jnp.concatenate(pulls)
+        products = (grads.astype(F32) * o_ref[...].astype(F32)).T
+        inner = [jnp.sum(products[h * DH : (h + 1) * DH], axis=0, keepdims=True) for h in range(2)]
+        grad_query = [None, None]
+        for at, count in chunks_of(size, 256):
+            place = pl.ds(start + at, count)
+            values = v_ref[0, place, :]
+            weights_low = []
+            grads_low = []
+            for h in range(2):
+                scores = nt(kx_ref[h, place, :], queries[h])
+                weights = jnp.exp2(scores * LOG2E - lse_ref[0, h : h + 1, :])
+                grad_scores = (weights * (nt(values, pulls[h]) - inner[h])).astype(BF16)
+                weights_low.append(weights.astype(BF16))
+                grads_low.append(grad_scores)
+                part = nn(kt_ref[h * DH : (h + 1) * DH, place], grad_scores)
+                grad_query[h] = part if grad_query[h] is None else grad_query[h] + part
+            dv_ref[place, :] += nn(jnp.concatenate(weights_low, axis=1), pulled)
+            dk_ref[place, :] += nn(jnp.concatenate(grads_low, axis=1), plain)
         place = pl.ds(pl.multiple_of(block * rows, rows), rows)
-        dq_ref[place, :] = jnp.where(first, grad_query[0], grad_query[1]) * (DH ** (-0.5))
+        dq_ref[place, :] = jnp.concatenate(grad_query).T * (DH ** (-0.5))
 
     for_window(limits_ref, block, sizes, body)
 
@@ -235,7 +283,7 @@
                 sums_ref[t : t + 1, :] = jnp.sum(low.astype(F32), axis=0, keepdims=True)
 
 
-def attend_backward(qkv, grad_context, lse, limits, seg_column, seg_row, block, base, pairs, earlier=None):
+def attend_backward(qkv, grad_context, context, lse, limits, seg_column, block, base, pairs, earlier=None):
     _, length, width = qkv.shape
     anywhere = pl.BlockSpec(memory_space=pl.ANY)
     made = (shape_of((3, length, width), BF16), shape_of((8, width), F32))
@@ -244,7 +292,7 @@
         inner = kernel
 
         def kernel(limits_ref, *refs):
-            inner(limits_ref, *refs[:7], *refs[9:])
+            inner(limits_ref, *refs[:8], *refs[10:])
 
     return pl.pallas_call(
         kernel,
@@ -257,21 +305,23 @@
                 pl.BlockSpec((1, length, LANES), lambda p, b, _: (1, 0, base + p)),
                 pl.BlockSpec((1, length, LANES), lambda p, b, _: (2, 0, base + p)),
                 pl.BlockSpec((block, LANES), lambda p, b, _: (b, base + p)),
+                pl.BlockSpec((block, LANES), lambda p, b, _: (b, base + p)),
                 pl.BlockSpec((1, 8, block), lambda p, b, _: (base + p, 0, b)),
+                pl.BlockSpec((block, 1), lambda p, b, _: (b, 0)),
                 pl.BlockSpec((length, 1), lambda p, b, _: (0, 0)),
-                pl.BlockSpec((1, block), lambda p, b, _: (0, b)),
             ]
             + ([] if earlier is None else [anywhere] * 2),
             out_specs=[
                 pl.BlockSpec((3, length, LANES), lambda p, b, _: (0, 0, base + p)),
                 pl.BlockSpec((8, LANES), lambda p, b, _: (0, base + p)),
             ],
-            scratch_shapes=[pltpu.VMEM((length, LANES), F32)] * 3,
+            scratch_shapes=[pltpu.VMEM((2, length, LANES), BF16), pltpu.VMEM((LANES, length), BF16)]
+            + [pltpu.VMEM((length, LANES), F32)] * 3,
         ),
-        input_output_aliases={} if earlier is None else {8: 0, 9: 1},
+        input_output_aliases={} if earlier is None else {9: 0, 10: 1},
         cost_estimate=cost(12 * length * length * LANES * pairs, qkv),
         name="attend_backward",
-    )(limits, qkv, qkv, qkv, grad_context, lse, seg_column, seg_row, *(earlier or ()))
+    )(limits, qkv, qkv, qkv, grad_context, context, lse, seg_column, seg_column, *(earlier or ()))
 
 
 def norm_values(values, gain, shift):
@@ -604,6 +654,36 @@
     return jnp.concatenate([chain, swap_first(chain, shards)])
 
 
+def lead_kernel(shard, me_ref, p_ref, c_ref, *refs):
+    vectors, out_ref = refs[:-1], refs[-1]
+    pl.when(me_ref[0] < 3)(lambda: out_ref.__setitem__((slice(0, shard), slice(None)), p_ref[...]))
+    pl.when(me_ref[0] == 3)(lambda: out_ref.__setitem__((slice(0, shard), slice(None)), c_ref[...]))
+    rows = [
+        jnp.pad(vector[...].astype(F32), ((0, 0), (0, out_ref.shape[1] - vector.shape[1]))) for vector in vectors
+    ]
+    out_ref[shard:, :] = jnp.concatenate(rows).astype(BF16)
+
+
+def lead_block(me, project_weight, combine_weight, vectors):
+    shard, width = combine_weight.shape
+    vectors = [v[None] for v in vectors]
+    return pl.pallas_call(
+        partial(lead_kernel, shard),
+        out_shape=shape_of((shard + TAIL_ROWS, width), BF16),
+        grid_spec=pltpu.PrefetchScalarGridSpec(
+            num_scalar_prefetch=1,
+            grid=(1,),
+            in_specs=[
+                pl.BlockSpec((shard, width), lambda i, me_ref: (0, jnp.minimum(me_ref[0], 2))),
+                full_spec(combine_weight.shape),
+            ]
+            + [full_spec(v.shape) for v in vectors],
+            out_specs=full_spec((shard + TAIL_ROWS, width)),
+        ),
+        name="lead",
+    )(me, project_weight, combine_weight, *vectors)
+
+
 def assemble_kernel(shard, depth, by_rows, has_tail, me_ref, *refs):
     sources, (out_ref, *tail), sems = refs[:4], refs[4:-1], refs[-1]
     g0, z0, c0 = me_ref[0], me_ref[1], me_ref[2]
@@ -890,57 +970,50 @@
     replica, member = lax.axis_index("grp"), lax.axis_index("fsdp")
     me = jnp.stack([replica, member // 2, member % 2]).astype(jnp.int32)
     fast = lax.axis_size("grp") == 4 and shards % 2 == 0 and shard % 32 == 0 and width == shard * 8
-    small = jnp.concatenate(
-        [project_bias, combine_bias, first_gain, first_shift, expand_bias, reduce_bias, second_gain, second_shift]
-    )
+    small = [project_bias, combine_bias, first_gain, first_shift, expand_bias, reduce_bias, second_gain, second_shift]
 
     if fast:
-        lead = jnp.where(
-            replica < 3,
-            lax.dynamic_slice(project_weight, (0, jnp.minimum(replica, 2) * width), (shard, width)),
-            combine_weight,
-        )
-        rows = jnp.pad(small, (0, TAIL_ROWS * width - small.shape[0])).reshape(TAIL_ROWS, width)
-        lead = jnp.concatenate([lead, rows])
+        lead = lead_block(me, project_weight, combine_weight, small)
         chain_a = chain_of(lead, shards)
-        part = after(lax.dynamic_slice(expand_weight, (0, replica * width), (shard, width)), chain_a)
-        chain_e = chain_of(part, shards)
+        part_e = lax.dynamic_slice(expand_weight, (0, replica * width), (shard, width))
         near_a = near_of(chain_a, shards)
-        far_a = swap_second(near_a, shards)
+        chain_e = chain_of(after(part_e, near_a), shards)
+        far_a, chain_e = lax.optimization_barrier((swap_second(near_a, shards), chain_e))
         arrays = (near_a, far_a, swap_core(near_a, shards), swap_core(far_a, shards))
         attend_full, small_full = assemble(me, arrays, shard, shards, False)
-        small_full = small_full.reshape(shards, -1)
-        near_e = near_of(after(chain_e, far_a), shards)
+        got_e = swap_first(after(chain_e, arrays[3]), shards)
+        small_full = [small_full[:, k, : v.shape[0]].reshape(-1).astype(F32) for k, v in enumerate(small)]
     else:
         attend_shard = jnp.concatenate(
             [project_weight.reshape(shard, 3, width).transpose(1, 0, 2), combine_weight[None]], axis=0
         )
         expand_shard = expand_weight.reshape(shard, 4, width).transpose(1, 0, 2)
         attend_full = lax.all_gather(attend_shard, "fsdp", axis=1, tiled=True)
-        small_full = lax.all_gather(small, "fsdp", axis=0, tiled=False)
+        small_full = split_small(
+            lax.all_gather(jnp.concatenate(small), "fsdp", axis=0, tiled=False), shard, SMALL_ATTEND + SMALL_FEED
+        )
         expand_full = lax.all_gather(expand_shard, "fsdp", axis=1, tiled=True)
         reduce_full = lax.all_gather(reduce_weight, "fsdp", axis=0, tiled=True)
-    bias_pair, bias_combine, gain_one, shift_one, bias_expand, bias_reduce, gain_two, shift_two = split_small(
-        small_full, shard, SMALL_ATTEND + SMALL_FEED
-    )
+    bias_pair, bias_combine, gain_one, shift_one, bias_expand, bias_reduce, gain_two, shift_two = small_full
     bias_all = jnp.stack([bias_pair[:width], jnp.zeros((width,), F32), bias_pair[width:]]).reshape(3, 1, width)
 
     qkv = project(flat, attend_full, bias_all)
     if fast:
-        qkv = after(qkv, near_e)
+        qkv, got_e = lax.optimization_barrier((qkv, got_e))
+        near_e = jnp.concatenate([chain_e, got_e])
         far_e = swap_second(near_e, shards)
-        part = lax.dynamic_slice(reduce_weight, (replica * shard, 0), (shard, width))
-        chain_r = chain_of(after(part, near_e), shards)
-    context, lse = attend_forward(qkv, limits, seg_column, seg_row, block)
+        part_r = lax.dynamic_slice(reduce_weight, (replica * shard, 0), (shard, width))
+        chain_r = chain_of(after(part_r, qkv), shards)
+    context, lse = attend_forward(qkv, limits, seg_column, block)
     vec_one = vector_rows(bias_combine, gain_one, shift_one)
     vec_two = vector_rows(bias_reduce, gain_two, shift_two)
     if fast:
-        context = after(context, far_e, chain_r)
+        context, far_e, chain_r = lax.optimization_barrier((context, far_e, chain_r))
         arrays = (near_e, far_e, swap_core(near_e, shards), swap_core(far_e, shards))
         near_r = near_of(chain_r, shards)
     hidden, hidden_low, normed, inverse = combine(context, attend_full, flat, vec_one, 256)
     if fast:
-        hidden_low, *arrays = lax.optimization_barrier((hidden_low, *arrays, near_r))[:-1]
+        hidden_low, near_r, *arrays = lax.optimization_barrier((hidden_low, near_r, *arrays))
         expand_full = assemble(me, arrays, shard, shards, False)[0]
         far_r = swap_second(near_r, shards)
     act, slope = expand(hidden_low, expand_full, bias_expand.reshape(4, 1, width))
@@ -987,7 +1060,7 @@
         keep_e, send_e = halves(keep_e, got_e)
         got_e = swap_first(send_e, shards)
         grad_qkv = attend_backward(
-            qkv, after(grad_context, own_r, send_e), lse, limits, seg_column, seg_row, block, 0, pieces
+            qkv, after(grad_context, own_r, send_e), context, lse, limits, seg_column, block, 0, pieces
         )
         first_qkv, got_e, *parts_r = lax.optimization_barrier((grad_qkv[0], got_e, *parts_r))
         own_r = add(own_r, *parts_r)
@@ -997,10 +1070,10 @@
         grad_qkv = attend_backward(
             qkv,
             after(grad_context, send_e, own_r),
+            context,
             lse,
             limits,
             seg_column,
-            seg_row,
             block,
             pieces,
             pieces,
@@ -1012,10 +1085,10 @@
         grad_qkv, sums_qkv = attend_backward(
             qkv,
             after(grad_context, own_e),
+            context,
             lse,
             limits,
             seg_column,
-            seg_row,
             block,
             2 * pieces,
             width // LANES - 2 * pieces,
@@ -1026,7 +1099,7 @@
         pair_e = jnp.stack([own_e, swap_second(own_e, shards)])
     else:
         grad_qkv, sums_qkv = attend_backward(
-            qkv, grad_context, lse, limits, seg_column, seg_row, block, 0, width // LANES
+            qkv, grad_context, context, lse, limits, seg_column, block, 0, width // LANES
         )
     attend_vectors = [jnp.concatenate([sums_qkv[0], sums_qkv[2]]), sums_one[2], sums_one[0], sums_one[1]]
     if fast:

time: 417 us -> 406 us (0.974)
  local copies, waits for them, and re-layouts: 28.5 us -> 21.4 us
  waiting for transfers between devices: 70.1 us -> 65.5 us
  starting transfers between devices: 58.3 us -> 54 us
    ppermute x45, waiting for transfers between devices: 70.1 us -> 65.5 us  [hop(): return lax.ppermute(value, AXES, pairs)]
    concatenate x1, local copies, waits for them, and re-layouts: 5.5 us -> 1.1 us  [per_device(): near_e = jnp.concatenate([chain_e, got_e])]
    ppermute x45, starting transfers between devices: 58.3 us -> 54 us  [hop(): return lax.ppermute(value, AXES, pairs)]
    unnamed x49 -> x39, local copies, waits for them, and re-layouts: 9.02 us -> 5.86 us
  transfers between devices with their start and end apart: 45 -> 45, of which waited for: 18 -> 18; matrix products, arithmetic and copies ran while one was open for 6% -> 6% of each run, Pallas kernels for 46% -> 48%
where the time goes in v2:
time: 406 us; the launch traced here: 401 us
  Pallas kernels  229 us (56%)
  waiting for transfers between devices  65.5 us (16%)
  starting transfers between devices  54 us (13%)
  other arithmetic  29.5 us (7%)
  local copies, waits for them, and re-layouts  21.4 us (5%)
    ppermute x45, waiting for transfers between devices, hop(): return lax.ppermute(value, AXES, pairs)  65.5 us
    ppermute x45, starting transfers between devices, hop(): return lax.ppermute(value, AXES, pairs)  54 us
    pallas_call x3, Pallas kernels, attend_backward(): pl.pallas_call(kernel, out_shape=made, grid_spec=pltpu.PrefetchScalarGrid...  44.8 us
    pallas_call x3, Pallas kernels, weight_grad(): pl.pallas_call(partial(weight_grad_kernel, shard, shards // 2, kind, has_...  33.7 us
    pallas_call x1, Pallas kernels, attend_forward(): pl.pallas_call(partial(attend_forward_kernel, window_sizes(block, length)...  29.3 us
    pallas_call x1, Pallas kernels, expand(): pl.pallas_call(expand_kernel, out_shape=(shape_of((rows, count * width),...  20.1 us
    convert_element_type x12, other arithmetic, add(): return sum((part.astype(F32) for part in parts)).astype(BF16)  18.5 us
    pallas_call x3, Pallas kernels, assemble(): pl.pallas_call(partial(assemble_kernel, shard, shards // 2, by_rows, has_...  17 us
  transfers between devices with their start and end apart: 45, of which 18 were waited for; matrix products, arithmetic and copies ran while one was open for 6% of the time, Pallas kernels for 48%

profile of v2, /device:TPU:0, one launch (start us, length us, event | category | flops | bytes accessed | tf_op | source)
XLA Modules:
  0.0 400.6 jit_solution(2828365483728828460)
XLA Ops:
  0.7 1.3 broadcast_in_dim.64.refs_4_
  3.8 2.4 lead.1
  6.2 3.1 collective-permute-start
  9.3 2.6 collective-permute-start.1
  11.9 1.3 collective-permute-start.2
  14.2 2.4 collective-permute-done
  16.6 6.0 %collective-permute-done.1 = bf16[104,768]{1,0:T(8,128)(2,1)S(1)} collective-permute-done((bf16[104,768]{1,0:T(8,128)(2,1)}, bf16[104,768]{1,0:T(8,128)(2,1)S(1)}, u32[]{:S(2)}, u32[]{:S(2)}) %collective-permute-start.1) | collective-permute-done | bytes 159776 | tf_op jit(solution)/shard_map/ppermute | solution.py:626
  23.6 1.6 collective-permute-start.3
  25.2 8.8 %collective-permute-done.3 = bf16[4,104,768]{2,1,0:T(8,128)(2,1)S(1)} collective-permute-done((bf16[4,104,768]{2,1,0:T(8,128)(2,1)S(1)}, bf16[4,104,768]{2,1,0:T(8,128)(2,1)S(1)}, u32[]{:S(2)}, u32[]{:S(2)}) %collective-permute-start.3) | collective-permute-done | bytes 639008 | tf_op jit(solution)/shard_map/ppermute | solution.py:626
  34.1 1.6 collective-permute-start.4
  35.7 3.9 collective-permute-start.5
  39.6 1.6 collective-permute-start.6
  42.1 3.4 collective-permute-done.5
  45.5 4.1 %collective-permute-done.6 = bf16[96,768]{1,0:T(8,128)(2,1)S(1)} collective-permute-done((bf16[96,768]{1,0:T(8,128)(2,1)S(1)}, bf16[96,768]{1,0:T(8,128)(2,1)S(1)}, u32[]{:S(2)}, u32[]{:S(2)}) %collective-permute-start.6) | collective-permute-done | bytes 147488 | tf_op jit(solution)/shard_map/ppermute | solution.py:626
  49.6 1.9 collective-permute-done.4.refs_1_
  54.9 1.5 collective-permute-start.10
  56.7 5.7 %assemble.3 = (bf16[4,768,768]{2,1,0:T(8,128)(2,1)}, bf16[8,8,768]{2,1,0:T(8,128)(2,1)}) custom-call(s32[3]{0:T(128)} %pad_add_fusion.1.me_ref, bf16[8,104,768]{2,1,0:T(8,128)(2,1)} %copy-done.6, bf16[8,104,768]{2,1,0:T(8,128)(2,1)} %collective-permute-done.4.refs_1_, bf16[8,104,768]{2,1,0:T(8,128)(2,1)} %collective-permute-done.8.refs_2_, ...), custom_call_target="tpu_custom_call" | custom-call | tf_op jit(solution)/shard_map/assemble/pallas_call | solution.py:722
  64.0 9.3 %project.1.q_ref.k_ref.v_ref.refs_0_.refs_1_.refs_2_ = bf16[3,1024,768]{2,1,0:T(8,128)(2,1)} custom-call(bf16[1024,768]{1,0:T(8,128)(2,1)} %bitcast.168, bf16[4,768,768]{2,1,0:T(8,128)(2,1)} %get-tuple-element.101.w_ref.wc_ref, f32[3,1,768]{2,1,0:T(1,128)} %copy.56.b_ref), custom_call_target="tpu_custom_call" | custom-call | flops 3623878656 | bytes 6291456 | tf_op jit(solution)/shard_map/project/pallas_call | solution.py:78
  74.5 1.6 collective-permute-start.11
  77.6 3.9 collective-permute-start.12
  81.5 1.6 collective-permute-start.13
  83.1 1.3 collective-permute-start.14
  84.5 29.3 %attend_forward.1 = (bf16[1024,768]{1,0:T(8,128)(2,1)}, f32[6,8,1024]{2,1,0:T(8,128)}) custom-call(s32[2,4]{1,0:T(2,128)} %pad_add_fusion.limits_ref, bf16[3,1024,768]{2,1,0:T(8,128)(2,1)} %project.1.q_ref.k_ref.v_ref.refs_0_.refs_1_.refs_2_, bf16[3,1024,768]{2,1,0:T(8,128)(2,1)} %project.1.q_ref.k_ref.v_ref.refs_0_.refs_1_.refs_2_, ...), custom_call_target="tpu_custom_call" | custom-call | flops 6442450944 | bytes 4718592 | tf_op jit(solution)/shard_map/attend_forward/pallas_call | solution.py:188
  117.1 7.2 %combine.1 = (f32[1024,768]{1,0:T(8,128)}, bf16[1024,768]{1,0:T(8,128)(2,1)}, f32[1024,768]{1,0:T(8,128)}, f32[1024,1]{1,0:T(8,128)}) custom-call(bf16[1024,768]{1,0:T(8,128)(2,1)} %get-tuple-element.109.c_ref.o_ref.refs_4_.refs_1_, bf16[4,768,768]{2,1,0:T(8,128)(2,1)} %get-tuple-element.101.w_ref.wc_ref, bf16[1024,768]{1,0:T(8,128)(2,1)} %bitcast.169, ...), custom_call_target="tpu_custom_call" | custom-call | flops 2415919104 | bytes 3145728 | tf_op jit(solution)/shard_map/combine/pallas_call | solution.py:359
  128.2 5.6 %assemble.4.w_ref.we_ref = bf16[4,768,768]{2,1,0:T(8,128)(2,1)} custom-call(s32[3]{0:T(128)} %pad_add_fusion.1.me_ref, bf16[8,96,768]{2,1,0:T(8,128)(2,1)} %copy-done.3, bf16[8,96,768]{2,1,0:T(8,128)(2,1)} %collective-permute-done.11.refs_1_, bf16[8,96,768]{2,1,0:T(8,128)(2,1)} %collective-permute-done.16.refs_2_, ...), custom_call_target="tpu_custom_call" | custom-call | tf_op jit(solution)/shard_map/assemble/pallas_call | solution.py:722
  133.8 20.1 %expand.1 = (bf16[1024,3072]{1,0:T(8,128)(2,1)}, bf16[1024,3072]{1,0:T(8,128)(2,1)}) custom-call(bf16[1024,768]{1,0:T(8,128)(2,1)} %get-tuple-element.113.x_ref.refs_0_, bf16[4,768,768]{2,1,0:T(8,128)(2,1)} %assemble.4.w_ref.we_ref, f32[4,1,768]{2,1,0:T(1,128)} %convert.48.b_ref), custom_call_target="tpu_custom_call" | custom-call | flops 9663676416 | bytes 6291456 | tf_op jit(solution)/shard_map/expand/pallas_call | solution.py:395
  155.4 1.7 collective-permute-done.20.refs_3_
  157.1 5.6 %assemble.5.w_ref = bf16[3072,768]{1,0:T(8,128)(2,1)} custom-call(s32[3]{0:T(128)} %pad_add_fusion.1.me_ref, bf16[8,96,768]{2,1,0:T(8,128)(2,1)} %copy-done.2, bf16[8,96,768]{2,1,0:T(8,128)(2,1)} %copy-done.9, bf16[8,96,768]{2,1,0:T(8,128)(2,1)} %collective-permute-done.19.refs_2_, bf16[8,96,768]{2,1,0:T(8,128)(2,1)} %collective-permute-done.20.refs_3_), custom_call_target="tpu_custom_call" | custom-call | tf_op jit(solution)/shard_map/assemble/pallas_call | solution.py:722
  162.8 15.6 %reduce.51 = (bf16[1024,768]{1,0:T(8,128)(2,1)}, f32[8,768]{1,0:T(8,128)}, f32[1024,768]{1,0:T(8,128)}, bf16[1024,768]{1,0:T(8,128)(2,1)}, f32[8,768]{1,0:T(8,128)}) custom-call(bf16[1024,3072]{1,0:T(8,128)(2,1)} %get-tuple-element.120.act_ref.refs_0_, bf16[3072,768]{1,0:T(8,128)(2,1)} %assemble.5.w_ref, f32[1024,768]{1,0:T(8,128)} %get-tuple-element.122.hidden_ref, ...), custom_call_target="tpu_custom_call" | custom-call | flops 7247757312 | bytes 11010048 | tf_op jit(solution)/shard_map/reduce/pallas_call | solution.py:474
  178.4 10.4 %weight_grad_rows.1 = (bf16[16,96,768]{2,1,0:T(8,128)(2,1)}, bf16[16,96,768]{2,1,0:T(8,128)(2,1)}) custom-call(s32[3]{0:T(128)} %pad_add_fusion.1.me_ref, bf16[1024,3072]{1,0:T(8,128)(2,1)} %get-tuple-element.120.act_ref.refs_0_, bf16[1024,768]{1,0:T(8,128)(2,1)} %get-tuple-element.127.refs_1_.g_ref), custom_call_target="tpu_custom_call" | custom-call | flops 4831838208 | bytes 7864320 | tf_op jit(solution)/shard_map/weight_grad_rows/pallas_call | solution.py:827
  189.2 13.3 %grad_pre.1 = (bf16[1024,3072]{1,0:T(8,128)(2,1)}, f32[8,3072]{1,0:T(8,128)}) custom-call(bf16[1024,768]{1,0:T(8,128)(2,1)} %get-tuple-element.127.refs_1_.g_ref, bf16[3072,768]{1,0:T(8,128)(2,1)} %assemble.5.w_ref, bf16[1024,3072]{1,0:T(8,128)(2,1)} %get-tuple-element.128.slope_ref), custom_call_target="tpu_custom_call" | custom-call | flops 7247757312 | bytes 6291456 | tf_op jit(solution)/shard_map/grad_pre/pallas_call | solution.py:524
  202.5 1.4 copy-done.5
  203.9 4.1 %add_convert_fusion.4 = (bf16[8,96,768]{2,1,0:T(8,128)(2,1)S(1)}, bf16[8,96,768]{2,1,0:T(8,128)(2,1)}) fusion(bf16[16,96,768]{2,1,0:T(8,128)(2,1)} %copy-done.5, bf16[16,96,768]{2,1,0:T(8,128)(2,1)} %get-tuple-element.131), kind=kLoop, calls=%fused_computation.4 | loop fusion | flops 4718592 | bytes 7077888 | tf_op jit(solution)/shard_map/convert_element_type | solution.py:847
  211.2 11.0 %weight_grad_columns.1 = (bf16[16,104,768]{2,1,0:T(8,128)(2,1)}, bf16[16,104,768]{2,1,0:T(8,128)(2,1)}) custom-call(s32[3]{0:T(128)} %pad_add_fusion.1.me_ref, bf16[1024,768]{1,0:T(8,128)(2,1)} %get-tuple-element.113.x_ref.refs_0_, bf16[1024,3072]{1,0:T(8,128)(2,1)} %get-tuple-element.139.refs_1_.gp_ref, bf16[4,8,8,768]{3,2,1,0:T(8,128)(2,1)} %pad.8.refs_2_), custom_call_target="tpu_custom_call" | custom-call | flops 4831838208 | bytes 7864320 | tf_op jit(solution)/shard_map/weight_grad_columns/pallas_call | solution.py:827
  222.2 2.2 collective-permute-done.22
  225.5 15.3 %grad_hidden.1 = (f32[1024,768]{1,0:T(8,128)}, bf16[1024,768]{1,0:T(8,128)(2,1)}, bf16[1024,768]{1,0:T(8,128)(2,1)}, f32[8,768]{1,0:T(8,128)}) custom-call(bf16[1024,3072]{1,0:T(8,128)(2,1)} %get-tuple-element.139.refs_1_.gp_ref, bf16[4,768,768]{2,1,0:T(8,128)(2,1)} %assemble.4.w_ref.we_ref, f32[1024,768]{1,0:T(8,128)} %get-tuple-element.140.second_ref, ...), custom_call_target="tpu_custom_call" | custom-call | flops 7247757312 | bytes 11010048 | tf_op jit(solution)/shard_map/grad_hidden/pallas_call | solution.py:567
  241.6 4.2 %add_convert_fusion.2 = (bf16[8,104,768]{2,1,0:T(8,128)(2,1)}, bf16[8,104,768]{2,1,0:T(8,128)(2,1)S(1)}) fusion(bf16[16,104,768]{2,1,0:T(8,128)(2,1)} %collective-permute-done.23, bf16[16,104,768]{2,1,0:T(8,128)(2,1)} %get-tuple-element.145), kind=kLoop, calls=%fused_computation.2 | loop fusion | flops 5111808 | bytes 7667712 | tf_op jit(solution)/shard_map/convert_element_type | solution.py:847
  247.0 2.0 fusion.14
  249.0 2.5 collective-permute-start.26
  252.4 1.5 collective-permute-start.28
  253.8 14.8 %attend_backward.3 = (bf16[3,1024,768]{2,1,0:T(8,128)(2,1)}, f32[8,768]{1,0:T(8,128)}) custom-call(s32[2,4]{1,0:T(2,128)} %pad_add_fusion.limits_ref, bf16[3,1024,768]{2,1,0:T(8,128)(2,1)} %project.1.q_ref.k_ref.v_ref.refs_0_.refs_1_.refs_2_, bf16[3,1024,768]{2,1,0:T(8,128)(2,1)} %project.1.q_ref.k_ref.v_ref.refs_0_.refs_1_.refs_2_, ...), custom_call_target="tpu_custom_call" | custom-call | flops 3221225472 | bytes 4718592 | tf_op jit(solution)/shard_map/attend_backward/pallas_call | solution.py:297
  269.7 1.6 add_convert_fusion.8
  271.8 1.8 collective-permute-start.30
  273.6 14.9 %attend_backward.4 = (bf16[3,1024,768]{2,1,0:T(8,128)(2,1)}, f32[8,768]{1,0:T(8,128)}) custom-call(s32[2,4]{1,0:T(2,128)} %pad_add_fusion.limits_ref, bf16[3,1024,768]{2,1,0:T(8,128)(2,1)} %project.1.q_ref.k_ref.v_ref.refs_0_.refs_1_.refs_2_, ...), custom_call_target="tpu_custom_call", output_to_operand_aliasing={{0}: (9, {}), {1}: (10, {})} | custom-call | flops 3221225472 | bytes 4718592 | tf_op jit(solution)/shard_map/attend_backward/pallas_call | solution.py:297
  288.8 2.6 collective-permute-start.32
  292.6 15.1 %attend_backward.5 = (bf16[3,1024,768]{2,1,0:T(8,128)(2,1)}, f32[8,768]{1,0:T(8,128)}) custom-call(s32[2,4]{1,0:T(2,128)} %pad_add_fusion.limits_ref, bf16[3,1024,768]{2,1,0:T(8,128)(2,1)} %project.1.q_ref.k_ref.v_ref.refs_0_.refs_1_.refs_2_, ...), custom_call_target="tpu_custom_call", output_to_operand_aliasing={{0}: (9, {}), {1}: (10, {})} | custom-call | flops 3221225472 | bytes 4718592 | tf_op jit(solution)/shard_map/attend_backward/pallas_call | solution.py:297
  309.7 2.6 collective-permute-start.34
  312.4 12.3 %weight_grad_attend.1 = (bf16[16,104,768]{2,1,0:T(8,128)(2,1)}, bf16[16,104,768]{2,1,0:T(8,128)(2,1)}) custom-call(s32[3]{0:T(128)} %pad_add_fusion.1.me_ref, bf16[1024,768]{1,0:T(8,128)(2,1)} %bitcast.170, bf16[1024,768]{1,0:T(8,128)(2,1)} %get-tuple-element.109.c_ref.o_ref.refs_4_.refs_1_, bf16[3,1024,768]{2,1,0:T(8,128)(2,1)} %get-tuple-element.175.refs_2_.g_ref, ...), custom_call_target="tpu_custom_call" | custom-call | flops 4831838208 | bytes 9437184 | tf_op jit(solution)/shard_map/weight_grad_attend/pallas_call | solution.py:827
  324.8 5.0 %collective-permute-done.35 = bf16[16,104,768]{2,1,0:T(8,128)(2,1)S(1)} collective-permute-done((bf16[16,104,768]{2,1,0:T(8,128)(2,1)}, bf16[16,104,768]{2,1,0:T(8,128)(2,1)S(1)}, u32[]{:S(2)}, u32[]{:S(2)}) %collective-permute-start.35) | collective-permute-done | bytes 2555936 | tf_op jit(solution)/shard_map/ppermute | solution.py:626
  329.9 3.4 add_convert_fusion
  333.3 2.0 collective-permute-start.44
  335.3 8.7 %token_grad.1 = bf16[1024,768]{1,0:T(8,128)(2,1)} custom-call(bf16[3,1024,768]{2,1,0:T(8,128)(2,1)} %get-tuple-element.175.refs_2_.g_ref, bf16[4,768,768]{2,1,0:T(8,128)(2,1)} %get-tuple-element.101.w_ref.wc_ref, f32[1024,768]{1,0:T(8,128)} %get-tuple-element.176.first_ref), custom_call_target="tpu_custom_call" | custom-call | flops 3623878656 | bytes 9437184 | tf_op jit(solution)/shard_map/token_grad/pallas_call | solution.py:601
  344.0 6.9 %collective-permute-done.36 = bf16[8,104,768]{2,1,0:T(8,128)(2,1)} collective-permute-done((bf16[8,104,768]{2,1,0:T(8,128)(2,1)}, bf16[8,104,768]{2,1,0:T(8,128)(2,1)}, u32[]{:S(2)}, u32[]{:S(2)}) %collective-permute-start.36) | collective-permute-done | bytes 1277984 | tf_op jit(solution)/shard_map/ppermute | solution.py:626
  350.9 2.4 add_convert_fusion.7
  354.0 1.8 pad_maximum_fusion.5.in_ref
  355.9 4.0 place_rows.1
  359.9 3.9 collective-permute-done.43
  363.8 1.7 collective-permute-done.37
  366.2 3.2 collective-permute-start.40
  369.4 5.1 %collective-permute-done.38 = bf16[104,768]{1,0:T(8,128)(2,1)S(1)} collective-permute-done((bf16[104,768]{1,0:T(8,128)(2,1)S(1)}, bf16[104,768]{1,0:T(8,128)(2,1)S(1)}, u32[]{:S(2)}, u32[]{:S(2)}) %collective-permute-start.38) | collective-permute-done | bytes 159776 | tf_op jit(solution)/shard_map/ppermute | solution.py:626
  374.5 5.9 %collective-permute-done.39 = bf16[104,768]{1,0:T(8,128)(2,1)S(1)} collective-permute-done((bf16[104,768]{1,0:T(8,128)(2,1)S(1)}, bf16[104,768]{1,0:T(8,128)(2,1)S(1)}, u32[]{:S(2)}, u32[]{:S(2)}) %collective-permute-start.39) | collective-permute-done | bytes 159776 | tf_op jit(solution)/shard_map/ppermute | solution.py:626
  381.0 4.0 place_columns.1
  387.8 5.2 %collective-permute-done.42 = bf16[2,104,768]{2,1,0:T(8,128)(2,1)S(1)} collective-permute-done((bf16[2,104,768]{2,1,0:T(8,128)(2,1)S(1)}, bf16[2,104,768]{2,1,0:T(8,128)(2,1)S(1)}, u32[]{:S(2)}, u32[]{:S(2)}) %collective-permute-start.42) | collective-permute-done | bytes 319520 | tf_op jit(solution)/shard_map/ppermute | solution.py:626
  393.9 4.1 %place_attend.1 = (f32[96,2304]{1,0:T(8,128)}, f32[96,768]{1,0:T(8,128)}) custom-call(s32[3]{0:T(128)} %pad_add_fusion.1.me_ref, bf16[4,104,768]{2,1,0:T(8,128)(2,1)} %copy-done.4), custom_call_target="tpu_custom_call" | custom-call | tf_op jit(solution)/shard_map/place_attend/pallas_call | solution.py:890
  (178 shorter events, 42.1 us)
Async XLA Ops:
  0.6 35.0 %copy-start = (bf16[96,3072]{1,0:T(8,128)(2,1)S(1)}, bf16[96,3072]{1,0:T(8,128)(2,1)}, u32[]{:S(2)}) copy-start(bf16[96,3072]{1,0:T(8,128)(2,1)} %param.24) | copy-start | bytes 1769476
  6.2 10.3 %collective-permute-start = (bf16[104,768]{1,0:T(8,128)(2,1)}, bf16[104,768]{1,0:T(8,128)(2,1)S(1)}, u32[]{:S(2)}, u32[]{:S(2)}) collective-permute-start(bf16[104,768]{1,0:T(8,128)(2,1)} %lead.1), channel_id=1, source_target_pairs={{0,2},{1,3},{2,4},{3,5},{4,6},{5,7},{6,0},{7,1},{8,10},{9,11},{10,... | collective-permute-start | bytes 479240 | tf_op jit(solution)/shard_map/ppermute | solution.py:626
  9.3 13.3 %collective-permute-start.1 = (bf16[104,768]{1,0:T(8,128)(2,1)}, bf16[104,768]{1,0:T(8,128)(2,1)S(1)}, u32[]{:S(2)}, u32[]{:S(2)}) collective-permute-start(bf16[104,768]{1,0:T(8,128)(2,1)} %lead.1), channel_id=1, source_target_pairs={{0,4},{1,5},{2,6},{3,7},{4,0},{5,1},{6,2},{7,3},{8,12},{9,13},{10,... | collective-permute-start | bytes 479240 | tf_op jit(solution)/shard_map/ppermute | solution.py:626
  11.9 10.7 %collective-permute-start.2 = (bf16[104,768]{1,0:T(8,128)(2,1)}, bf16[104,768]{1,0:T(8,128)(2,1)S(1)}, u32[]{:S(2)}, u32[]{:S(2)}) collective-permute-start(bf16[104,768]{1,0:T(8,128)(2,1)} %lead.1), channel_id=1, source_target_pairs={{0,6},{1,7},{2,0},{3,1},{4,2},{5,3},{6,4},{7,5},{8,14},{9,15},{10,... | collective-permute-start | bytes 479240 | tf_op jit(solution)/shard_map/ppermute | solution.py:626
  23.6 10.5 %collective-permute-start.3 = (bf16[4,104,768]{2,1,0:T(8,128)(2,1)S(1)}, bf16[4,104,768]{2,1,0:T(8,128)(2,1)S(1)}, u32[]{:S(2)}, u32[]{:S(2)}) collective-permute-start(bf16[4,104,768]{2,1,0:T(8,128)(2,1)S(1)} %pad_maximum_fusion.1), channel_id=1, source_target_pairs={{0,8},{1,17},{2,10},{3,19},{4,12},{5,21},{6,14},{7,23},{8,0},{9,25... | collective-permute-start | bytes 1916936 | tf_op jit(solution)/shard_map/ppermute | solution.py:626
  25.2 27.4 %copy-start.12 = (s32[1,1024]{1,0:T(1,128)S(1)}, s32[1,1024]{1,0:T(1,128)}, u32[]{:S(2)}) copy-start(s32[1,1024]{1,0:T(1,128)} %seg_row_ref.1) | copy-start | bytes 12292
  34.1 20.7 %copy-start.6 = (bf16[8,104,768]{2,1,0:T(8,128)(2,1)}, bf16[8,104,768]{2,1,0:T(8,128)(2,1)S(1)}, u32[]{:S(2)}) copy-start(bf16[8,104,768]{2,1,0:T(8,128)(2,1)S(1)} %constant_dynamic-update-slice_fusion.refs_0_) | copy-start | bytes 3833860
  34.1 17.4 %collective-permute-start.4 = (bf16[8,104,768]{2,1,0:T(8,128)(2,1)S(1)}, bf16[8,104,768]{2,1,0:T(8,128)(2,1)}, u32[]{:S(2)}, u32[]{:S(2)}) collective-permute-start(bf16[8,104,768]{2,1,0:T(8,128)(2,1)S(1)} %constant_dynamic-update-slice_fusion.refs_0_), channel_id=1, source_target_pairs={{0,16},{1,9},{2,18},{3,11},{4,20},{5,13},{6,22},{7,15},{8,24},{9,1... | collective-permute-start | bytes 3833864 | tf_op jit(solution)/shard_map/ppermute | solution.py:626
  35.7 9.8 %collective-permute-start.5 = (bf16[96,768]{1,0:T(8,128)(2,1)S(1)}, bf16[96,768]{1,0:T(8,128)(2,1)S(1)}, u32[]{:S(2)}, u32[]{:S(2)}) collective-permute-start(bf16[96,768]{1,0:T(8,128)(2,1)S(1)} %constant_dynamic-slice_fusion.9), channel_id=1, source_target_pairs={{0,2},{1,3},{2,4},{3,5},{4,6},{5,7},{6,0},{7,1},{8,10},{9,11},{10,... | collective-permute-start | bytes 442376 | tf_op jit(solution)/shard_map/ppermute | solution.py:626
  39.6 9.9 %collective-permute-start.6 = (bf16[96,768]{1,0:T(8,128)(2,1)S(1)}, bf16[96,768]{1,0:T(8,128)(2,1)S(1)}, u32[]{:S(2)}, u32[]{:S(2)}) collective-permute-start(bf16[96,768]{1,0:T(8,128)(2,1)S(1)} %constant_dynamic-slice_fusion.9), channel_id=1, source_target_pairs={{0,4},{1,5},{2,6},{3,7},{4,0},{5,1},{6,2},{7,3},{8,12},{9,13},{10,... | collective-permute-start | bytes 442376 | tf_op jit(solution)/shard_map/ppermute | solution.py:626
  41.3 8.2 %collective-permute-start.7 = (bf16[96,768]{1,0:T(8,128)(2,1)S(1)}, bf16[96,768]{1,0:T(8,128)(2,1)S(1)}, u32[]{:S(2)}, u32[]{:S(2)}) collective-permute-start(bf16[96,768]{1,0:T(8,128)(2,1)S(1)} %constant_dynamic-slice_fusion.9), channel_id=1, source_target_pairs={{0,6},{1,7},{2,0},{3,1},{4,2},{5,3},{6,4},{7,5},{8,14},{9,15},{10,... | collective-permute-start | bytes 442376 | tf_op jit(solution)/shard_map/ppermute | solution.py:626
  51.5 3.3 collective-permute-start.9
  51.5 5.2 %collective-permute-start.8 = (bf16[8,104,768]{2,1,0:T(8,128)(2,1)S(1)}, bf16[8,104,768]{2,1,0:T(8,128)(2,1)}, u32[]{:S(2)}, u32[]{:S(2)}) collective-permute-start(bf16[8,104,768]{2,1,0:T(8,128)(2,1)S(1)} %constant_dynamic-update-slice_fusion.refs_0_), channel_id=1, source_target_pairs={{0,1},{1,0},{2,3},{3,2},{4,5},{5,4},{6,7},{7,6},{8,9},{9,8},{10,11... | collective-permute-start | bytes 3833864 | tf_op jit(solution)/shard_map/ppermute | solution.py:626
  54.9 18.5 %collective-permute-start.10 = (bf16[4,96,768]{2,1,0:T(8,128)(2,1)S(1)}, bf16[4,96,768]{2,1,0:T(8,128)(2,1)}, u32[]{:S(2)}, u32[]{:S(2)}) collective-permute-start(bf16[4,96,768]{2,1,0:T(8,128)(2,1)S(1)} %pad_maximum_fusion.3), channel_id=1, source_target_pairs={{0,8},{1,17},{2,10},{3,19},{4,12},{5,21},{6,14},{7,23},{8,0},{9,25... | collective-permute-start | bytes 1769480 | tf_op jit(solution)/shard_map/ppermute | solution.py:626
  74.5 39.3 %copy-start.3 = (bf16[8,96,768]{2,1,0:T(8,128)(2,1)}, bf16[8,96,768]{2,1,0:T(8,128)(2,1)S(1)}, u32[]{:S(2)}) copy-start(bf16[8,96,768]{2,1,0:T(8,128)(2,1)S(1)} %constant_dynamic-update-slice_fusion.5.refs_0_) | copy-start | bytes 3538948
  74.5 39.4 %collective-permute-start.11 = (bf16[8,96,768]{2,1,0:T(8,128)(2,1)S(1)}, bf16[8,96,768]{2,1,0:T(8,128)(2,1)}, u32[]{:S(2)}, u32[]{:S(2)}) collective-permute-start(bf16[8,96,768]{2,1,0:T(8,128)(2,1)S(1)} %constant_dynamic-update-slice_fusion.5.refs_0_), channel_id=1, source_target_pairs={{0,16},{1,9},{2,18},{3,11},{4,20},{5,13},{6,22},{7,15},{8,24},{9,1... | collective-permute-start | bytes 3538952 | tf_op jit(solution)/shard_map/ppermute | solution.py:626
  77.6 36.2 %collective-permute-start.12 = (bf16[96,768]{1,0:T(8,128)(2,1)S(1)}, bf16[96,768]{1,0:T(8,128)(2,1)S(1)}, u32[]{:S(2)}, u32[]{:S(2)}) collective-permute-start(bf16[96,768]{1,0:T(8,128)(2,1)S(1)} %constant_dynamic-slice_fusion.8), channel_id=1, source_target_pairs={{0,2},{1,3},{2,4},{3,5},{4,6},{5,7},{6,0},{7,1},{8,10},{9,11},{10,... | collective-permute-start | bytes 442376 | tf_op jit(solution)/shard_map/ppermute | solution.py:626
  81.5 32.2 %collective-permute-start.13 = (bf16[96,768]{1,0:T(8,128)(2,1)S(1)}, bf16[96,768]{1,0:T(8,128)(2,1)S(1)}, u32[]{:S(2)}, u32[]{:S(2)}) collective-permute-start(bf16[96,768]{1,0:T(8,128)(2,1)S(1)} %constant_dynamic-slice_fusion.8), channel_id=1, source_target_pairs={{0,4},{1,5},{2,6},{3,7},{4,0},{5,1},{6,2},{7,3},{8,12},{9,13},{10,... | collective-permute-start | bytes 442376 | tf_op jit(solution)/shard_map/ppermute | solution.py:626
  83.1 30.6 %collective-permute-start.14 = (bf16[96,768]{1,0:T(8,128)(2,1)S(1)}, bf16[96,768]{1,0:T(8,128)(2,1)S(1)}, u32[]{:S(2)}, u32[]{:S(2)}) collective-permute-start(bf16[96,768]{1,0:T(8,128)(2,1)S(1)} %constant_dynamic-slice_fusion.8), channel_id=1, source_target_pairs={{0,6},{1,7},{2,0},{3,1},{4,2},{5,3},{6,4},{7,5},{8,14},{9,15},{10,... | collective-permute-start | bytes 442376 | tf_op jit(solution)/shard_map/ppermute | solution.py:626
  84.5 41.0 %collective-permute-start.16 = (bf16[8,96,768]{2,1,0:T(8,128)(2,1)S(1)}, bf16[8,96,768]{2,1,0:T(8,128)(2,1)}, u32[]{:S(2)}, u32[]{:S(2)}) collective-permute-start(bf16[8,96,768]{2,1,0:T(8,128)(2,1)S(1)} %constant_dynamic-update-slice_fusion.5.refs_0_), channel_id=1, source_target_pairs={{0,1},{1,0},{2,3},{3,2},{4,5},{5,4},{6,7},{7,6},{8,9},{9,8},{10,11... | collective-permute-start | bytes 3538952 | tf_op jit(solution)/shard_map/ppermute | solution.py:626
  113.9 11.6 %collective-permute-start.17 = (bf16[8,96,768]{2,1,0:T(8,128)(2,1)}, bf16[8,96,768]{2,1,0:T(8,128)(2,1)}, u32[]{:S(2)}, u32[]{:S(2)}) collective-permute-start(bf16[8,96,768]{2,1,0:T(8,128)(2,1)} %collective-permute-done.11.refs_1_), channel_id=1, source_target_pairs={{0,1},{1,0},{2,3},{3,2},{4,5},{5,4},{6,7},{7,6},{8,9},{9,8},{10,11... | collective-permute-start | bytes 3538952 | tf_op jit(solution)/shard_map/ppermute | solution.py:626
  114.0 10.3 %collective-permute-start.15 = (bf16[4,96,768]{2,1,0:T(8,128)(2,1)S(1)}, bf16[4,96,768]{2,1,0:T(8,128)(2,1)}, u32[]{:S(2)}, u32[]{:S(2)}) collective-permute-start(bf16[4,96,768]{2,1,0:T(8,128)(2,1)S(1)} %pad_maximum_fusion.4), channel_id=1, source_target_pairs={{0,8},{1,17},{2,10},{3,19},{4,12},{5,21},{6,14},{7,23},{8,0},{9,25... | collective-permute-start | bytes 1769480 | tf_op jit(solution)/shard_map/ppermute | solution.py:626
  125.4 8.4 %copy-start.2 = (bf16[8,96,768]{2,1,0:T(8,128)(2,1)}, bf16[8,96,768]{2,1,0:T(8,128)(2,1)S(1)}, u32[]{:S(2)}) copy-start(bf16[8,96,768]{2,1,0:T(8,128)(2,1)S(1)} %pad_maximum_fusion.refs_0_) | copy-start | bytes 3538948
  125.5 28.4 %collective-permute-start.18 = (bf16[8,96,768]{2,1,0:T(8,128)(2,1)S(1)}, bf16[8,96,768]{2,1,0:T(8,128)(2,1)S(1)}, u32[]{:S(2)}, u32[]{:S(2)}) collective-permute-start(bf16[8,96,768]{2,1,0:T(8,128)(2,1)S(1)} %pad_maximum_fusion.refs_0_), channel_id=1, source_target_pairs={{0,16},{1,9},{2,18},{3,11},{4,20},{5,13},{6,22},{7,15},{8,24},{9,1... | collective-permute-start | bytes 3538952 | tf_op jit(solution)/shard_map/ppermute | solution.py:626
  128.2 27.2 %collective-permute-start.19 = (bf16[8,96,768]{2,1,0:T(8,128)(2,1)S(1)}, bf16[8,96,768]{2,1,0:T(8,128)(2,1)}, u32[]{:S(2)}, u32[]{:S(2)}) collective-permute-start(bf16[8,96,768]{2,1,0:T(8,128)(2,1)S(1)} %pad_maximum_fusion.refs_0_), channel_id=1, source_target_pairs={{0,1},{1,0},{2,3},{3,2},{4,5},{5,4},{6,7},{7,6},{8,9},{9,8},{10,11... | collective-permute-start | bytes 3538952 | tf_op jit(solution)/shard_map/ppermute | solution.py:626
  153.9 3.2 copy-start.9
  153.9 3.2 collective-permute-start.20
  188.8 13.7 %collective-permute-start.21 = (bf16[16,96,768]{2,1,0:T(8,128)(2,1)}, bf16[16,96,768]{2,1,0:T(8,128)(2,1)S(1)}, u32[]{:S(2)}, u32[]{:S(2)}) collective-permute-start(bf16[16,96,768]{2,1,0:T(8,128)(2,1)} %get-tuple-element.126), channel_id=1, source_target_pairs={{0,1},{1,0},{2,3},{3,2},{4,5},{5,4},{6,7},{7,6},{8,9},{9,8},{10,11... | collective-permute-start | bytes 7077896 | tf_op jit(solution)/shard_map/ppermute | solution.py:626
  202.5 1.4 copy-start.5
  203.9 5.9 %copy-start.13 = (f32[8,768]{1,0:T(8,128)S(1)}, f32[8,768]{1,0:T(8,128)}, u32[]{:S(2)}) copy-start(f32[8,768]{1,0:T(8,128)} %get-tuple-element.135) | copy-start | bytes 73732
  208.0 16.4 %collective-permute-start.22 = (bf16[8,96,768]{2,1,0:T(8,128)(2,1)}, bf16[8,96,768]{2,1,0:T(8,128)(2,1)S(1)}, u32[]{:S(2)}, u32[]{:S(2)}) collective-permute-start(bf16[8,96,768]{2,1,0:T(8,128)(2,1)} %get-tuple-element.206), channel_id=1, source_target_pairs={{0,8},{1,17},{2,10},{3,19},{4,12},{5,21},{6,14},{7,23},{8,0},{9,25... | collective-permute-start | bytes 3538952 | tf_op jit(solution)/shard_map/ppermute | solution.py:626
  224.4 16.4 %collective-permute-start.23 = (bf16[16,104,768]{2,1,0:T(8,128)(2,1)}, bf16[16,104,768]{2,1,0:T(8,128)(2,1)}, u32[]{:S(2)}, u32[]{:S(2)}) collective-permute-start(bf16[16,104,768]{2,1,0:T(8,128)(2,1)} %get-tuple-element.137), channel_id=1, source_target_pairs={{0,1},{1,0},{2,3},{3,2},{4,5},{5,4},{6,7},{7,6},{8,9},{9,8},{10,11... | collective-permute-start | bytes 7667720 | tf_op jit(solution)/shard_map/ppermute | solution.py:626
  224.7 16.1 %collective-permute-start.24 = (bf16[4,96,768]{2,1,0:T(8,128)(2,1)S(1)}, bf16[4,96,768]{2,1,0:T(8,128)(2,1)S(1)}, u32[]{:S(2)}, u32[]{:S(2)}) collective-permute-start(bf16[4,96,768]{2,1,0:T(8,128)(2,1)S(1)} %get-tuple-element.212), channel_id=1, source_target_pairs={{0,16},{1,9},{2,18},{3,11},{4,20},{5,13},{6,22},{7,15},{8,24},{9,1... | collective-permute-start | bytes 1769480 | tf_op jit(solution)/shard_map/ppermute | solution.py:626
  240.8 0.8 copy-start.10
  241.6 5.1 %copy-start.14 = (f32[8,768]{1,0:T(8,128)S(1)}, f32[8,768]{1,0:T(8,128)}, u32[]{:S(2)}) copy-start(f32[8,768]{1,0:T(8,128)} %get-tuple-element.171) | copy-start | bytes 73732
  245.8 22.9 %collective-permute-start.25 = (bf16[8,104,768]{2,1,0:T(8,128)(2,1)}, bf16[8,104,768]{2,1,0:T(8,128)(2,1)S(1)}, u32[]{:S(2)}, u32[]{:S(2)}) collective-permute-start(bf16[8,104,768]{2,1,0:T(8,128)(2,1)} %get-tuple-element.203), channel_id=1, source_target_pairs={{0,8},{1,17},{2,10},{3,19},{4,12},{5,21},{6,14},{7,23},{8,0},{9,25... | collective-permute-start | bytes 3833864 | tf_op jit(solution)/shard_map/ppermute | solution.py:626
  249.0 19.6 %collective-permute-start.26 = (bf16[96,768]{1,0:T(8,128)(2,1)}, bf16[96,768]{1,0:T(8,128)(2,1)S(1)}, u32[]{:S(2)}, u32[]{:S(2)}) collective-permute-start(bf16[96,768]{1,0:T(8,128)(2,1)} %get-tuple-element.222), channel_id=1, source_target_pairs={{0,2},{1,3},{2,4},{3,5},{4,6},{5,7},{6,0},{7,1},{8,10},{9,11},{10,... | collective-permute-start | bytes 442376 | tf_op jit(solution)/shard_map/ppermute | solution.py:626
  251.5 17.2 %collective-permute-start.27 = (bf16[96,768]{1,0:T(8,128)(2,1)S(1)}, bf16[96,768]{1,0:T(8,128)(2,1)S(1)}, u32[]{:S(2)}, u32[]{:S(2)}) collective-permute-start(bf16[96,768]{1,0:T(8,128)(2,1)S(1)} %get-tuple-element.221), channel_id=1, source_target_pairs={{0,4},{1,5},{2,6},{3,7},{4,0},{5,1},{6,2},{7,3},{8,12},{9,13},{10,... | collective-permute-start | bytes 442376 | tf_op jit(solution)/shard_map/ppermute | solution.py:626
  252.4 16.3 %collective-permute-start.28 = (bf16[96,768]{1,0:T(8,128)(2,1)S(1)}, bf16[96,768]{1,0:T(8,128)(2,1)S(1)}, u32[]{:S(2)}, u32[]{:S(2)}) collective-permute-start(bf16[96,768]{1,0:T(8,128)(2,1)S(1)} %get-tuple-element.220), channel_id=1, source_target_pairs={{0,6},{1,7},{2,0},{3,1},{4,2},{5,3},{6,4},{7,5},{8,14},{9,15},{10,... | collective-permute-start | bytes 442376 | tf_op jit(solution)/shard_map/ppermute | solution.py:626
  268.7 1.0 copy-start.8
  269.7 2.0 copy-start.11
  271.3 17.2 %collective-permute-start.29 = (bf16[4,104,768]{2,1,0:T(8,128)(2,1)S(1)}, bf16[4,104,768]{2,1,0:T(8,128)(2,1)S(1)}, u32[]{:S(2)}, u32[]{:S(2)}) collective-permute-start(bf16[4,104,768]{2,1,0:T(8,128)(2,1)S(1)} %get-tuple-element.209), channel_id=1, source_target_pairs={{0,16},{1,9},{2,18},{3,11},{4,20},{5,13},{6,22},{7,15},{8,24},{9,1... | collective-permute-start | bytes 1916936 | tf_op jit(solution)/shard_map/ppermute | solution.py:626
  271.8 16.7 %collective-permute-start.30 = (bf16[96,768]{1,0:T(8,128)(2,1)S(1)}, bf16[96,768]{1,0:T(8,128)(2,1)S(1)}, u32[]{:S(2)}, u32[]{:S(2)}) collective-permute-start(bf16[96,768]{1,0:T(8,128)(2,1)S(1)} %add_convert_fusion.21), channel_id=1, source_target_pairs={{0,16},{1,9},{2,18},{3,11},{4,20},{5,13},{6,22},{7,15},{8,24},{9,1... | collective-permute-start | bytes 442376 | tf_op jit(solution)/shard_map/ppermute | solution.py:626
  288.7 20.9 %collective-permute-start.31 = (bf16[104,768]{1,0:T(8,128)(2,1)S(1)}, bf16[104,768]{1,0:T(8,128)(2,1)S(1)}, u32[]{:S(2)}, u32[]{:S(2)}) collective-permute-start(bf16[104,768]{1,0:T(8,128)(2,1)S(1)} %get-tuple-element.218), channel_id=1, source_target_pairs={{0,2},{1,3},{2,4},{3,5},{4,6},{5,7},{6,0},{7,1},{8,10},{9,11},{10,... | collective-permute-start | bytes 479240 | tf_op jit(solution)/shard_map/ppermute | solution.py:626
  288.8 20.9 %collective-permute-start.32 = (bf16[104,768]{1,0:T(8,128)(2,1)S(1)}, bf16[104,768]{1,0:T(8,128)(2,1)S(1)}, u32[]{:S(2)}, u32[]{:S(2)}) collective-permute-start(bf16[104,768]{1,0:T(8,128)(2,1)S(1)} %get-tuple-element.217), channel_id=1, source_target_pairs={{0,4},{1,5},{2,6},{3,7},{4,0},{5,1},{6,2},{7,3},{8,12},{9,13},{10,... | collective-permute-start | bytes 479240 | tf_op jit(solution)/shard_map/ppermute | solution.py:626
  291.3 18.3 %collective-permute-start.33 = (bf16[104,768]{1,0:T(8,128)(2,1)S(1)}, bf16[104,768]{1,0:T(8,128)(2,1)S(1)}, u32[]{:S(2)}, u32[]{:S(2)}) collective-permute-start(bf16[104,768]{1,0:T(8,128)(2,1)S(1)} %get-tuple-element.216), channel_id=1, source_target_pairs={{0,6},{1,7},{2,0},{3,1},{4,2},{5,3},{6,4},{7,5},{8,14},{9,15},{10,... | collective-permute-start | bytes 479240 | tf_op jit(solution)/shard_map/ppermute | solution.py:626
  309.7 15.0 %collective-permute-start.34 = (bf16[104,768]{1,0:T(8,128)(2,1)S(1)}, bf16[104,768]{1,0:T(8,128)(2,1)S(1)}, u32[]{:S(2)}, u32[]{:S(2)}) collective-permute-start(bf16[104,768]{1,0:T(8,128)(2,1)S(1)} %add_convert_fusion.16), channel_id=1, source_target_pairs={{0,16},{1,9},{2,18},{3,11},{4,20},{5,13},{6,22},{7,15},{8,24},{9,1... | collective-permute-start | bytes 479240 | tf_op jit(solution)/shard_map/ppermute | solution.py:626
  324.8 5.1 %collective-permute-start.35 = (bf16[16,104,768]{2,1,0:T(8,128)(2,1)}, bf16[16,104,768]{2,1,0:T(8,128)(2,1)S(1)}, u32[]{:S(2)}, u32[]{:S(2)}) collective-permute-start(bf16[16,104,768]{2,1,0:T(8,128)(2,1)} %get-tuple-element.174), channel_id=1, source_target_pairs={{0,1},{1,0},{2,3},{3,2},{4,5},{5,4},{6,7},{7,6},{8,9},{9,8},{10,11... | collective-permute-start | bytes 7667720 | tf_op jit(solution)/shard_map/ppermute | solution.py:626
  333.3 17.6 %collective-permute-start.36 = (bf16[8,104,768]{2,1,0:T(8,128)(2,1)}, bf16[8,104,768]{2,1,0:T(8,128)(2,1)}, u32[]{:S(2)}, u32[]{:S(2)}) collective-permute-start(bf16[8,104,768]{2,1,0:T(8,128)(2,1)} %get-tuple-element.202), channel_id=1, source_target_pairs={{0,8},{1,17},{2,10},{3,19},{4,12},{5,21},{6,14},{7,23},{8,0},{9,25... | collective-permute-start | bytes 3833864 | tf_op jit(solution)/shard_map/ppermute | solution.py:626
  333.3 20.7 %collective-permute-start.44 = (bf16[2,96,768]{2,1,0:T(8,128)(2,1)S(1)}, bf16[2,96,768]{2,1,0:T(8,128)(2,1)}, u32[]{:S(2)}, u32[]{:S(2)}) collective-permute-start(bf16[2,96,768]{2,1,0:T(8,128)(2,1)S(1)} %pad_maximum_fusion.8), channel_id=1, source_target_pairs={{0,8},{1,17},{2,10},{3,19},{4,12},{5,21},{6,14},{7,23},{8,0},{9,25... | collective-permute-start | bytes 884744 | tf_op jit(solution)/shard_map/ppermute | solution.py:626
  353.3 12.1 %collective-permute-start.37 = (bf16[4,104,768]{2,1,0:T(8,128)(2,1)}, bf16[4,104,768]{2,1,0:T(8,128)(2,1)S(1)}, u32[]{:S(2)}, u32[]{:S(2)}) collective-permute-start(bf16[4,104,768]{2,1,0:T(8,128)(2,1)} %get-tuple-element.208), channel_id=1, source_target_pairs={{0,16},{1,9},{2,18},{3,11},{4,20},{5,13},{6,22},{7,15},{8,24},{9,1... | collective-permute-start | bytes 1916936 | tf_op jit(solution)/shard_map/ppermute | solution.py:626
  353.3 10.4 %collective-permute-start.43 = (bf16[2,104,768]{2,1,0:T(8,128)(2,1)S(1)}, bf16[2,104,768]{2,1,0:T(8,128)(2,1)S(1)}, u32[]{:S(2)}, u32[]{:S(2)}) collective-permute-start(bf16[2,104,768]{2,1,0:T(8,128)(2,1)S(1)} %pad_maximum_fusion.6), channel_id=1, source_target_pairs={{0,8},{1,17},{2,10},{3,19},{4,12},{5,21},{6,14},{7,23},{8,0},{9,25... | collective-permute-start | bytes 958472 | tf_op jit(solution)/shard_map/ppermute | solution.py:626
  363.8 17.2 %copy-start.7 = (bf16[4,104,768]{2,1,0:T(8,128)(2,1)}, bf16[4,104,768]{2,1,0:T(8,128)(2,1)S(1)}, u32[]{:S(2)}) copy-start(bf16[4,104,768]{2,1,0:T(8,128)(2,1)S(1)} %constant_dynamic-update-slice_fusion.7.in_ref) | copy-start | bytes 1916932
  365.5 9.0 %collective-permute-start.38 = (bf16[104,768]{1,0:T(8,128)(2,1)S(1)}, bf16[104,768]{1,0:T(8,128)(2,1)S(1)}, u32[]{:S(2)}, u32[]{:S(2)}) collective-permute-start(bf16[104,768]{1,0:T(8,128)(2,1)S(1)} %get-tuple-element.213), channel_id=1, source_target_pairs={{0,2},{1,3},{2,4},{3,5},{4,6},{5,7},{6,0},{7,1},{8,10},{9,11},{10,... | collective-permute-start | bytes 479240 | tf_op jit(solution)/shard_map/ppermute | solution.py:626
  365.6 14.8 %collective-permute-start.39 = (bf16[104,768]{1,0:T(8,128)(2,1)S(1)}, bf16[104,768]{1,0:T(8,128)(2,1)S(1)}, u32[]{:S(2)}, u32[]{:S(2)}) collective-permute-start(bf16[104,768]{1,0:T(8,128)(2,1)S(1)} %get-tuple-element.215), channel_id=1, source_target_pairs={{0,4},{1,5},{2,6},{3,7},{4,0},{5,1},{6,2},{7,3},{8,12},{9,13},{10,... | collective-permute-start | bytes 479240 | tf_op jit(solution)/shard_map/ppermute | solution.py:626
  366.2 14.2 %collective-permute-start.40 = (bf16[104,768]{1,0:T(8,128)(2,1)S(1)}, bf16[104,768]{1,0:T(8,128)(2,1)S(1)}, u32[]{:S(2)}, u32[]{:S(2)}) collective-permute-start(bf16[104,768]{1,0:T(8,128)(2,1)S(1)} %get-tuple-element.214), channel_id=1, source_target_pairs={{0,6},{1,7},{2,0},{3,1},{4,2},{5,3},{6,4},{7,5},{8,14},{9,15},{10,... | collective-permute-start | bytes 479240 | tf_op jit(solution)/shard_map/ppermute | solution.py:626
  380.6 5.3 %collective-permute-start.41 = (bf16[104,768]{1,0:T(8,128)(2,1)S(1)}, bf16[104,768]{1,0:T(8,128)(2,1)S(1)}, u32[]{:S(2)}, u32[]{:S(2)}) collective-permute-start(bf16[104,768]{1,0:T(8,128)(2,1)S(1)} %fusion.2), channel_id=1, source_target_pairs={{0,16},{1,9},{2,18},{3,11},{4,20},{5,13},{6,22},{7,15},{8,24},{9,1... | collective-permute-start | bytes 479240 | tf_op jit(solution)/shard_map/ppermute | solution.py:626
  385.9 14.5 %copy-start.1 = (bf16[96,3072]{1,0:T(8,128)(2,1)S(1)}, bf16[96,3072]{1,0:T(8,128)(2,1)}, u32[]{:S(2)}) copy-start(bf16[96,3072]{1,0:T(8,128)(2,1)} %param.24) | copy-start | bytes 1769476
  385.9 7.1 %collective-permute-start.42 = (bf16[2,104,768]{2,1,0:T(8,128)(2,1)S(1)}, bf16[2,104,768]{2,1,0:T(8,128)(2,1)S(1)}, u32[]{:S(2)}, u32[]{:S(2)}) collective-permute-start(bf16[2,104,768]{2,1,0:T(8,128)(2,1)S(1)} %pad_maximum_fusion.7), channel_id=1, source_target_pairs={{0,8},{1,17},{2,10},{3,19},{4,12},{5,21},{6,14},{7,23},{8,0},{9,25... | collective-permute-start | bytes 958472 | tf_op jit(solution)/shard_map/ppermute | solution.py:626
  393.1 0.8 copy-start.4
